TPU v7x, 32 devices: a whole 2x2x4 slice. The times are simulated.
32 devices in a mesh: gx: 4 (over y, x), gy: 4 (over z), gz: 2 (over core).
Axes of the slice: x: 2, y: 2, z: 4, core: 2. Of those that a mesh axis runs over, the one named last changes fastest.
Arguments:
- pressure: float32 [64, 128, 512], P('gz', 'gx', 'gy'), may hold values from 0.5 to 1.5
- saturation: float32 [64, 128, 512], P('gz', 'gx', 'gy'), may hold values from 0 to 0.5
- dissolved: float32 [64, 128, 512], P('gz', 'gx', 'gy'), may hold values from 0 to 0.12
- old_water: float32 [64, 128, 512], P('gz', 'gx', 'gy'), may hold values from 0.3 to 1
- old_hydrogen: float32 [64, 128, 512], P('gz', 'gx', 'gy'), may hold values from 0 to 0.2
- pore_volume: float32 [64, 128, 512], P('gz', 'gx', 'gy'), may hold values from 1 to 8
- permeability: float32 [64, 128, 512], P('gz', 'gx', 'gy'), may hold values from 0.1 to 10
- frac_pressure: float32 [64, 4096], P('gz', ('gx', 'gy')), may hold values from 0.5 to 1.5
- frac_saturation: float32 [64, 4096], P('gz', ('gx', 'gy')), may hold values from 0 to 0.5
- frac_dissolved: float32 [64, 4096], P('gz', ('gx', 'gy')), may hold values from 0 to 0.12
- frac_old_water: float32 [64, 4096], P('gz', ('gx', 'gy')), may hold values from 0.3 to 1
- frac_old_hydrogen: float32 [64, 4096], P('gz', ('gx', 'gy')), may hold values from 0 to 0.2
- frac_volume: float32 [64, 4096], P('gz', ('gx', 'gy')), may hold values from 0.5 to 4
- pair_segment: int32 [16, 256], P(('gx', 'gy')), may hold values from 0 to 255
- pair_column: int32 [16, 256], P(('gx', 'gy')), may hold values from 0 to 4095
- pair_kind: int32 [16, 256], P(('gx', 'gy')), may hold values from 0 to 63
- pair_count: int32 [16, 16], P(('gx', 'gy')), may hold values from 0 to 16, as said below
- transfer_table: float32 [64], replicated, may hold values from 0.5 to 4
Outputs:
- newton_step: float32 [3, 64, 128, 512], P(None, 'gz', 'gx', 'gy')
- frac_newton_step: float32 [3, 64, 4096], P(None, 'gz', ('gx', 'gy'))
- residual: float32 [3, 64, 128, 512], P(None, 'gz', 'gx', 'gy')
- frac_residual: float32 [3, 64, 4096], P(None, 'gz', ('gx', 'gy'))
Inputs may be any that keep to these rules, and one draw needn't show every extreme that they name: `pair_count`: entry [q, o] counts the live pairs between segment block o and column block q; they use slots 0 to that count less one. Some entry equals 16 in every draw.
All inputs are finite; a program needn't handle non-finite values.
Results may differ from a plain program's by a relative error of at most 0.0019.
Values sent between devices are 32-bit elements; how exact they have to be, the bound alone decides.
No kernel may reach another device: no remote copies, remote signals or barrier semaphores. Data moves between devices by JAX's collectives and lax.ppermute only.
A program may use at most 128 MiB of HBM per device.

v0:
```python
import jax
import jax.numpy as jnp
from jax import lax
from jax.sharding import PartitionSpec as P

LIQUID_SLOPE = 0.05
GAS_BASE = 0.2
GAS_SLOPE = 0.1
GAS_VISCOSITY = 0.1
SOLUBLE_BASE = 0.05
SOLUBLE_SLOPE = 0.025
SMOOTHING = 0.0001
GRAVITY = 0.5
VERTICAL_RATIO = 0.2
NORM_SHIFT = 1e-06


def with_halo(shard, sides, width):
    for axis, dim in sides:
        size, length = (lax.axis_size(axis), shard.shape[dim])
        up = [(i, (i + 1) % size) for i in range(size - 1)]
        down = [(j, i) for i, j in up]
        last = lax.slice_in_dim(shard, length - width, length, axis=dim)
        first = lax.slice_in_dim(shard, 0, width, axis=dim)
        before = lax.ppermute(last, axis, up)
        after = lax.ppermute(first, axis, down)
        shard = jnp.concatenate([before, shard, after], axis=dim)
    return shard


def phase_terms(pressure, saturation, dissolved):
    liquid_density = 1.0 + LIQUID_SLOPE * pressure
    gas_density = GAS_BASE + GAS_SLOPE * pressure
    liquid_share = (1.0 - saturation) * (1.0 - saturation)
    water_mobility = liquid_density * (1.0 - dissolved) * liquid_share
    solute_mobility = liquid_density * dissolved * liquid_share
    gas_mobility = gas_density * saturation * saturation / GAS_VISCOSITY
    return (water_mobility, solute_mobility, gas_mobility)


def phase_steps(pressure, saturation, dissolved, step_pressure, step_saturation, step_dissolved):
    liquid_density = 1.0 + LIQUID_SLOPE * pressure
    gas_density = GAS_BASE + GAS_SLOPE * pressure
    liquid_share = (1.0 - saturation) * (1.0 - saturation)
    step_density = LIQUID_SLOPE * step_pressure
    step_share = -2.0 * (1.0 - saturation) * step_saturation
    step_water = (
        step_density * (1.0 - dissolved) * liquid_share
        - liquid_density * step_dissolved * liquid_share
        + liquid_density * (1.0 - dissolved) * step_share
    )
    step_solute = (
        step_density * dissolved * liquid_share
        + liquid_density * step_dissolved * liquid_share
        + liquid_density * dissolved * step_share
    )
    step_gas = (
        GAS_SLOPE * step_pressure * saturation * saturation
        + 2.0 * gas_density * saturation * step_saturation
    ) / GAS_VISCOSITY
    return (step_water, step_solute, step_gas)


def phase_masses(pressure, saturation, dissolved):
    liquid_density = 1.0 + LIQUID_SLOPE * pressure
    gas_density = GAS_BASE + GAS_SLOPE * pressure
    water_mass = liquid_density * (1.0 - saturation) * (1.0 - dissolved)
    hydrogen_mass = liquid_density * (1.0 - saturation) * dissolved + gas_density * saturation
    return (water_mass, hydrogen_mass)


def mass_steps(pressure, saturation, dissolved, step_pressure, step_saturation, step_dissolved):
    liquid_density = 1.0 + LIQUID_SLOPE * pressure
    gas_density = GAS_BASE + GAS_SLOPE * pressure
    step_density = LIQUID_SLOPE * step_pressure
    step_water_mass = (
        step_density * (1.0 - saturation) * (1.0 - dissolved)
        - liquid_density * step_saturation * (1.0 - dissolved)
        - liquid_density * (1.0 - saturation) * step_dissolved
    )
    step_hydrogen_mass = (
        step_density * (1.0 - saturation) * dissolved
        - liquid_density * step_saturation * dissolved
        + liquid_density * (1.0 - saturation) * step_dissolved
        + GAS_SLOPE * step_pressure * saturation
        + gas_density * step_saturation
    )
    return (step_water_mass, step_hydrogen_mass)


def closure_residual(pressure, saturation, dissolved):
    solubility_gap = SOLUBLE_BASE + SOLUBLE_SLOPE * pressure - dissolved
    root_value = jnp.sqrt(saturation * saturation + solubility_gap * solubility_gap + SMOOTHING)
    return saturation + solubility_gap - root_value


def closure_step(pressure, saturation, dissolved, step_pressure, step_saturation, step_dissolved):
    solubility_gap = SOLUBLE_BASE + SOLUBLE_SLOPE * pressure - dissolved
    root_value = jnp.sqrt(saturation * saturation + solubility_gap * solubility_gap + SMOOTHING)
    step_gap = SOLUBLE_SLOPE * step_pressure - step_dissolved
    return (
        step_saturation
        + step_gap
        - (saturation * step_saturation + solubility_gap * step_gap) / root_value
    )


def face_sides(padded, spatial):
    window = [slice(1, -1), slice(1, -1), slice(1, -1)]
    window[spatial] = slice(0, -1)
    lower_side = padded[tuple(window)]
    window[spatial] = slice(1, None)
    upper_side = padded[tuple(window)]
    return (lower_side, upper_side)


def face_difference(face_flux, spatial):
    extent = face_flux.shape[spatial]
    return lax.slice_in_dim(face_flux, 1, extent, axis=spatial) - lax.slice_in_dim(
        face_flux, 0, extent - 1, axis=spatial
    )


def flux_divergence(base_padded, step_padded):
    permeability, pressure, water_mobility, solute_mobility, gas_mobility = base_padded
    water_parts = []
    hydrogen_parts = []
    for spatial in range(3):
        perm_lower, perm_upper = face_sides(permeability, spatial)
        transmit = 2.0 * perm_lower * perm_upper / (perm_lower + perm_upper)
        press_lower, press_upper = face_sides(pressure, spatial)
        liquid_drop = press_lower - press_upper
        gas_drop = press_lower - press_upper
        if spatial == 0:
            transmit = VERTICAL_RATIO * transmit
            mean_pressure = 0.5 * (press_lower + press_upper)
            liquid_drop = liquid_drop + GRAVITY * (1.0 + LIQUID_SLOPE * mean_pressure)
            gas_drop = gas_drop + GRAVITY * (GAS_BASE + GAS_SLOPE * mean_pressure)
        water_lower, water_upper = face_sides(water_mobility, spatial)
        solute_lower, solute_upper = face_sides(solute_mobility, spatial)
        gas_lower, gas_upper = face_sides(gas_mobility, spatial)
        water_mean = 0.5 * (water_lower + water_upper)
        solute_mean = 0.5 * (solute_lower + solute_upper)
        gas_mean = 0.5 * (gas_lower + gas_upper)
        if step_padded is None:
            water_flux = transmit * water_mean * liquid_drop
            hydrogen_flux = transmit * (solute_mean * liquid_drop + gas_mean * gas_drop)
        else:
            step_pressure, step_water, step_solute, step_gas = step_padded
            step_lower, step_upper = face_sides(step_pressure, spatial)
            step_liquid_drop = step_lower - step_upper
            step_gas_drop = step_lower - step_upper
            if spatial == 0:
                step_mean = 0.5 * (step_lower + step_upper)
                step_liquid_drop = step_liquid_drop + GRAVITY * LIQUID_SLOPE * step_mean
                step_gas_drop = step_gas_drop + GRAVITY * GAS_SLOPE * step_mean
            sw_lower, sw_upper = face_sides(step_water, spatial)
            ss_lower, ss_upper = face_sides(step_solute, spatial)
            sg_lower, sg_upper = face_sides(step_gas, spatial)
            water_flux = transmit * (
                0.5 * (sw_lower + sw_upper) * liquid_drop + water_mean * step_liquid_drop
            )
            hydrogen_flux = transmit * (
                0.5 * (ss_lower + ss_upper) * liquid_drop
                + solute_mean * step_liquid_drop
                + 0.5 * (sg_lower + sg_upper) * gas_drop
                + gas_mean * step_gas_drop
            )
        water_parts.append(face_difference(water_flux, spatial))
        hydrogen_parts.append(face_difference(hydrogen_flux, spatial))
    return (
        water_parts[0] + water_parts[1] + water_parts[2],
        hydrogen_parts[0] + hydrogen_parts[1] + hydrogen_parts[2],
    )


def add_columns(grid_field, column_index, values):
    shape_kept = grid_field.shape
    flat_field = grid_field.reshape(shape_kept[0], shape_kept[1] * shape_kept[2])
    return flat_field.at[:, column_index].add(values).reshape(shape_kept)


def send_rows(stacked):
    return lax.all_to_all(stacked, ("gx", "gy"), split_axis=2, concat_axis=2, tiled=True)


def return_rates(stacked):
    return lax.all_to_all(stacked, ("gx", "gy"), split_axis=2, concat_axis=2, tiled=True)


def inner_product(left_pair, right_pair):
    return jnp.sum(left_pair[0] * right_pair[0]) + jnp.sum(left_pair[1] * right_pair[1])


def on_device(
    pressure,
    saturation,
    dissolved,
    old_water,
    old_hydrogen,
    pore_volume,
    permeability,
    frac_pressure,
    frac_saturation,
    frac_dissolved,
    frac_old_water,
    frac_old_hydrogen,
    frac_volume,
    pair_segment,
    pair_column,
    pair_kind,
    pair_count,
    transfer_table,
):
    layers = pressure.shape[0]
    columns_total = pressure.shape[1] * pressure.shape[2]
    segment_index = pair_segment[0]
    column_index = pair_column[0]
    slot_total = column_index.shape[0]
    capacity = slot_total // pair_count.shape[1]
    live_slots = (jnp.arange(capacity, dtype=jnp.int32)[None, :] < pair_count[0][:, None]).reshape(
        slot_total
    )
    kind_match = (
        pair_kind[0][:, None] == jnp.arange(transfer_table.shape[0], dtype=jnp.int32)[None, :]
    )
    pair_weight = jnp.where(
        live_slots, jnp.sum(jnp.where(kind_match, transfer_table[None, :], 0.0), axis=1), 0.0
    )
    water_mob, solute_mob, gas_mob = phase_terms(pressure, saturation, dissolved)
    padded = with_halo(
        jnp.stack([permeability, pressure, water_mob, solute_mob, gas_mob]),
        (("gx", 2), ("gy", 3), ("gz", 1)),
        1,
    )
    base_padded = (padded[0], padded[1], padded[2], padded[3], padded[4])
    water_div, hydrogen_div = flux_divergence(base_padded, None)
    water_mass, hydrogen_mass = phase_masses(pressure, saturation, dissolved)
    frac_water_mob, frac_solute_mob, frac_gas_mob = phase_terms(
        frac_pressure, frac_saturation, frac_dissolved
    )
    frac_water_mass, frac_hydrogen_mass = phase_masses(
        frac_pressure, frac_saturation, frac_dissolved
    )
    frac_rows = send_rows(
        jnp.take(
            jnp.stack([frac_pressure, frac_water_mob, frac_solute_mob + frac_gas_mob]),
            segment_index,
            axis=2,
        )
    )
    cell_rows = jnp.take(
        jnp.stack([pressure, water_mob, solute_mob + gas_mob]).reshape(3, layers, columns_total),
        column_index,
        axis=2,
    )
    pressure_gap = frac_rows[0] - cell_rows[0]
    water_rate = pair_weight * 0.5 * (frac_rows[1] + cell_rows[1]) * pressure_gap
    hydrogen_rate = pair_weight * 0.5 * (frac_rows[2] + cell_rows[2]) * pressure_gap
    returned = return_rates(jnp.stack([water_rate, hydrogen_rate]))
    matrix_res = jnp.stack(
        [
            add_columns(
                pore_volume * (water_mass - old_water) + water_div, column_index, -water_rate
            ),
            add_columns(
                pore_volume * (hydrogen_mass - old_hydrogen) + hydrogen_div,
                column_index,
                -hydrogen_rate,
            ),
            closure_residual(pressure, saturation, dissolved),
        ]
    )
    frac_res = jnp.stack(
        [
            (frac_volume * (frac_water_mass - frac_old_water))
            .at[:, segment_index]
            .add(returned[0]),
            (frac_volume * (frac_hydrogen_mass - frac_old_hydrogen))
            .at[:, segment_index]
            .add(returned[1]),
            closure_residual(frac_pressure, frac_saturation, frac_dissolved),
        ]
    )

    def jacobian(direction):
        step_cells, step_frac = direction
        cell_steps = phase_steps(
            pressure, saturation, dissolved, step_cells[0], step_cells[1], step_cells[2]
        )
        step_pad = with_halo(
            jnp.stack([step_cells[0], cell_steps[0], cell_steps[1], cell_steps[2]]),
            (("gx", 2), ("gy", 3), ("gz", 1)),
            1,
        )
        step_padded = (step_pad[0], step_pad[1], step_pad[2], step_pad[3])
        step_water_div, step_hydrogen_div = flux_divergence(base_padded, step_padded)
        step_water_mass, step_hydrogen_mass = mass_steps(
            pressure, saturation, dissolved, step_cells[0], step_cells[1], step_cells[2]
        )
        frac_steps = phase_steps(
            frac_pressure, frac_saturation, frac_dissolved, step_frac[0], step_frac[1], step_frac[2]
        )
        frac_mass_steps = mass_steps(
            frac_pressure, frac_saturation, frac_dissolved, step_frac[0], step_frac[1], step_frac[2]
        )
        step_rows = send_rows(
            jnp.take(
                jnp.stack([step_frac[0], frac_steps[0], frac_steps[1] + frac_steps[2]]),
                segment_index,
                axis=2,
            )
        )
        step_cell_rows = jnp.take(
            jnp.stack([step_cells[0], cell_steps[0], cell_steps[1] + cell_steps[2]]).reshape(
                3, layers, columns_total
            ),
            column_index,
            axis=2,
        )
        step_gap = step_rows[0] - step_cell_rows[0]
        step_water_rate = pair_weight * (
            0.5 * (step_rows[1] + step_cell_rows[1]) * pressure_gap
            + 0.5 * (frac_rows[1] + cell_rows[1]) * step_gap
        )
        step_hydrogen_rate = pair_weight * (
            0.5 * (step_rows[2] + step_cell_rows[2]) * pressure_gap
            + 0.5 * (frac_rows[2] + cell_rows[2]) * step_gap
        )
        step_returned = return_rates(jnp.stack([step_water_rate, step_hydrogen_rate]))
        matrix_image = jnp.stack(
            [
                add_columns(
                    pore_volume * step_water_mass + step_water_div, column_index, -step_water_rate
                ),
                add_columns(
                    pore_volume * step_hydrogen_mass + step_hydrogen_div,
                    column_index,
                    -step_hydrogen_rate,
                ),
                closure_step(
                    pressure, saturation, dissolved, step_cells[0], step_cells[1], step_cells[2]
                ),
            ]
        )
        frac_image = jnp.stack(
            [
                (frac_volume * frac_mass_steps[0]).at[:, segment_index].add(step_returned[0]),
                (frac_volume * frac_mass_steps[1]).at[:, segment_index].add(step_returned[1]),
                closure_step(
                    frac_pressure,
                    frac_saturation,
                    frac_dissolved,
                    step_frac[0],
                    step_frac[1],
                    step_frac[2],
                ),
            ]
        )
        return (matrix_image, frac_image)

    residual_pair = (matrix_res, frac_res)
    initial_norm = jnp.sqrt(
        lax.psum(inner_product(residual_pair, residual_pair), ("gx", "gy", "gz")) + NORM_SHIFT
    )
    first = (-matrix_res / initial_norm, -frac_res / initial_norm)
    image = jacobian(first)
    first_coef = lax.psum(inner_product(image, first), ("gx", "gy", "gz"))
    left_over = (image[0] - first_coef * first[0], image[1] - first_coef * first[1])
    first_length = jnp.sqrt(
        lax.psum(inner_product(left_over, left_over), ("gx", "gy", "gz")) + NORM_SHIFT
    )
    second = (left_over[0] / first_length, left_over[1] / first_length)
    second_image = jacobian(second)
    coef_one, coef_two = lax.psum(
        (inner_product(second_image, first), inner_product(second_image, second)),
        ("gx", "gy", "gz"),
    )
    remainder = (
        second_image[0] - coef_one * first[0] - coef_two * second[0],
        second_image[1] - coef_one * first[1] - coef_two * second[1],
    )
    second_length = jnp.sqrt(
        lax.psum(inner_product(remainder, remainder), ("gx", "gy", "gz")) + NORM_SHIFT
    )
    rotate_norm = jnp.sqrt(first_coef * first_coef + first_length * first_length)
    cosine = first_coef / rotate_norm
    sine_part = first_length / rotate_norm
    upper_coef = cosine * coef_one + sine_part * coef_two
    lower_coef = cosine * coef_two - sine_part * coef_one
    weight_two = (
        -sine_part
        * initial_norm
        * lower_coef
        / (lower_coef * lower_coef + second_length * second_length)
    )
    weight_one = (cosine * initial_norm - upper_coef * weight_two) / rotate_norm
    newton_step = weight_one * first[0] + weight_two * second[0]
    frac_newton_step = weight_one * first[1] + weight_two * second[1]
    return (newton_step, frac_newton_step, matrix_res, frac_res)


def solution(mesh):
    placed = (
        P("gz", "gx", "gy"),
        P("gz", "gx", "gy"),
        P("gz", "gx", "gy"),
        P("gz", "gx", "gy"),
        P("gz", "gx", "gy"),
        P("gz", "gx", "gy"),
        P("gz", "gx", "gy"),
        P("gz", ("gx", "gy")),
        P("gz", ("gx", "gy")),
        P("gz", ("gx", "gy")),
        P("gz", ("gx", "gy")),
        P("gz", ("gx", "gy")),
        P("gz", ("gx", "gy")),
        P(("gx", "gy"), None),
        P(("gx", "gy"), None),
        P(("gx", "gy"), None),
        P(("gx", "gy"), None),
        P(),
    )
    return jax.shard_map(
        on_device,
        mesh=mesh,
        in_specs=placed,
        out_specs=(
            P(None, "gz", "gx", "gy"),
            P(None, "gz", ("gx", "gy")),
            P(None, "gz", "gx", "gy"),
            P(None, "gz", ("gx", "gy")),
        ),
        check_vma=False,
    )
```

profile of v0, /device:TPU:0, one launch (start us, length us, event | category | flops | bytes accessed | tf_op | source)
XLA Modules:
  0.0 770.2 jit_solution(1601846299745156565)
XLA Ops:
  6.3 5.5 collective-permute-start
  23.6 7.3 all-to-all-start
  38.5 3.7 fusion.174
  49.7 5.2 collective-permute-start.2
  70.5 4.4 collective-permute-start.4
  83.8 7.4 pad_maximum_fusion.2
  108.0 7.2 copy.718
  115.2 5.1 gather_fusion.1
  125.1 5.5 scatter_fusion.1
  137.4 5.0 scatter_fusion
  148.9 6.0 all-to-all-start.1
  158.5 4.0 all-to-all-done.1
  167.0 3.7 scatter_fusion.3
  171.6 3.7 scatter_fusion.2
  179.6 38.6 %psum.42 = f32[]{:T(128)} all-reduce(f32[]{:T(128)S(6)} %add.726), channel_id=1, replica_groups=mesh['gx'=4,'gy'=4,'gz'=2] {'gx','gy','gz'}, use_global_device_ids=true, to_apply=%region_7.10 | all-reduce | flops 1 | bytes 8 | tf_op jit(solution)/shard_map/psum | solution.py:364
  225.2 5.4 collective-permute-start.6
  243.3 4.9 all-to-all-start.2
  251.3 5.5 copy.743
  269.9 5.2 collective-permute-start.8
  275.0 10.2 %pad_maximum_fusion = f32[3,32,4096]{1,0,2:T(4,128)} fusion(f32[1,32,4096]{1,0,2:T(1,128)} %bitcast.581, f32[1,32,4096]{1,0,2:T(1,128)} %bitcast.580, f32[1,32,4096]{1,0,2:T(1,128)} %copy.743), kind=kLoop, calls=%fused_computation.18 | loop fusion | flops 786432 | bytes 3145728 | tf_op jit(solution)/shard_map/stack | solution.py:315
  285.2 5.2 gather_fusion.3
  298.9 7.2 pad_maximum_fusion.5
  308.1 4.3 collective-permute-start.10
  316.1 7.9 %pad_maximum_fusion.3 = f32[4,34,34,130]{3,2,1,0:T(8,128)S(1)} fusion(f32[4,1,34,130]{3,2,1,0:T(8,128)} %collective-permute-done.11, f32[4,32,34,1]{3,2,1,0:T(8,128)} %copy.739, f32[4,32,1,128]{3,2,1,0:T(1,128)} %collective-permute-done.7, f32[1,32,32,128]{3,2,1,0:T(8,128)} %bitcast.567, f32[1,32,32,128]{3,2,1,0:T(8,128)} %bitcast.563, ...), kind=kLoop, calls=%fused_computation.21 | loop fusion | flops 5410080 | bytes 4808960 | tf_op jit(solution)/shard_map/concatenate | solution.py:27
  326.0 4.1 fusion.23
  363.0 5.1 scatter_fusion.5
  371.8 5.4 scatter_fusion.4
  383.8 6.2 all-to-all-start.3
  392.8 4.6 all-to-all-done.3
  406.5 3.7 scatter_fusion.6
  413.1 38.6 %psum.43 = f32[]{:T(128)} all-reduce(f32[]{:T(128)S(6)} %add.784), channel_id=1, replica_groups=mesh['gx'=4,'gy'=4,'gz'=2] {'gx','gy','gz'}, use_global_device_ids=true, to_apply=%region_14.17 | all-reduce | flops 1 | bytes 8 | tf_op jit(solution)/shard_map/psum | solution.py:368
  457.8 40.1 %psum.44 = f32[]{:T(128)} all-reduce(f32[]{:T(128)S(6)} %add.785), channel_id=1, replica_groups=mesh['gx'=4,'gy'=4,'gz'=2] {'gx','gy','gz'}, use_global_device_ids=true, to_apply=%region_17.20 | all-reduce | flops 1 | bytes 8 | tf_op jit(solution)/shard_map/psum | solution.py:371
  512.3 5.6 collective-permute-start.12
  521.0 5.5 copy.767
  526.5 10.2 %pad_maximum_fusion.1 = f32[3,32,4096]{1,0,2:T(4,128)} fusion(f32[1,32,4096]{1,0,2:T(1,128)} %bitcast.583, f32[1,32,4096]{1,0,2:T(1,128)} %bitcast.582, f32[1,32,4096]{1,0,2:T(1,128)} %copy.767), kind=kLoop, calls=%fused_computation.19 | loop fusion | flops 786432 | bytes 3145728 | tf_op jit(solution)/shard_map/stack | solution.py:315
  555.3 5.2 collective-permute-start.14
  562.6 5.2 gather_fusion.5
  576.3 7.2 pad_maximum_fusion.6
  585.6 4.4 collective-permute-start.16
  594.1 4.2 all-to-all-start.4
  601.3 7.9 %pad_maximum_fusion.4 = f32[4,34,34,130]{3,2,1,0:T(8,128)S(1)} fusion(f32[4,1,34,130]{3,2,1,0:T(8,128)} %collective-permute-done.17, f32[4,32,34,1]{3,2,1,0:T(8,128)} %copy.763, f32[4,32,1,128]{3,2,1,0:T(1,128)} %copy-done.69, f32[1,32,32,128]{3,2,1,0:T(8,128)} %bitcast.559, f32[1,32,32,128]{3,2,1,0:T(8,128)} %bitcast.555, f32[1,32,32,128]{3,2,1,0:T(8,128)} %bitcast.545, ...), kind=kLoop, calls=%fused_computation.22 | loop fusion | flops 5410080 | bytes 4808960 | tf_op jit(solution)/shard_map/concatenate | solution.py:27
  611.2 4.1 fusion.11
  635.0 5.0 scatter_fusion.8
  645.8 6.9 all-to-all-start.5
  655.9 4.3 all-to-all-done.5
  676.2 38.6 %all-reduce = (f32[]{:T(128)}, f32[]{:T(128)}) all-reduce(f32[]{:T(128)S(6)} %add.845, f32[]{:T(128)S(6)} %add.844), channel_id=1, replica_groups=mesh['gx'=4,'gy'=4,'gz'=2] {'gx','gy','gz'}, use_global_device_ids=true, to_apply=%region_27.30 | all-reduce | flops 2 | bytes 16 | tf_op jit(solution)/shard_map/psum | solution.py:375
  716.0 4.4 multiply_reduce_fusion
  725.4 40.0 %psum.47 = f32[]{:T(128)} all-reduce(f32[]{:T(128)S(6)} %add.847), channel_id=1, replica_groups=mesh['gx'=4,'gy'=4,'gz'=2] {'gx','gy','gz'}, use_global_device_ids=true, to_apply=%region_30.33 | all-reduce | flops 1 | bytes 8 | tf_op jit(solution)/shard_map/psum | solution.py:384
  (441 shorter events, 319.2 us)
Async XLA Ops:
  5.1 33.0 %collective-permute-start.1 = (f32[5,32,1,128]{3,2,1,0:T(1,128)}, f32[5,32,1,128]{3,2,1,0:T(1,128)S(1)}, u32[]{:S(2)}, u32[]{:S(2)}) collective-permute-start(f32[5,32,1,128]{3,2,1,0:T(1,128)} %get-tuple-element.108), channel_id=1, source_target_pairs={{8,0},{16,8},{24,16},{9,1},{17,9},{25,17},{10,2},{18,10},{26,18},{... | collective-permute-start | bytes 245768 | tf_op jit(solution)/shard_map/ppermute | solution.py:26
  6.3 31.7 %collective-permute-start = (f32[5,32,1,128]{3,2,1,0:T(1,128)S(1)}, f32[5,32,1,128]{3,2,1,0:T(1,128)S(1)}, u32[]{:S(2)}, u32[]{:S(2)}) collective-permute-start(f32[5,32,1,128]{3,2,1,0:T(1,128)S(1)} %get-tuple-element.107), channel_id=1, source_target_pairs={{0,8},{8,16},{16,24},{1,9},{9,17},{17,25},{2,10},{10,18},{18,26},{... | collective-permute-start | bytes 245768 | tf_op jit(solution)/shard_map/ppermute | solution.py:25
  23.6 51.3 %all-to-all-start = ((f32[16,1,1536]{2,1,0:T(1,128)}), f32[16,1,1536]{2,1,0:T(1,128)S(1)}, u32[]{:S(2)}, u32[]{:S(2)}) async-start(f32[16,1,1536]{2,1,0:T(1,128)} %reshape.384), calls=%async_computation | async-start | bytes 196608 | tf_op jit(solution)/shard_map/all_to_all | solution.py:184
  45.0 15.4 %collective-permute-start.3 = (f32[5,32,34,1]{2,1,3,0:T(8,128)S(1)}, f32[5,32,34,1]{2,1,3,0:T(8,128)}, u32[]{:S(2)}, u32[]{:S(2)}) collective-permute-start(f32[5,32,34,1]{2,1,3,0:T(8,128)S(1)} %copy.712), channel_id=1, source_target_pairs={{2,0},{4,2},{6,4},{3,1},{5,3},{7,5},{10,8},{12,10},{14,12},{11,9},... | collective-permute-start | bytes 65288 | tf_op jit(solution)/shard_map/ppermute | solution.py:26
  49.7 14.1 %collective-permute-start.2 = (f32[5,32,34,1]{2,1,3,0:T(8,128)}, f32[5,32,34,1]{2,1,3,0:T(8,128)}, u32[]{:S(2)}, u32[]{:S(2)}) collective-permute-start(f32[5,32,34,1]{2,1,3,0:T(8,128)} %copy.711), channel_id=1, source_target_pairs={{0,2},{2,4},{4,6},{1,3},{3,5},{5,7},{8,10},{10,12},{12,14},{9,11},... | collective-permute-start | bytes 65288 | tf_op jit(solution)/shard_map/ppermute | solution.py:25
  69.2 14.6 %collective-permute-start.5 = (f32[5,1,34,130]{3,2,1,0:T(8,128)}, f32[5,1,34,130]{3,2,1,0:T(8,128)}, u32[]{:S(2)}, u32[]{:S(2)}) collective-permute-start(f32[5,1,34,130]{3,2,1,0:T(8,128)} %get-tuple-element.69), channel_id=1, source_target_pairs={{1,0},{3,2},{5,4},{7,6},{9,8},{11,10},{13,12},{15,14},{17,16},{19,... | collective-permute-start | bytes 265208 | tf_op jit(solution)/shard_map/ppermute | solution.py:26
  70.5 13.3 %collective-permute-start.4 = (f32[5,1,34,130]{3,2,1,0:T(8,128)}, f32[5,1,34,130]{3,2,1,0:T(8,128)}, u32[]{:S(2)}, u32[]{:S(2)}) collective-permute-start(f32[5,1,34,130]{3,2,1,0:T(8,128)} %get-tuple-element.68), channel_id=1, source_target_pairs={{0,1},{2,3},{4,5},{6,7},{8,9},{10,11},{12,13},{14,15},{16,17},{18,... | collective-permute-start | bytes 265208 | tf_op jit(solution)/shard_map/ppermute | solution.py:25
  108.0 13.5 %copy-start.105 = (pred[256]{0:T(512)(128)(4,1)S(1)}, pred[256]{0:T(512)(128)(4,1)}, u32[]{:S(2)}) copy-start(pred[256]{0:T(512)(128)(4,1)} %compare_and_fusion) | copy-start | bytes 772
  108.0 13.6 %copy-start.100 = (f32[256]{0:T(256)S(1)}, f32[256]{0:T(256)}, u32[]{:S(2)}) copy-start(f32[256]{0:T(256)} %get-tuple-element.64) | copy-start | bytes 3076
  108.0 17.1 %copy-start.96 = (s32[256,1]{0,1:T(1,128)S(1)}, s32[256,1]{0,1:T(1,128)}, u32[]{:S(2)}) copy-start(s32[256,1]{0,1:T(1,128)} %compare_select_fusion.1) | copy-start | bytes 3076
  123.0 235.6 %copy-start.67 = (f32[1,32,256]{2,1,0:T(8,128)}, f32[1,32,256]{2,1,0:T(8,128)S(1)}, u32[]{:S(2)}) copy-start(f32[1,32,256]{2,1,0:T(8,128)S(1)} %get-tuple-element.49) | copy-start | bytes 98308
  124.4 235.7 %copy-start.65 = (f32[1,32,256]{2,1,0:T(8,128)}, f32[1,32,256]{2,1,0:T(8,128)S(1)}, u32[]{:S(2)}) copy-start(f32[1,32,256]{2,1,0:T(8,128)S(1)} %get-tuple-element.52) | copy-start | bytes 98308
  148.9 13.6 %all-to-all-start.1 = ((f32[16,1,1024]{2,1,0:T(1,128)}), f32[16,1,1024]{2,1,0:T(1,128)}, u32[]{:S(2)}, u32[]{:S(2)}) async-start(f32[16,1,1024]{2,1,0:T(1,128)} %reshape.386), calls=%async_computation.1 | async-start | bytes 131072 | tf_op jit(solution)/shard_map/all_to_all | solution.py:188
  178.3 590.1 %copy-start.52 = (f32[3,32,256]{2,1,0:T(8,128)}, f32[3,32,256]{2,1,0:T(8,128)S(1)}, u32[]{:S(2)}) copy-start(f32[3,32,256]{2,1,0:T(8,128)S(1)} %get-tuple-element.47) | copy-start | bytes 294916
  222.1 14.0 %copy-start.103 = (pred[256]{0:T(512)(128)(4,1)S(1)}, pred[256]{0:T(512)(128)(4,1)}, u32[]{:S(2)}) copy-start(pred[256]{0:T(512)(128)(4,1)} %compare_and_fusion.1) | copy-start | bytes 772
  223.1 281.4 %copy-start.59 = (f32[1,32,256]{2,1,0:T(8,128)}, f32[1,32,256]{2,1,0:T(8,128)S(1)}, u32[]{:S(2)}) copy-start(f32[1,32,256]{2,1,0:T(8,128)S(1)} %get-tuple-element.140) | copy-start | bytes 98308
  223.9 32.9 %collective-permute-start.7 = (f32[4,32,1,128]{3,2,1,0:T(1,128)}, f32[4,32,1,128]{3,2,1,0:T(1,128)}, u32[]{:S(2)}, u32[]{:S(2)}) collective-permute-start(f32[4,32,1,128]{3,2,1,0:T(1,128)} %get-tuple-element.112), channel_id=1, source_target_pairs={{8,0},{16,8},{24,16},{9,1},{17,9},{25,17},{10,2},{18,10},{26,18},{... | collective-permute-start | bytes 196616 | tf_op jit(solution)/shard_map/ppermute | solution.py:26
  225.2 31.6 %collective-permute-start.6 = (f32[4,32,1,128]{3,2,1,0:T(1,128)}, f32[4,32,1,128]{3,2,1,0:T(1,128)}, u32[]{:S(2)}, u32[]{:S(2)}) collective-permute-start(f32[4,32,1,128]{3,2,1,0:T(1,128)} %get-tuple-element.111), channel_id=1, source_target_pairs={{0,8},{8,16},{16,24},{1,9},{9,17},{17,25},{2,10},{10,18},{18,26},{... | collective-permute-start | bytes 196616 | tf_op jit(solution)/shard_map/ppermute | solution.py:25
  243.3 102.1 %all-to-all-start.2 = ((f32[16,1,1536]{2,1,0:T(1,128)}), f32[16,1,1536]{2,1,0:T(1,128)}, u32[]{:S(2)}, u32[]{:S(2)}) async-start(f32[16,1,1536]{2,1,0:T(1,128)} %reshape.388), calls=%async_computation.2 | async-start | bytes 196608 | tf_op jit(solution)/shard_map/all_to_all | solution.py:184
  265.2 27.0 %collective-permute-start.9 = (f32[4,32,34,1]{2,1,3,0:T(8,128)}, f32[4,32,34,1]{2,1,3,0:T(8,128)}, u32[]{:S(2)}, u32[]{:S(2)}) collective-permute-start(f32[4,32,34,1]{2,1,3,0:T(8,128)} %copy.737), channel_id=1, source_target_pairs={{2,0},{4,2},{6,4},{3,1},{5,3},{7,5},{10,8},{12,10},{14,12},{11,9},... | collective-permute-start | bytes 52232 | tf_op jit(solution)/shard_map/ppermute | solution.py:26
  269.9 25.6 %collective-permute-start.8 = (f32[4,32,34,1]{2,1,3,0:T(8,128)}, f32[4,32,34,1]{2,1,3,0:T(8,128)}, u32[]{:S(2)}, u32[]{:S(2)}) collective-permute-start(f32[4,32,34,1]{2,1,3,0:T(8,128)} %copy.736), channel_id=1, source_target_pairs={{0,2},{2,4},{4,6},{1,3},{3,5},{5,7},{8,10},{10,12},{12,14},{9,11},... | collective-permute-start | bytes 52232 | tf_op jit(solution)/shard_map/ppermute | solution.py:25
  298.8 13.6 %copy-start.77 = (f32[256,3,32]{0,2,1:T(8,128)S(1)}, f32[256,3,32]{0,2,1:T(8,128)}, u32[]{:S(2)}) copy-start(f32[256,3,32]{0,2,1:T(8,128)} %copy.746) | copy-start | bytes 294916
  298.9 13.6 %copy-start.106 = (pred[256]{0:T(512)(128)(4,1)S(1)}, pred[256]{0:T(512)(128)(4,1)}, u32[]{:S(2)}) copy-start(pred[256]{0:T(512)(128)(4,1)} %compare_and_fusion) | copy-start | bytes 772
  306.8 9.3 %collective-permute-start.11 = (f32[4,1,34,130]{3,2,1,0:T(8,128)}, f32[4,1,34,130]{3,2,1,0:T(8,128)}, u32[]{:S(2)}, u32[]{:S(2)}) collective-permute-start(f32[4,1,34,130]{3,2,1,0:T(8,128)} %get-tuple-element.86), channel_id=1, source_target_pairs={{1,0},{3,2},{5,4},{7,6},{9,8},{11,10},{13,12},{15,14},{17,16},{19,... | collective-permute-start | bytes 212168 | tf_op jit(solution)/shard_map/ppermute | solution.py:26
  308.1 8.0 %collective-permute-start.10 = (f32[4,1,34,130]{3,2,1,0:T(8,128)}, f32[4,1,34,130]{3,2,1,0:T(8,128)}, u32[]{:S(2)}, u32[]{:S(2)}) collective-permute-start(f32[4,1,34,130]{3,2,1,0:T(8,128)} %get-tuple-element.85), channel_id=1, source_target_pairs={{0,1},{2,3},{4,5},{6,7},{8,9},{10,11},{12,13},{14,15},{16,17},{18,... | collective-permute-start | bytes 212168 | tf_op jit(solution)/shard_map/ppermute | solution.py:25
  342.4 14.7 %copy-start.97 = (f32[256]{0:T(256)S(1)}, f32[256]{0:T(256)}, u32[]{:S(2)}) copy-start(f32[256]{0:T(256)} %get-tuple-element.65) | copy-start | bytes 3076
  383.8 13.7 %all-to-all-start.3 = ((f32[16,1,1024]{2,1,0:T(1,128)}), f32[16,1,1024]{2,1,0:T(1,128)}, u32[]{:S(2)}, u32[]{:S(2)}) async-start(f32[16,1,1024]{2,1,0:T(1,128)} %reshape.390), calls=%async_computation.3 | async-start | bytes 131072 | tf_op jit(solution)/shard_map/all_to_all | solution.py:188
  406.5 97.9 %copy-start.61 = (f32[32,256]{1,0:T(8,128)}, f32[32,256]{1,0:T(8,128)S(1)}, u32[]{:S(2)}) copy-start(f32[32,256]{1,0:T(8,128)S(1)} %copy.759) | copy-start | bytes 98308
  411.2 93.3 %copy-start.63 = (f32[32,256]{1,0:T(8,128)}, f32[32,256]{1,0:T(8,128)S(1)}, u32[]{:S(2)}) copy-start(f32[32,256]{1,0:T(8,128)S(1)} %copy.757) | copy-start | bytes 98308
  511.0 31.2 %collective-permute-start.13 = (f32[4,32,1,128]{3,2,1,0:T(1,128)}, f32[4,32,1,128]{3,2,1,0:T(1,128)S(1)}, u32[]{:S(2)}, u32[]{:S(2)}) collective-permute-start(f32[4,32,1,128]{3,2,1,0:T(1,128)} %get-tuple-element.110), channel_id=1, source_target_pairs={{8,0},{16,8},{24,16},{9,1},{17,9},{25,17},{10,2},{18,10},{26,18},{... | collective-permute-start | bytes 196616 | tf_op jit(solution)/shard_map/ppermute | solution.py:26
  512.3 29.9 %collective-permute-start.12 = (f32[4,32,1,128]{3,2,1,0:T(1,128)}, f32[4,32,1,128]{3,2,1,0:T(1,128)}, u32[]{:S(2)}, u32[]{:S(2)}) collective-permute-start(f32[4,32,1,128]{3,2,1,0:T(1,128)} %get-tuple-element.109), channel_id=1, source_target_pairs={{0,8},{8,16},{16,24},{1,9},{9,17},{17,25},{2,10},{10,18},{18,26},{... | collective-permute-start | bytes 196616 | tf_op jit(solution)/shard_map/ppermute | solution.py:25
  542.2 34.1 %copy-start.69 = (f32[4,32,1,128]{3,2,1,0:T(1,128)}, f32[4,32,1,128]{3,2,1,0:T(1,128)S(1)}, u32[]{:S(2)}) copy-start(f32[4,32,1,128]{3,2,1,0:T(1,128)S(1)} %collective-permute-done.13) | copy-start | bytes 196612
  547.3 13.2 %copy-start.104 = (pred[256]{0:T(512)(128)(4,1)S(1)}, pred[256]{0:T(512)(128)(4,1)}, u32[]{:S(2)}) copy-start(pred[256]{0:T(512)(128)(4,1)} %compare_and_fusion.1) | copy-start | bytes 772
  550.6 19.0 %collective-permute-start.15 = (f32[4,32,34,1]{2,1,3,0:T(8,128)}, f32[4,32,34,1]{2,1,3,0:T(8,128)}, u32[]{:S(2)}, u32[]{:S(2)}) collective-permute-start(f32[4,32,34,1]{2,1,3,0:T(8,128)} %copy.761), channel_id=1, source_target_pairs={{2,0},{4,2},{6,4},{3,1},{5,3},{7,5},{10,8},{12,10},{14,12},{11,9},... | collective-permute-start | bytes 52232 | tf_op jit(solution)/shard_map/ppermute | solution.py:26
  555.3 17.7 %collective-permute-start.14 = (f32[4,32,34,1]{2,1,3,0:T(8,128)}, f32[4,32,34,1]{2,1,3,0:T(8,128)}, u32[]{:S(2)}, u32[]{:S(2)}) collective-permute-start(f32[4,32,34,1]{2,1,3,0:T(8,128)} %copy.760), channel_id=1, source_target_pairs={{0,2},{2,4},{4,6},{1,3},{3,5},{5,7},{8,10},{10,12},{12,14},{9,11},... | collective-permute-start | bytes 52232 | tf_op jit(solution)/shard_map/ppermute | solution.py:25
  576.3 13.6 %copy-start.76 = (f32[256,3,32]{0,2,1:T(8,128)S(1)}, f32[256,3,32]{0,2,1:T(8,128)}, u32[]{:S(2)}) copy-start(f32[256,3,32]{0,2,1:T(8,128)} %copy.770) | copy-start | bytes 294916
  576.3 13.6 %copy-start.107 = (pred[256]{0:T(512)(128)(4,1)S(1)}, pred[256]{0:T(512)(128)(4,1)}, u32[]{:S(2)}) copy-start(pred[256]{0:T(512)(128)(4,1)} %compare_and_fusion) | copy-start | bytes 772
  584.3 17.0 %collective-permute-start.17 = (f32[4,1,34,130]{3,2,1,0:T(8,128)}, f32[4,1,34,130]{3,2,1,0:T(8,128)}, u32[]{:S(2)}, u32[]{:S(2)}) collective-permute-start(f32[4,1,34,130]{3,2,1,0:T(8,128)} %get-tuple-element.84), channel_id=1, source_target_pairs={{1,0},{3,2},{5,4},{7,6},{9,8},{11,10},{13,12},{15,14},{17,16},{19,... | collective-permute-start | bytes 212168 | tf_op jit(solution)/shard_map/ppermute | solution.py:26
  585.6 15.7 %collective-permute-start.16 = (f32[4,1,34,130]{3,2,1,0:T(8,128)}, f32[4,1,34,130]{3,2,1,0:T(8,128)}, u32[]{:S(2)}, u32[]{:S(2)}) collective-permute-start(f32[4,1,34,130]{3,2,1,0:T(8,128)} %get-tuple-element.83), channel_id=1, source_target_pairs={{0,1},{2,3},{4,5},{6,7},{8,9},{10,11},{12,13},{14,15},{16,17},{18,... | collective-permute-start | bytes 212168 | tf_op jit(solution)/shard_map/ppermute | solution.py:25
  594.1 32.1 %all-to-all-start.4 = ((f32[16,1,1536]{2,1,0:T(1,128)}), f32[16,1,1536]{2,1,0:T(1,128)}, u32[]{:S(2)}, u32[]{:S(2)}) async-start(f32[16,1,1536]{2,1,0:T(1,128)} %reshape.392), calls=%async_computation.4 | async-start | bytes 196608 | tf_op jit(solution)/shard_map/all_to_all | solution.py:184
  634.9 17.8 %copy-start.3 = (f32[3,32,32,128]{3,2,1,0:T(8,128)S(1)}, f32[3,32,32,128]{3,2,1,0:T(8,128)}, u32[]{:S(2)}) copy-start(f32[3,32,32,128]{3,2,1,0:T(8,128)} %get-tuple-element.54) | copy-start | bytes 4718596
  634.9 17.8 %copy-start.24 = (f32[1,32,32,128]{3,2,1,0:T(8,128)S(1)}, f32[1,32,32,128]{3,2,1,0:T(8,128)}, u32[]{:S(2)}) copy-start(f32[1,32,32,128]{3,2,1,0:T(8,128)} %copy.754) | copy-start | bytes 1572868
  634.9 17.8 %copy-start.25 = (f32[1,32,32,128]{3,2,1,0:T(8,128)S(1)}, f32[1,32,32,128]{3,2,1,0:T(8,128)}, u32[]{:S(2)}) copy-start(f32[1,32,32,128]{3,2,1,0:T(8,128)} %copy.753) | copy-start | bytes 1572868
  634.9 17.8 %copy-start.26 = (f32[1,32,32,128]{3,2,1,0:T(8,128)S(1)}, f32[1,32,32,128]{3,2,1,0:T(8,128)}, u32[]{:S(2)}) copy-start(f32[1,32,32,128]{3,2,1,0:T(8,128)} %get-tuple-element.97) | copy-start | bytes 1572868
  645.8 14.4 %all-to-all-start.5 = ((f32[16,1,1024]{2,1,0:T(1,128)}), f32[16,1,1024]{2,1,0:T(1,128)}, u32[]{:S(2)}, u32[]{:S(2)}) async-start(f32[16,1,1024]{2,1,0:T(1,128)} %reshape.394), calls=%async_computation.5 | async-start | bytes 131072 | tf_op jit(solution)/shard_map/all_to_all | solution.py:188
  652.8 13.4 %copy-start.58 = (f32[32,256]{0,1:T(8,128)S(1)}, f32[32,256]{0,1:T(8,128)}, u32[]{:S(2)}) copy-start(f32[32,256]{0,1:T(8,128)} %copy.781) | copy-start | bytes 98308
  652.8 16.5 %copy-start.57 = (f32[32,256]{0,1:T(8,128)S(1)}, f32[32,256]{0,1:T(8,128)}, u32[]{:S(2)}) copy-start(f32[32,256]{0,1:T(8,128)} %copy.779) | copy-start | bytes 98308
  655.9 15.8 %copy-start.60 = (f32[1,32,256]{2,1,0:T(8,128)S(1)}, f32[1,32,256]{2,1,0:T(8,128)}, u32[]{:S(2)}) copy-start(f32[1,32,256]{2,1,0:T(8,128)} %copy-done.59) | copy-start | bytes 98308
  (86 other events, 310.8 us)
where the time goes:
time: 783 us; the launch traced here: 770 us
  other arithmetic  230 us (29%)
  local copies, waits for them, and re-layouts  222 us (28%)
  blocking collectives  196 us (25%)
  starting transfers between devices  92.1 us (12%)
  between operations  16.6 us (2%)
  waiting for transfers between devices  13 us (2%)
    ppermute x9, starting transfers between devices, with_halo(): before = lax.ppermute(last, axis, up)  45.1 us
    concatenate x8, other arithmetic, with_halo(): shard = jnp.concatenate([before, shard, after], axis=dim)  41.9 us
    psum x1, blocking collectives, on_device(): lax.psum(inner_product(left_over, left_over), ('gx', 'gy', 'gz'))  40.1 us
    psum x1, blocking collectives, on_device(): lax.psum(inner_product(remainder, remainder), ('gx', 'gy', 'gz'))  40 us
    psum x1, blocking collectives, on_device(): lax.psum((inner_product(second_image, first), inner_product(second_image,...  38.6 us
    psum x1, blocking collectives, on_device(): lax.psum(inner_product(residual_pair, residual_pair), ('gx', 'gy', 'gz'))  38.6 us
    psum x1, blocking collectives, on_device(): first_coef = lax.psum(inner_product(image, first), ('gx', 'gy', 'gz'))  38.6 us
    unnamed x241, local copies, waits for them, and re-layouts  35.4 us
  transfers between devices with their start and end apart: 24, of which 3 were waited for; matrix products, arithmetic and copies ran while one was open for 29% of the time, Pallas kernels for 0%

commit v1 on v0

v1 whole, which is shorter than its diff:
```python
import functools

import jax
import jax.numpy as jnp
from jax import lax
from jax.experimental import pallas as pl
from jax.experimental.pallas import tpu as pltpu
from jax.sharding import PartitionSpec as P

F32 = jnp.float32
BF16 = jnp.bfloat16
EPS = 1e-06
PLANE = ("gx", "gy")


def swap_slots(mesh_shape):
    slots = []
    for axis in ("gx", "gy", "gz"):
        if mesh_shape[axis] > 1:
            slots.append((axis, 0))
        if mesh_shape[axis] > 2:
            slots.append((axis, 1))
    return tuple(slots)


def swap_pairs(size, odd):
    pairs = []
    for i in range(size):
        up = i % 2 == odd
        partner = (i + 1 if up else i - 1) % size
        pairs.append((i, partner))
    if sorted(j for _, j in pairs) != list(range(size)):
        pairs = [(i, j if abs(i - j) == 1 else i) for i, j in pairs]
    return pairs


def slot_side(axis, odd, sizes):
    index = lax.axis_index(axis)
    high = lax.rem(index, 2) == odd
    valid = jnp.where(high, index + 1 < sizes[axis], index > 0)
    return high, valid


def mobilities(p, s, d):
    share = (1.0 - s) * (1.0 - s)
    scaled = (1.0 + 0.05 * p) * share
    mg = (2.0 + p) * (s * s)
    return scaled * (1.0 - d), scaled * d + mg, mg


def mobility_steps(p, s, d, dp, ds, dd):
    lb = 1.0 + 0.05 * p
    open_s = 1.0 - s
    share = open_s * open_s
    scaled = lb * share
    gas = 2.0 + p
    mg = gas * (s * s)
    step = (0.05 * share) * dp - (2.0 * (lb * open_s)) * ds
    dmg = s * (s * dp + (2.0 * gas) * ds)
    step_d = scaled * dd
    return (
        scaled * (1.0 - d),
        scaled * d + mg,
        mg,
        step * (1.0 - d) - step_d,
        step * d + step_d + dmg,
        dmg,
    )


def masses(p, s, d):
    lb_open = (1.0 + 0.05 * p) * (1.0 - s)
    return lb_open * (1.0 - d), lb_open * d + (0.2 + 0.1 * p) * s


def mass_steps(p, s, d, dp, ds, dd):
    lb = 1.0 + 0.05 * p
    open_s = 1.0 - s
    step = (0.05 * open_s) * dp - lb * ds
    step_d = (lb * open_s) * dd
    return (
        step * (1.0 - d) - step_d,
        step * d + step_d + (0.1 * s) * dp + (0.2 + 0.1 * p) * ds,
    )


def closure(p, s, d):
    gap = 0.05 + 0.025 * p - d
    return s + gap - jnp.sqrt(s * s + gap * gap + 1e-4)


def closure_step(p, s, d, dp, ds, dd):
    gap = 0.05 + 0.025 * p - d
    inverse = lax.rsqrt(s * s + gap * gap + 1e-4)
    dgap = 0.025 * dp - dd
    return ds + dgap - (s * ds + gap * dgap) * inverse


def halves(value):
    high = value.astype(BF16)
    return high, (value - high.astype(F32)).astype(BF16)


def split_dot(value, weights, dims):
    high, low = halves(value)
    dot = functools.partial(
        lax.dot_general, dimension_numbers=(dims, ((), ())), preferred_element_type=F32
    )
    return dot(high, weights) + dot(low, weights)


def one_hot(size, index_row):
    shape = (size, index_row.shape[1])
    rows = lax.broadcasted_iota(jnp.int32, shape, 0)
    return jnp.where(rows == index_row, 1.0, 0.0)


class Plan:
    def __init__(self, mesh_shape, pressure, frac, column, cap):
        self.sizes = dict(mesh_shape)
        self.slots = swap_slots(mesh_shape)
        self.z, self.x, self.y = pressure.shape
        self.seg = frac.shape[1]
        self.pairs = column.shape[1]
        self.peers = self.pairs // cap
        self.cap = cap
        self.rows = self.z * self.x
        self.groups = 128 // cap
        self.pack_rows = 6 * self.z // self.groups
        assert self.y == 128 and self.peers % self.groups == 0


def plane_rows(plan, z):
    return pl.ds(pl.multiple_of(z * plan.x, 8), plan.x)


def gather_cells(plan, fields, column, dst):
    one_y = one_hot(plan.y, lax.rem(column, plan.y)).astype(BF16)
    one_x = one_hot(plan.x, lax.div(column, plan.y))
    step = 8

    def body(c, carry):
        for f, field in enumerate(fields):
            rows = pl.ds(pl.multiple_of(c * step * plan.x, 8), step * plan.x)
            got = split_dot(field[rows, :], one_y, ((1,), (0,)))
            got = got.reshape(step, plan.x, plan.pairs) * one_x[None]
            start = pl.multiple_of((3 + f) * plan.z + c * step, 8)
            dst[pl.ds(start, step), :] = jnp.sum(got, axis=1)
        return carry

    lax.fori_loop(0, plan.z // step, body, 0)


def scatter_cells(plan, rates, column, dsts):
    one_y = one_hot(plan.y, lax.rem(column, plan.y)).astype(BF16)
    one_x = one_hot(plan.x, lax.div(column, plan.y))
    step = 8

    def body(c, carry):
        for f, dst in enumerate(dsts):
            block = rates[pl.ds(pl.multiple_of(f * plan.z + c * step, 8), step), :]
            spread = jnp.concatenate(
                [one_x * block[j : j + 1, :] for j in range(step)], axis=0
            )
            rows = pl.ds(pl.multiple_of(c * step * plan.x, 8), step * plan.x)
            dst[rows, :] = -split_dot(spread, one_y, ((1,), (1,)))
        return carry

    lax.fori_loop(0, plan.z // step, body, 0)


def gather_segments(plan, fields, segment, dst):
    one_s = one_hot(plan.seg, segment).astype(BF16)
    for f, field in enumerate(fields):
        dst[f * plan.z : (f + 1) * plan.z, :] = split_dot(field[...], one_s, ((1,), (0,)))


def scatter_segments(plan, rate, segment):
    one_s = one_hot(plan.seg, segment).astype(BF16)
    return split_dot(rate, one_s, ((1,), (1,)))


def pack_pairs(plan, own, dst):
    n = plan.pack_rows
    lane = lax.broadcasted_iota(jnp.int32, (n, 128), 1) // plan.cap
    for half in range(plan.pairs // 128):
        tiles = [own[g * n : (g + 1) * n, half * 128 : (half + 1) * 128] for g in range(plan.groups)]
        for c in range(plan.groups):
            total = None
            for g in range(plan.groups):
                shift = (g - c) % plan.groups * plan.cap
                moved = pltpu.roll(tiles[g], shift, 1) if shift else tiles[g]
                total = moved if total is None else jnp.where(lane == g, moved, total)
            dst[half * plan.groups + c, 0:n, :] = total


def unpack_pairs(plan, src, dst):
    n = plan.pack_rows
    lane = lax.broadcasted_iota(jnp.int32, (n, 128), 1) // plan.cap
    for half in range(plan.pairs // 128):
        tiles = [src[half * plan.groups + c, 0:n, :] for c in range(plan.groups)]
        for g in range(plan.groups):
            total = None
            for c in range(plan.groups):
                shift = (c - g) % plan.groups * plan.cap
                moved = pltpu.roll(tiles[c], shift, 1) if shift else tiles[c]
                total = moved if total is None else jnp.where(lane == c, moved, total)
            dst[g * n : (g + 1) * n, half * 128 : (half + 1) * 128] = total


def write_faces(plan, fields, outs):
    lane = lax.broadcasted_iota(jnp.int32, (plan.x, 128), 1)
    y_outs = []
    for (axis, odd), out in zip(plan.slots, outs):
        high, _ = slot_side(axis, odd, plan.sizes)
        if axis == "gx":
            row = jnp.where(high, plan.x - 1, 0)
            for f, field in enumerate(fields):
                out[f] = field[pl.ds(row, plan.z, stride=plan.x), :]
        elif axis == "gz":
            start = pl.multiple_of(jnp.where(high, (plan.z - 1) * plan.x, 0), 8)
            for f, field in enumerate(fields):
                out[f] = field[pl.ds(start, plan.x), :]
        else:
            y_outs.append((out, jnp.where(high, 1, 0)))
            out[...] = jnp.zeros(out.shape, F32)
    if not y_outs:
        return

    def body(z, carry):
        for f, field in enumerate(fields):
            value = field[plane_rows(plan, z), :]
            for out, extra in y_outs:
                out[f] = jnp.where(lane == z, pltpu.roll(value, z + extra, 1), out[f])
        return carry

    lax.fori_loop(0, plan.z, body, 0, unroll=4)


def vertical_sign(axis, high):
    if axis != "gz":
        return None
    return jnp.where(high, 1.0, -1.0).astype(F32)


def add_faces(plan, fluxes, dsts, y_store):
    k = 0
    for (axis, odd), pair in zip(plan.slots, fluxes):
        high, _ = slot_side(axis, odd, plan.sizes)
        for dst, flux in zip(dsts, pair):
            if axis == "gx":
                rows = pl.ds(jnp.where(high, plan.x - 1, 0), plan.z, stride=plan.x)
                dst[rows, :] = dst[rows, :] + flux
            elif axis == "gz":
                start = pl.multiple_of(jnp.where(high, (plan.z - 1) * plan.x, 0), 8)
                rows = pl.ds(start, plan.x)
                dst[rows, :] = dst[rows, :] + flux
            else:
                y_store[k] = flux
                k += 1


def y_correction(plan, y_store, z, lane):
    water = hydrogen = None
    k = 0
    for axis, odd in plan.slots:
        if axis != "gy":
            continue
        high, _ = slot_side(axis, odd, plan.sizes)
        target = jnp.where(high, 127, 0)
        shift = lax.rem(target - z + 128, 128)
        parts = [
            jnp.where(lane == target, pltpu.roll(y_store[k + i], shift, 1), 0.0) for i in (0, 1)
        ]
        k += 2
        water = parts[0] if water is None else water + parts[0]
        hydrogen = parts[1] if hydrogen is None else hydrogen + parts[1]
    return water, hydrogen


def divergence(plan, base, steps, conduct, dsts, y_store, fx, fz):
    lane = lax.broadcasted_iota(jnp.int32, (plan.x, 128), 1)
    zero = jnp.zeros((plan.x, 128), F32)
    p_ref, w_ref, h_ref, g_ref = base
    kx, ky, kz = conduct
    for i in (0, 1):
        fz[i] = zero
        fx[i, 0:8, :] = jnp.zeros((8, 128), F32)

    def body(z, carry):
        here = plane_rows(plan, z)
        below = plane_rows(plan, z + 1)
        beside = pl.ds(z * plan.x + 1, plan.x)
        back = lambda v: pltpu.roll(v, 127, 1)
        p0, w0, h0 = p_ref[here, :], w_ref[here, :], h_ref[here, :]
        if steps is not None:
            q0, a0, b0 = steps[0][here, :], steps[1][here, :], steps[2][here, :]

        def flat(conductance, p1, w1, h1, q1=None, a1=None, b1=None):
            drop = p0 - p1
            if steps is None:
                flow = conductance * drop
                return flow * (w0 + w1), flow * (h0 + h1)
            dq = q0 - q1
            return (
                conductance * ((a0 + a1) * drop + (w0 + w1) * dq),
                conductance * ((b0 + b1) * drop + (h0 + h1) * dq),
            )

        fields = (p_ref, w_ref, h_ref) + (() if steps is None else tuple(steps[:3]))
        water, hydrogen = y_correction(plan, y_store, z, lane)
        yw, yh = flat(ky[here, :], *(back(f[here, :]) for f in fields))
        water = water + yw - pltpu.roll(yw, 1, 1)
        hydrogen = hydrogen + yh - pltpu.roll(yh, 1, 1)
        xw, xh = flat(kx[here, :], *(f[beside, :] for f in fields))
        fx[0, 8 : 8 + plan.x, :] = xw
        fx[1, 8 : 8 + plan.x, :] = xh
        water = water + xw - fx[0, 7 : 7 + plan.x, :]
        hydrogen = hydrogen + xh - fx[1, 7 : 7 + plan.x, :]
        p1, w1, h1 = p_ref[below, :], w_ref[below, :], h_ref[below, :]
        g = g_ref[here, :] + g_ref[below, :]
        total = 0.0125 * (p0 + p1)
        drop = p0 - p1 + (0.5 + total)
        extra = total - 0.4
        conductance = kz[here, :]
        if steps is None:
            zw = conductance * ((w0 + w1) * drop)
            zh = conductance * ((h0 + h1) * drop + g * extra)
        else:
            q1, a1, b1 = steps[0][below, :], steps[1][below, :], steps[2][below, :]
            c = steps[3][here, :] + steps[3][below, :]
            dtotal = 0.0125 * (q0 + q1)
            dq = q0 - q1 + dtotal
            zw = conductance * ((a0 + a1) * drop + (w0 + w1) * dq)
            zh = conductance * (
                (b0 + b1) * drop + (h0 + h1) * dq + c * extra + g * dtotal
            )
        dsts[0][here, :] = dsts[0][here, :] + water + zw - fz[0]
        dsts[1][here, :] = dsts[1][here, :] + hydrogen + zh - fz[1]
        fz[0] = zw
        fz[1] = zh
        return carry

    lax.fori_loop(0, plan.z, body, 0)


def clear_tails(plan, refs):
    for ref in refs:
        ref[plan.rows : plan.rows + plan.x + 8, :] = jnp.zeros((plan.x + 8, 128), F32)


def face_flux(sign, conductance, own, other, own_step=None, other_step=None):
    p0, p1 = own[0], other[0]
    if own_step is None:
        (w0, h0, g0), (w1, h1, g1) = mobilities(*own), mobilities(*other)
    else:
        w0, h0, g0, a0, b0, c0 = mobility_steps(*own, *own_step)
        w1, h1, g1, a1, b1, c1 = mobility_steps(*other, *other_step)
        q0, q1 = own_step[0], other_step[0]
    drop = p0 - p1
    if sign is not None:
        total = 0.0125 * (p0 + p1)
        drop = drop + sign * (0.5 + total)
        extra = sign * (total - 0.4)
    if own_step is None:
        water = (w0 + w1) * drop
        hydrogen = (h0 + h1) * drop
        if sign is not None:
            hydrogen = hydrogen + (g0 + g1) * extra
        return conductance * water, conductance * hydrogen
    dq = q0 - q1
    if sign is not None:
        dtotal = sign * (0.0125 * (q0 + q1))
        dq = dq + dtotal
    water = (a0 + a1) * drop + (w0 + w1) * dq
    hydrogen = (b0 + b1) * drop + (h0 + h1) * dq
    if sign is not None:
        hydrogen = hydrogen + (c0 + c1) * extra + (g0 + g1) * dtotal
    return conductance * water, conductance * hydrogen


def first_kernel(plan, *refs):
    n = len(plan.slots)
    p, s, d, k, fp, fs, fd, segment, column, kind, count, table = refs[:12]
    faces, (pack, own, weight) = refs[12 : 12 + n], refs[12 + n :]
    write_faces(plan, (p, s, d, k), faces)
    gather_segments(plan, (fp, fs, fd), segment[...], own)
    gather_cells(plan, (p, s, d), column[...], own)
    pack_pairs(plan, own, pack)
    kinds = kind[...]
    picked = jnp.zeros(kinds.shape, F32)
    for j in range(table.shape[0]):
        picked = jnp.where(kinds == j, table[j], picked)
    slot = lax.broadcasted_iota(jnp.int32, kinds.shape, 1)
    block, rank = slot // plan.cap, lax.rem(slot, plan.cap)
    live = jnp.zeros(kinds.shape, jnp.int32)
    for j in range(plan.peers):
        live = jnp.where(block == j, count[0, j], live)
    picked = jnp.where(rank < live, picked, 0.0)
    weight[...] = picked
    for half in range(plan.pairs // 128):
        tile = jnp.broadcast_to(picked[:, half * 128 : (half + 1) * 128], (8, 128))
        for c in range(plan.groups):
            moved = pltpu.roll(tile, 128 - c * plan.cap, 1) if c else tile
            pack[half * plan.groups + c, plan.pack_rows : plan.pack_rows + 8, :] = moved


def pair_values(plan, ref, side):
    first = 3 * side
    return tuple(ref[(first + f) * plan.z : (first + f + 1) * plan.z, :] for f in range(3))


def residual_kernel(plan, *refs):
    n = len(plan.slots)
    refs = list(refs)
    take = lambda count: [refs.pop(0) for _ in range(count)]
    p, s, d, k, old_water, old_hydrogen, volume = take(7)
    fp, fs, fd, frac_water, frac_hydrogen, frac_volume = take(6)
    segment, column, weight, own, recv = take(5)
    own_faces, recv_faces = take(n), take(n)
    res, frac_res, kx, ky, kz, kb = take(6)
    faces = take(n)
    pack, own_res, got, weight_back = take(4)
    sp, sw, sh, sg, sk, fx, fz, y_store, rates = take(9)
    res_w, res_h, res_c = (res.at[i] for i in range(3))

    unpack_pairs(plan, recv, got)
    lane8 = lax.broadcasted_iota(jnp.int32, (8, 128), 1) // plan.cap
    for half in range(plan.pairs // 128):
        total = None
        for c in range(plan.groups):
            tile = recv[half * plan.groups + c, plan.pack_rows : plan.pack_rows + 8, :]
            moved = pltpu.roll(tile, c * plan.cap, 1) if c else tile
            total = moved if total is None else jnp.where(lane8 == c, moved, total)
        weight_back[:, half * 128 : (half + 1) * 128] = total[0:1, :]

    def pair_rates(weights, seg_values, cell_values):
        w0, h0, _ = mobilities(*seg_values)
        w1, h1, _ = mobilities(*cell_values)
        flow = (0.5 * weights) * (seg_values[0] - cell_values[0])
        return flow * (w0 + w1), flow * (h0 + h1)

    rate_w, rate_h = pair_rates(weight[...], pair_values(plan, got, 0), pair_values(plan, own, 1))
    rates[0 : plan.z, :] = rate_w
    rates[plan.z : 2 * plan.z, :] = rate_h
    scatter_cells(plan, rates, column[...], (res_w, res_h))
    rate_w, rate_h = pair_rates(
        weight_back[...], pair_values(plan, own, 0), pair_values(plan, got, 1)
    )
    fpv, fsv, fdv = fp[...], fs[...], fd[...]
    mass_w, mass_h = masses(fpv, fsv, fdv)
    vol = frac_volume[...]
    frac_res[0] = vol * (mass_w - frac_water[...]) + scatter_segments(plan, rate_w, segment[...])
    frac_res[1] = vol * (mass_h - frac_hydrogen[...]) + scatter_segments(
        plan, rate_h, segment[...]
    )
    frac_res[2] = closure(fpv, fsv, fdv)

    clear_tails(plan, (sp, sw, sh, sg))
    sk[plan.rows : plan.rows + plan.x + 8, :] = jnp.ones((plan.x + 8, 128), F32)
    lane = lax.broadcasted_iota(jnp.int32, (plan.x, 128), 1)
    row = lax.broadcasted_iota(jnp.int32, (plan.x, 128), 0)

    def cells(z, carry):
        here = plane_rows(plan, z)
        pv, sv, dv = p[here, :], s[here, :], d[here, :]
        sp[here, :] = pv
        sw[here, :], sh[here, :], sg[here, :] = mobilities(pv, sv, dv)
        sk[here, :] = k[here, :]
        mw, mh = masses(pv, sv, dv)
        vol = volume[here, :]
        res_w[here, :] = res_w[here, :] + vol * (mw - old_water[here, :])
        res_h[here, :] = res_h[here, :] + vol * (mh - old_hydrogen[here, :])
        res_c[here, :] = closure(pv, sv, dv)
        return carry

    lax.fori_loop(0, plan.z, cells, 0)

    def conductances(z, carry):
        here = plane_rows(plan, z)
        k0 = sk[here, :]
        kx1 = sk[pl.ds(z * plan.x + 1, plan.x), :]
        ky1 = pltpu.roll(k0, 127, 1)
        kz1 = sk[plane_rows(plan, z + 1), :]
        kx[here, :] = jnp.where(row == plan.x - 1, 0.0, k0 * kx1 / (k0 + kx1))
        ky[here, :] = jnp.where(lane == 127, 0.0, k0 * ky1 / (k0 + ky1))
        inner = jnp.where(z == plan.z - 1, 0.0, 0.2).astype(F32)
        kz[here, :] = inner * (k0 * kz1 / (k0 + kz1))
        return carry

    lax.fori_loop(0, plan.z, conductances, 0)

    fluxes = []
    for i, (axis, odd) in enumerate(plan.slots):
        high, valid = slot_side(axis, odd, plan.sizes)
        mine, theirs = own_faces[i], recv_faces[i]
        k0, k1 = mine[3], theirs[3]
        if axis == "gy":
            k0, k1 = jnp.where(lane < plan.z, k0, 1.0), jnp.where(lane < plan.z, k1, 1.0)
        scale = jnp.where(valid, 0.2 if axis == "gz" else 1.0, 0.0).astype(F32)
        conductance = scale * (k0 * k1 / (k0 + k1))
        kb[i] = conductance
        fluxes.append(
            face_flux(
                vertical_sign(axis, high),
                conductance,
                tuple(mine[f] for f in range(3)),
                tuple(theirs[f] for f in range(3)),
            )
        )
    add_faces(plan, fluxes, (res_w, res_h), y_store)
    divergence(plan, (sp, sw, sh, sg), None, (kx, ky, kz), (res_w, res_h), y_store, fx, fz)
    fields = (res_w, res_h, res_c)
    write_faces(plan, fields, faces)
    gather_segments(plan, tuple(frac_res.at[i] for i in range(3)), segment[...], own_res)
    gather_cells(plan, fields, column[...], own_res)
    pack_pairs(plan, own_res, pack)


def total_of(value):
    return jnp.sum(jnp.sum(value, axis=0, keepdims=True), axis=1, keepdims=True)


def block_sums(plan, cell_refs, frac_refs, function, count):
    def body(z, carry):
        here = plane_rows(plan, z)
        for f in range(3):
            parts = function(*(ref[f, here, :] for ref in cell_refs))
            carry = tuple(c + part for c, part in zip(carry, parts))
        return carry

    zero = jnp.zeros((plan.x, 128), F32)
    sums = lax.fori_loop(0, plan.z, body, (zero,) * count, unroll=2)
    sums = [total_of(v) for v in sums]
    for f in range(3):
        parts = function(*(ref[f] for ref in frac_refs))
        sums = [v + total_of(part) for v, part in zip(sums, parts)]
    return sums


def safe_ratio(top, bottom):
    good = bottom > 0.0
    return jnp.where(good, top / jnp.where(good, bottom, 1.0), 0.0)


def jacobian_kernel(plan, last, *refs):
    n = len(plan.slots)
    refs = list(refs)
    take = lambda count: [refs.pop(0) for _ in range(count)]
    p, s, d, volume, kx, ky, kz, kb, vec = take(9)
    fp, fs, fd, frac_volume, frac_vec = take(5)
    segment, column, weight, weight_back, own, got, own_vec, recv = take(8)
    own_faces, recv_faces = take(n), take(n)
    own_vec_faces, recv_vec_faces = take(n), take(n)
    if last:
        base_vec, base_frac, stats_in = take(3)
        out, frac_out, stats = take(3)
    else:
        out, frac_out = take(2)
        faces = take(n)
        pack, own_out, stats = take(3)
    sp, sw, sh, sg, sq, sa, sb, sc, fx, fz, y_store, rates, got_vec = take(13)
    out_w, out_h, out_c = (out.at[i] for i in range(3))

    unpack_pairs(plan, recv, got_vec)

    def pair_rates(weights, seg_values, seg_steps, cell_values, cell_steps):
        w0, h0, _, a0, b0, _ = mobility_steps(*seg_values, *seg_steps)
        w1, h1, _, a1, b1, _ = mobility_steps(*cell_values, *cell_steps)
        drop = seg_values[0] - cell_values[0]
        dq = seg_steps[0] - cell_steps[0]
        half = 0.5 * weights
        return (
            half * ((a0 + a1) * drop + (w0 + w1) * dq),
            half * ((b0 + b1) * drop + (h0 + h1) * dq),
        )

    rate_w, rate_h = pair_rates(
        weight[...],
        pair_values(plan, got, 0),
        pair_values(plan, got_vec, 0),
        pair_values(plan, own, 1),
        pair_values(plan, own_vec, 1),
    )
    rates[0 : plan.z, :] = rate_w
    rates[plan.z : 2 * plan.z, :] = rate_h
    scatter_cells(plan, rates, column[...], (out_w, out_h))
    rate_w, rate_h = pair_rates(
        weight_back[...],
        pair_values(plan, own, 0),
        pair_values(plan, own_vec, 0),
        pair_values(plan, got, 1),
        pair_values(plan, got_vec, 1),
    )
    values = (fp[...], fs[...], fd[...], frac_vec[0], frac_vec[1], frac_vec[2])
    mass_w, mass_h = mass_steps(*values)
    vol = frac_volume[...]
    frac_out[0] = vol * mass_w + scatter_segments(plan, rate_w, segment[...])
    frac_out[1] = vol * mass_h + scatter_segments(plan, rate_h, segment[...])
    frac_out[2] = closure_step(*values)

    clear_tails(plan, (sp, sw, sh, sg, sq, sa, sb, sc))

    def cells(z, carry):
        here = plane_rows(plan, z)
        values = (p[here, :], s[here, :], d[here, :]) + tuple(vec[f, here, :] for f in range(3))
        sp[here, :] = values[0]
        sq[here, :] = values[3]
        moves = mobility_steps(*values)
        for ref, value in zip((sw, sh, sg, sa, sb, sc), moves):
            ref[here, :] = value
        mw, mh = mass_steps(*values)
        vol = volume[here, :]
        out_w[here, :] = out_w[here, :] + vol * mw
        out_h[here, :] = out_h[here, :] + vol * mh
        out_c[here, :] = closure_step(*values)
        return carry

    lax.fori_loop(0, plan.z, cells, 0)
    fluxes = []
    for i, (axis, odd) in enumerate(plan.slots):
        high, _ = slot_side(axis, odd, plan.sizes)
        three = lambda ref: tuple(ref[f] for f in range(3))
        fluxes.append(
            face_flux(
                vertical_sign(axis, high),
                kb[i],
                three(own_faces[i]),
                three(recv_faces[i]),
                three(own_vec_faces[i]),
                three(recv_vec_faces[i]),
            )
        )
    add_faces(plan, fluxes, (out_w, out_h), y_store)
    divergence(
        plan, (sp, sw, sh, sg), (sq, sa, sb, sc), (kx, ky, kz), (out_w, out_h), y_store, fx, fz
    )
    fields = (out_w, out_h, out_c)
    if not last:
        write_faces(plan, fields, faces)
        gather_segments(plan, tuple(frac_out.at[i] for i in range(3)), segment[...], own_out)
        gather_cells(plan, fields, column[...], own_out)
        pack_pairs(plan, own_out, pack)
        rr, rw = block_sums(
            plan, (vec, out), (frac_vec, frac_out), lambda r, w: (r * r, r * w), 2
        )
        share = safe_ratio(rw, rr)
        (uu,) = block_sums(
            plan,
            (vec, out),
            (frac_vec, frac_out),
            lambda r, w: (jnp.square(w - share * r),),
            1,
        )
        r11 = jnp.sqrt(rr)
        found = (r11, safe_ratio(rw, r11), jnp.sqrt(uu), share, uu)
        lane = lax.broadcasted_iota(jnp.int32, (8, 128), 1)
        total = jnp.zeros((8, 128), F32)
        for j, value in enumerate(found):
            total = jnp.where(lane == j, value, total)
        stats[...] = total
        return
    known = stats_in[0:1, :]
    lane1 = lax.broadcasted_iota(jnp.int32, (1, 128), 1)
    r11, r12, r22, share, uu = (
        jnp.sum(jnp.where(lane1 == j, known, 0.0), axis=1, keepdims=True) for j in range(5)
    )
    refs3 = (base_vec, vec, out)
    fracs3 = (base_frac, frac_vec, frac_out)
    rz, uz = block_sums(
        plan, refs3, fracs3, lambda r, w, v: (r * v, (w - share * r) * v), 2
    )
    along_r, along_u = safe_ratio(rz, r11 * r11), safe_ratio(uz, uu)
    (vv,) = block_sums(
        plan,
        refs3,
        fracs3,
        lambda r, w, v: (jnp.square(v - along_r * r - along_u * (w - share * r)),),
        1,
    )
    found = (r11, r12, r22, safe_ratio(rz, r11), safe_ratio(uz, r22), jnp.sqrt(vv))
    lane = lax.broadcasted_iota(jnp.int32, stats.shape, 1)
    total = jnp.zeros(stats.shape, F32)
    for j, value in enumerate(found):
        total = jnp.where(lane == j, value, total)
    stats[...] = total


def step_kernel(plan, stats, res, frac_res, vec, frac_vec, step, frac_step):
    table = stats[...]
    lane = lax.broadcasted_iota(jnp.int32, table.shape, 1)
    r11, r12, r22, r13, r23, r33 = (
        jnp.sum(jnp.where(lane == j, table, 0.0), axis=1, keepdims=True) for j in range(6)
    )
    add = lambda v: jnp.sum(v, axis=0, keepdims=True)
    norm2 = add(r11 * r11) + EPS
    norm = jnp.sqrt(norm2)
    c11 = add(r11 * r12) / norm2
    left1, left2 = r12 - c11 * r11, r22
    c21 = jnp.sqrt(add(left1 * left1 + left2 * left2) / norm2 + EPS)
    scale = 1.0 / (norm * c21)
    second1, second2 = -scale * left1, -scale * left2
    image1 = -scale * (r13 - c11 * r12)
    image2 = -scale * (r23 - c11 * r22)
    image3 = -scale * r33
    first1 = -r11 / norm
    c12 = add(image1 * first1)
    c22 = add(image1 * second1 + image2 * second2)
    u1 = image1 - c12 * first1 - c22 * second1
    u2 = image2 - c22 * second2
    c32_2 = add(u1 * u1 + u2 * u2 + image3 * image3) + EPS
    rho = jnp.sqrt(c11 * c11 + c21 * c21)
    co, si = c11 / rho, c21 / rho
    t1 = co * c12 + si * c22
    t2 = co * c22 - si * c12
    y2 = -si * norm * t2 / (t2 * t2 + c32_2)
    y1 = (co * norm - t1 * y2) / rho
    on_vec = -y2 * scale
    on_res = -y1 / norm - c11 * on_vec

    def body(z, carry):
        here = plane_rows(plan, z)
        for f in range(3):
            step[f, here, :] = on_res * res[f, here, :] + on_vec * vec[f, here, :]
        return carry

    lax.fori_loop(0, plan.z, body, 0, unroll=2)
    for f in range(3):
        frac_step[f] = on_res * frac_res[f] + on_vec * frac_vec[f]


def call(kernel, out_shapes, args, scratch=(), smem=(), flops=0):
    specs = [
        pl.BlockSpec(memory_space=pltpu.SMEM if i in smem else pltpu.VMEM)
        for i in range(len(args))
    ]
    return pl.pallas_call(
        kernel,
        out_shape=[jax.ShapeDtypeStruct(shape, F32) for shape in out_shapes],
        in_specs=specs,
        out_specs=[pl.BlockSpec(memory_space=pltpu.VMEM)] * len(out_shapes),
        scratch_shapes=[pltpu.VMEM(shape, F32) for shape in scratch],
        compiler_params=pltpu.CompilerParams(vmem_limit_bytes=56 << 20),
    )(*args)


def on_device(mesh_shape, *args):
    (
        pressure,
        saturation,
        dissolved,
        old_water,
        old_hydrogen,
        pore_volume,
        permeability,
        frac_pressure,
        frac_saturation,
        frac_dissolved,
        frac_old_water,
        frac_old_hydrogen,
        frac_volume,
        pair_segment,
        pair_column,
        pair_kind,
        pair_count,
        transfer_table,
    ) = args
    cap = pair_column.shape[1] // pair_count.shape[1]
    plan = Plan(mesh_shape, pressure, frac_pressure, pair_column, cap)
    slots = len(plan.slots)
    devices = plan.sizes["gx"] * plan.sizes["gy"] * plan.sizes["gz"]
    flat = lambda a: a.reshape(plan.rows, plan.y)
    p, s, d, k = (flat(a) for a in (pressure, saturation, dissolved, permeability))
    volume = flat(pore_volume)
    field = (plan.rows, plan.y)
    padded = (plan.rows + plan.x + 8, plan.y)
    pair_shape = (6 * plan.z, plan.pairs)
    y_slots = sum(axis == "gy" for axis, _ in plan.slots)
    flux_scratch = [(2, plan.x + 8, plan.y), (2, plan.x, plan.y), (2 * y_slots, plan.x, plan.y)]
    rate_scratch = (2 * plan.z, plan.pairs)

    def exchange(faces, pack):
        got = lax.all_to_all(pack, PLANE, 0, 0, tiled=True)
        moved = [
            lax.ppermute(face, axis, swap_pairs(plan.sizes[axis], odd))
            for (axis, odd), face in zip(plan.slots, faces)
        ]
        return moved, got

    outs = call(
        functools.partial(first_kernel, plan),
        [(4, 32, 128)] * slots
        + [(plan.peers, plan.pack_rows + 8, 128), pair_shape, (1, plan.pairs)],
        [p, s, d, k, frac_pressure, frac_saturation, frac_dissolved]
        + [pair_segment, pair_column, pair_kind, pair_count, transfer_table],
        smem=(10, 11),
    )
    faces, (pack, own, weight) = outs[:slots], outs[slots:]
    recv_faces, recv = exchange(faces, pack)
    outs = call(
        functools.partial(residual_kernel, plan),
        [(3,) + field, (3, plan.z, plan.seg), field, field, field, (slots, 32, 128)]
        + [(3, 32, 128)] * slots
        + [(plan.peers, plan.pack_rows, 128), pair_shape, pair_shape, (1, plan.pairs)],
        [p, s, d, k, flat(old_water), flat(old_hydrogen), volume]
        + [frac_pressure, frac_saturation, frac_dissolved]
        + [frac_old_water, frac_old_hydrogen, frac_volume]
        + [pair_segment, pair_column, weight, own, recv]
        + list(faces)
        + list(recv_faces),
        scratch=[padded] * 5 + flux_scratch + [rate_scratch],
    )
    res, frac_res, kx, ky, kz, kb = outs[:6]
    vec_faces = outs[6 : 6 + slots]
    pack, own_vec, got, weight_back = outs[6 + slots :]

    def image(vec, frac_vec, vec_faces, pack, own_vec, extra):
        recv_vec_faces, recv_vec = exchange(vec_faces, pack)
        last = extra is not None
        shapes = [(3,) + field, (3, plan.z, plan.seg)]
        if last:
            shapes += [(devices, 128)]
        else:
            shapes += [(3, 32, 128)] * slots
            shapes += [(plan.peers, plan.pack_rows, 128), pair_shape, (8, 128)]
        return call(
            functools.partial(jacobian_kernel, plan, last),
            shapes,
            [p, s, d, volume, kx, ky, kz, kb, vec]
            + [frac_pressure, frac_saturation, frac_dissolved, frac_volume, frac_vec]
            + [pair_segment, pair_column, weight, weight_back, own, got, own_vec, recv_vec]
            + list(faces)
            + list(recv_faces)
            + list(vec_faces)
            + list(recv_vec_faces)
            + (list(extra) if last else []),
            scratch=[padded] * 8 + flux_scratch + [rate_scratch, pair_shape],
        )

    outs = image(res, frac_res, vec_faces, pack, own_vec, None)
    vec, frac_vec = outs[:2]
    vec_faces = outs[2 : 2 + slots]
    pack, own_vec, stats = outs[2 + slots :]
    _, _, stats = image(vec, frac_vec, vec_faces, pack, own_vec, (res, frac_res, stats))
    stats = lax.all_to_all(stats, ("gx", "gy", "gz"), 0, 0, tiled=True)
    step, frac_step = call(
        functools.partial(step_kernel, plan),
        [(3,) + field, (3, plan.z, plan.seg)],
        [stats, res, frac_res, vec, frac_vec],
    )
    whole = (3, plan.z, plan.x, plan.y)
    return step.reshape(whole), frac_step, res.reshape(whole), frac_res


def solution(mesh):
    grid = P("gz", "gx", "gy")
    segments = P("gz", PLANE)
    lists = P(PLANE, None)
    return jax.shard_map(
        functools.partial(on_device, dict(mesh.shape)),
        mesh=mesh,
        in_specs=(grid,) * 7 + (segments,) * 6 + (lists,) * 4 + (P(),),
        out_specs=(
            P(None, "gz", "gx", "gy"),
            P(None, "gz", PLANE),
            P(None, "gz", "gx", "gy"),
            P(None, "gz", PLANE),
        ),
        check_vma=False,
    )
```

time: 783 us -> 126 us (0.16); the launches traced: 770 us -> 126 us
  other arithmetic: 230 us -> 0 us
  local copies, waits for them, and re-layouts: 222 us -> 2.04 us
  blocking collectives: 196 us -> 10.9 us
  Pallas kernels: 0 us -> 61.3 us
  starting transfers between devices: 92.1 us -> 38.6 us
  between operations: 16.6 us -> 0.79 us
    psum x5 -> x0, blocking collectives: 196 us -> none  [the longest x1 40.1 us: on_device(): lax.psum(inner_product(left_over, left_over), ('gx', 'gy', 'gz'))]
    pallas_call x0 -> x5, Pallas kernels: none -> 61.3 us  [call(): pl.pallas_call(kernel, out_shape=[jax.ShapeDtypeStruct(shape, F32) for sh...]
    another operation x22 -> x0, local copies, waits for them, and re-layouts: 59.2 us -> none  [the longest x6 23.1 us: jacobian(): jnp.stack([step_cells[0], cell_steps[0], cell_steps[1] + cell_steps[2]])]
    scatter-add x12 -> x0, other arithmetic: 48.2 us -> none  [the longest x6 28.7 us: add_columns(): return flat_field.at[:, column_index].add(values).reshape(shape_kept)]
    slice x23 -> x0, local copies, waits for them, and re-layouts: 44.2 us -> none  [the longest x9 22.4 us: with_halo(): last = lax.slice_in_dim(shard, length - width, length, axis=dim)]
    concatenate x8 -> x0, other arithmetic: 41.9 us -> none  [with_halo(): shard = jnp.concatenate([before, shard, after], axis=dim)]
    ppermute x18 -> x15, starting transfers between devices: 56.7 us -> 21.7 us  [exchange(): lax.ppermute(face, axis, swap_pairs(plan.sizes[axis], odd))]
    mul x24 -> x0, other arithmetic: 34.3 us -> none  [the longest x6 14.8 us: flux_divergence(): transmit * (0.5 * (sw_lower + sw_upper) * liquid_drop + water_mean * step...]
  transfers between devices with their start and end apart: 24 -> 18, of which waited for: 3 -> 9; matrix products, arithmetic and copies ran while one was open for 29% -> 0% of each run, Pallas kernels for 0% -> 0%
where the time goes in v1:
time: 126 us
  Pallas kernels  61.3 us (49%)
  starting transfers between devices  38.6 us (31%)
  waiting for transfers between devices  12.2 us (10%)
  blocking collectives  10.9 us (9%)
  local copies, waits for them, and re-layouts  2.04 us (2%)
    pallas_call x5, Pallas kernels, call(): pl.pallas_call(kernel, out_shape=[jax.ShapeDtypeStruct(shape, F32) for sh...  61.3 us
    ppermute x15, starting transfers between devices, exchange(): lax.ppermute(face, axis, swap_pairs(plan.sizes[axis], odd))  21.7 us
    all_to_all x3, starting transfers between devices, exchange(): got = lax.all_to_all(pack, PLANE, 0, 0, tiled=True)  16.9 us
    ppermute x15, waiting for transfers between devices, exchange(): lax.ppermute(face, axis, swap_pairs(plan.sizes[axis], odd))  11.5 us
    all_to_all x1, blocking collectives, on_device(): stats = lax.all_to_all(stats, ('gx', 'gy', 'gz'), 0, 0, tiled=True)  10.9 us
  transfers between devices with their start and end apart: 18, of which 9 were waited for; matrix products, arithmetic and copies ran while one was open for 0% of the time, Pallas kernels for 0%

profile of v1, /device:TPU:0, one launch (start us, length us, event | category | flops | bytes accessed | tf_op | source)
XLA Modules:
  0.0 125.8 jit_solution(17231230409939534269)
XLA Ops:
  0.6 6.3 %shard_map.201 = (f32[4,32,128]{2,1,0:T(8,128)}, f32[4,32,128]{2,1,0:T(8,128)}, f32[4,32,128]{2,1,0:T(8,128)}, f32[4,32,128]{2,1,0:T(8,128)}, f32[4,32,128]{2,1,...) custom-call(f32[1024,128]{1,0:T(8,128)} %bitcast.14, f32[1024,128]{1,0:T(8,128)} %bitcast.18, ...), custom_call_target="tpu_custom_call" | custom-call | tf_op jit(solution)/shard_map/pallas_call | solution.py:737
  7.0 8.3 %all-to-all-start = ((f32[16,32,128]{2,1,0:T(8,128)}), f32[16,32,128]{2,1,0:T(8,128)S(1)}, u32[]{:S(2)}, u32[]{:S(2)}) async-start(f32[16,32,128]{2,1,0:T(8,128)} %get-tuple-element.42), calls=%async_computation | async-start | bytes 524288 | tf_op jit(solution)/shard_map/all_to_all | solution.py:783
  15.3 1.9 %collective-permute-start = (f32[4,32,128]{2,1,0:T(8,128)}, f32[4,32,128]{2,1,0:T(8,128)S(1)}, u32[]{:S(2)}, u32[]{:S(2)}) collective-permute-start(f32[4,32,128]{2,1,0:T(8,128)} %get-tuple-element.43.refs_18_.refs_22_), channel_id=1, source_target_pairs={{0,8},{8,0},{16,24},{24,16},{1,9},{9,1},{17,25},{25,17},{2,10},{10... | collective-permute-start | bytes 196616 | tf_op jit(solution)/shard_map/ppermute | solution.py:785
  17.2 1.5 %collective-permute-start.1 = (f32[4,32,128]{2,1,0:T(8,128)}, f32[4,32,128]{2,1,0:T(8,128)S(1)}, u32[]{:S(2)}, u32[]{:S(2)}) collective-permute-start(f32[4,32,128]{2,1,0:T(8,128)} %get-tuple-element.44.refs_19_.refs_23_), channel_id=1, source_target_pairs={{0,24},{8,16},{16,8},{24,0},{1,25},{9,17},{17,9},{25,1},{2,26},{10... | collective-permute-start | bytes 196616 | tf_op jit(solution)/shard_map/ppermute | solution.py:785
  18.7 1.5 %collective-permute-start.2 = (f32[4,32,128]{2,1,0:T(8,128)}, f32[4,32,128]{2,1,0:T(8,128)S(1)}, u32[]{:S(2)}, u32[]{:S(2)}) collective-permute-start(f32[4,32,128]{2,1,0:T(8,128)} %get-tuple-element.45.refs_20_.refs_24_), channel_id=1, source_target_pairs={{0,2},{2,0},{4,6},{6,4},{1,3},{3,1},{5,7},{7,5},{8,10},{10,8},{12,... | collective-permute-start | bytes 196616 | tf_op jit(solution)/shard_map/ppermute | solution.py:785
  20.2 2.4 %collective-permute-start.3 = (f32[4,32,128]{2,1,0:T(8,128)}, f32[4,32,128]{2,1,0:T(8,128)S(1)}, u32[]{:S(2)}, u32[]{:S(2)}) collective-permute-start(f32[4,32,128]{2,1,0:T(8,128)} %get-tuple-element.46.refs_21_.refs_25_), channel_id=1, source_target_pairs={{0,6},{2,4},{4,2},{6,0},{1,7},{3,5},{5,3},{7,1},{8,14},{10,12},{12... | collective-permute-start | bytes 196616 | tf_op jit(solution)/shard_map/ppermute | solution.py:785
  22.5 0.0 collective-permute-start.4
  22.5 0.0 collective-permute-done.refs_23_.refs_27_
  22.5 0.7 collective-permute-done.1.refs_24_.refs_28_
  23.3 0.3 collective-permute-done.2.refs_25_.refs_29_
  23.6 2.9 %collective-permute-done.3.refs_26_.refs_30_ = f32[4,32,128]{2,1,0:T(8,128)S(1)} collective-permute-done((f32[4,32,128]{2,1,0:T(8,128)}, f32[4,32,128]{2,1,0:T(8,128)S(1)}, u32[]{:S(2)}, u32[]{:S(2)}) %collective-permute-start.3) | collective-permute-done | bytes 65568 | tf_op jit(solution)/shard_map/ppermute | solution.py:785
  26.6 0.0 collective-permute-done.4.refs_27_.refs_31_
  26.6 0.7 all-to-all-done.refs_17_
  27.3 0.7 copy-done
  28.0 18.2 %shard_map.202 = (f32[3,1024,128]{2,1,0:T(8,128)}, f32[3,32,256]{2,1,0:T(8,128)}, f32[1024,128]{1,0:T(8,128)}, f32[1024,128]{1,0:T(8,128)}, f32[1024,128]{1,0:T(...) custom-call(f32[1024,128]{1,0:T(8,128)} %bitcast.15, ...), custom_call_target="tpu_custom_call" | custom-call | tf_op jit(solution)/shard_map/pallas_call | solution.py:737
  46.2 3.9 %all-to-all-start.1 = ((f32[16,24,128]{2,1,0:T(8,128)}), f32[16,24,128]{2,1,0:T(8,128)S(1)}, u32[]{:S(2)}, u32[]{:S(2)}) async-start(f32[16,24,128]{2,1,0:T(8,128)} %get-tuple-element.57), calls=%async_computation.1 | async-start | bytes 393216 | tf_op jit(solution)/shard_map/all_to_all | solution.py:783
  50.2 1.9 %collective-permute-start.5 = (f32[3,32,128]{2,1,0:T(8,128)}, f32[3,32,128]{2,1,0:T(8,128)S(1)}, u32[]{:S(2)}, u32[]{:S(2)}) collective-permute-start(f32[3,32,128]{2,1,0:T(8,128)} %get-tuple-element.58.refs_32_), channel_id=1, source_target_pairs={{0,8},{8,0},{16,24},{24,16},{1,9},{9,1},{17,25},{25,17},{2,10},{10... | collective-permute-start | bytes 147464 | tf_op jit(solution)/shard_map/ppermute | solution.py:785
  52.1 1.5 %collective-permute-start.6 = (f32[3,32,128]{2,1,0:T(8,128)}, f32[3,32,128]{2,1,0:T(8,128)S(1)}, u32[]{:S(2)}, u32[]{:S(2)}) collective-permute-start(f32[3,32,128]{2,1,0:T(8,128)} %get-tuple-element.59.refs_33_), channel_id=1, source_target_pairs={{0,24},{8,16},{16,8},{24,0},{1,25},{9,17},{17,9},{25,1},{2,26},{10... | collective-permute-start | bytes 147464 | tf_op jit(solution)/shard_map/ppermute | solution.py:785
  53.6 1.5 %collective-permute-start.7 = (f32[3,32,128]{2,1,0:T(8,128)}, f32[3,32,128]{2,1,0:T(8,128)S(1)}, u32[]{:S(2)}, u32[]{:S(2)}) collective-permute-start(f32[3,32,128]{2,1,0:T(8,128)} %get-tuple-element.60.refs_34_), channel_id=1, source_target_pairs={{0,2},{2,0},{4,6},{6,4},{1,3},{3,1},{5,7},{7,5},{8,10},{10,8},{12,... | collective-permute-start | bytes 147464 | tf_op jit(solution)/shard_map/ppermute | solution.py:785
  55.0 2.4 %collective-permute-start.8 = (f32[3,32,128]{2,1,0:T(8,128)}, f32[3,32,128]{2,1,0:T(8,128)S(1)}, u32[]{:S(2)}, u32[]{:S(2)}) collective-permute-start(f32[3,32,128]{2,1,0:T(8,128)} %get-tuple-element.61.refs_35_), channel_id=1, source_target_pairs={{0,6},{2,4},{4,2},{6,0},{1,7},{3,5},{5,3},{7,1},{8,14},{10,12},{12... | collective-permute-start | bytes 147464 | tf_op jit(solution)/shard_map/ppermute | solution.py:785
  57.4 0.0 collective-permute-start.9
  57.4 0.0 collective-permute-done.5.refs_37_
  57.4 0.0 collective-permute-done.6.refs_38_
  57.4 0.7 collective-permute-done.7.refs_39_
  58.2 3.0 %collective-permute-done.8.refs_40_ = f32[3,32,128]{2,1,0:T(8,128)S(1)} collective-permute-done((f32[3,32,128]{2,1,0:T(8,128)}, f32[3,32,128]{2,1,0:T(8,128)S(1)}, u32[]{:S(2)}, u32[]{:S(2)}) %collective-permute-start.8) | collective-permute-done | bytes 49184 | tf_op jit(solution)/shard_map/ppermute | solution.py:785
  61.1 0.0 collective-permute-done.9.refs_41_
  61.1 0.0 all-to-all-done.1.refs_21_
  61.1 0.0 copy-start.1
  61.2 0.6 copy-done.16
  61.7 0.0 copy-done.17
  61.8 0.1 copy-done.1
  61.8 17.9 %shard_map.203 = (f32[3,1024,128]{2,1,0:T(8,128)}, f32[3,32,256]{2,1,0:T(8,128)}, f32[3,32,128]{2,1,0:T(8,128)}, f32[3,32,128]{2,1,0:T(8,128)}, f32[3,32,128]{2,...) custom-call(f32[1024,128]{1,0:T(8,128)} %bitcast.16, ...), custom_call_target="tpu_custom_call" | custom-call | tf_op jit(solution)/shard_map/pallas_call | solution.py:737
  79.8 4.7 %all-to-all-start.2 = ((f32[16,24,128]{2,1,0:T(8,128)}), f32[16,24,128]{2,1,0:T(8,128)S(1)}, u32[]{:S(2)}, u32[]{:S(2)}) async-start(f32[16,24,128]{2,1,0:T(8,128)} %get-tuple-element.66), calls=%async_computation.2 | async-start | bytes 393216 | tf_op jit(solution)/shard_map/all_to_all | solution.py:783
  84.4 1.9 %collective-permute-start.10 = (f32[3,32,128]{2,1,0:T(8,128)}, f32[3,32,128]{2,1,0:T(8,128)S(1)}, u32[]{:S(2)}, u32[]{:S(2)}) collective-permute-start(f32[3,32,128]{2,1,0:T(8,128)} %get-tuple-element.67.refs_32_), channel_id=1, source_target_pairs={{0,8},{8,0},{16,24},{24,16},{1,9},{9,1},{17,25},{25,17},{2,10},{10... | collective-permute-start | bytes 147464 | tf_op jit(solution)/shard_map/ppermute | solution.py:785
  86.4 1.5 %collective-permute-start.11 = (f32[3,32,128]{2,1,0:T(8,128)}, f32[3,32,128]{2,1,0:T(8,128)S(1)}, u32[]{:S(2)}, u32[]{:S(2)}) collective-permute-start(f32[3,32,128]{2,1,0:T(8,128)} %get-tuple-element.68.refs_33_), channel_id=1, source_target_pairs={{0,24},{8,16},{16,8},{24,0},{1,25},{9,17},{17,9},{25,1},{2,26},{10... | collective-permute-start | bytes 147464 | tf_op jit(solution)/shard_map/ppermute | solution.py:785
  87.8 1.5 %collective-permute-start.12 = (f32[3,32,128]{2,1,0:T(8,128)}, f32[3,32,128]{2,1,0:T(8,128)S(1)}, u32[]{:S(2)}, u32[]{:S(2)}) collective-permute-start(f32[3,32,128]{2,1,0:T(8,128)} %get-tuple-element.69.refs_34_), channel_id=1, source_target_pairs={{0,2},{2,0},{4,6},{6,4},{1,3},{3,1},{5,7},{7,5},{8,10},{10,8},{12,... | collective-permute-start | bytes 147464 | tf_op jit(solution)/shard_map/ppermute | solution.py:785
  89.3 2.4 %collective-permute-start.13 = (f32[3,32,128]{2,1,0:T(8,128)}, f32[3,32,128]{2,1,0:T(8,128)S(1)}, u32[]{:S(2)}, u32[]{:S(2)}) collective-permute-start(f32[3,32,128]{2,1,0:T(8,128)} %get-tuple-element.70.refs_35_), channel_id=1, source_target_pairs={{0,6},{2,4},{4,2},{6,0},{1,7},{3,5},{5,3},{7,1},{8,14},{10,12},{12... | collective-permute-start | bytes 147464 | tf_op jit(solution)/shard_map/ppermute | solution.py:785
  91.7 0.0 collective-permute-start.14
  91.7 0.0 collective-permute-done.10.refs_37_
  91.7 0.2 collective-permute-done.11.refs_38_
  91.8 0.3 collective-permute-done.12.refs_39_
  92.2 3.2 %collective-permute-done.13.refs_40_ = f32[3,32,128]{2,1,0:T(8,128)S(1)} collective-permute-done((f32[3,32,128]{2,1,0:T(8,128)}, f32[3,32,128]{2,1,0:T(8,128)S(1)}, u32[]{:S(2)}, u32[]{:S(2)}) %collective-permute-start.13) | collective-permute-done | bytes 49184 | tf_op jit(solution)/shard_map/ppermute | solution.py:785
  95.5 0.6 copy-done.11
  96.0 0.0 copy-done.13
  96.0 0.1 copy-done.2
  96.1 15.3 %shard_map.204 = (f32[3,1024,128]{2,1,0:T(8,128)}, f32[3,32,256]{2,1,0:T(8,128)}, f32[32,128]{1,0:T(8,128)}) custom-call(f32[1024,128]{1,0:T(8,128)} %bitcast.17, f32[1024,128]{1,0:T(8,128)} %bitcast.21, f32[1024,128]{1,0:T(8,128)} %bitcast.25, f32[1024,128]{1,0:T(8,128)} %bitcast.28, f32[1024,128]{1,0:T(8,128)} %get-tuple-element.48.refs_4_, ...), custom_call_target="tpu_custom_call" | custom-call | tf_op jit(solution)/shard_map/pallas_call | solution.py:737
  111.5 10.9 %all_to_all.26 = f32[32,1,128]{2,1,0:T(1,128)} all-to-all(f32[32,1,128]{2,1,0:T(1,128)} %bitcast.34), channel_id=1, replica_groups=mesh['gx'=4,'gy'=4,'gz'=2] {'gx','gy','gz'}, dimensions={0} | all-to-all | bytes 32768 | tf_op jit(solution)/shard_map/all_to_all | solution.py:845
  122.4 3.4 %shard_map.205 = (f32[3,1024,128]{2,1,0:T(8,128)}, f32[3,32,256]{2,1,0:T(8,128)}) custom-call(f32[32,128]{1,0:T(8,128)} %bitcast.33, f32[3,1024,128]{2,1,0:T(8,128)} %get-tuple-element.52.refs_8_.refs_42_.res, f32[3,32,256]{2,1,0:T(8,128)} %get-tuple-element.39.refs_13_.refs_43_.frac_res, f32[3,1024,128]{2,1,0:T(8,128)} %get-tuple-element.63.refs_8_.vec, ...), custom_call_target="tpu_custom_call" | custom-call | tf_op jit(solution)/shard_map/pallas_call | solution.py:737
  (30 shorter events, 0.1 us)
Async XLA Ops:
  7.0 20.3 %all-to-all-start = ((f32[16,32,128]{2,1,0:T(8,128)}), f32[16,32,128]{2,1,0:T(8,128)S(1)}, u32[]{:S(2)}, u32[]{:S(2)}) async-start(f32[16,32,128]{2,1,0:T(8,128)} %get-tuple-element.42), calls=%async_computation | async-start | bytes 524288 | tf_op jit(solution)/shard_map/all_to_all | solution.py:783
  15.3 7.2 %collective-permute-start = (f32[4,32,128]{2,1,0:T(8,128)}, f32[4,32,128]{2,1,0:T(8,128)S(1)}, u32[]{:S(2)}, u32[]{:S(2)}) collective-permute-start(f32[4,32,128]{2,1,0:T(8,128)} %get-tuple-element.43.refs_18_.refs_22_), channel_id=1, source_target_pairs={{0,8},{8,0},{16,24},{24,16},{1,9},{9,1},{17,25},{25,17},{2,10},{10... | collective-permute-start | bytes 196616 | tf_op jit(solution)/shard_map/ppermute | solution.py:785
  17.2 6.0 %collective-permute-start.1 = (f32[4,32,128]{2,1,0:T(8,128)}, f32[4,32,128]{2,1,0:T(8,128)S(1)}, u32[]{:S(2)}, u32[]{:S(2)}) collective-permute-start(f32[4,32,128]{2,1,0:T(8,128)} %get-tuple-element.44.refs_19_.refs_23_), channel_id=1, source_target_pairs={{0,24},{8,16},{16,8},{24,0},{1,25},{9,17},{17,9},{25,1},{2,26},{10... | collective-permute-start | bytes 196616 | tf_op jit(solution)/shard_map/ppermute | solution.py:785
  18.7 4.9 %collective-permute-start.2 = (f32[4,32,128]{2,1,0:T(8,128)}, f32[4,32,128]{2,1,0:T(8,128)S(1)}, u32[]{:S(2)}, u32[]{:S(2)}) collective-permute-start(f32[4,32,128]{2,1,0:T(8,128)} %get-tuple-element.45.refs_20_.refs_24_), channel_id=1, source_target_pairs={{0,2},{2,0},{4,6},{6,4},{1,3},{3,1},{5,7},{7,5},{8,10},{10,8},{12,... | collective-permute-start | bytes 196616 | tf_op jit(solution)/shard_map/ppermute | solution.py:785
  20.2 6.4 %collective-permute-start.3 = (f32[4,32,128]{2,1,0:T(8,128)}, f32[4,32,128]{2,1,0:T(8,128)S(1)}, u32[]{:S(2)}, u32[]{:S(2)}) collective-permute-start(f32[4,32,128]{2,1,0:T(8,128)} %get-tuple-element.46.refs_21_.refs_25_), channel_id=1, source_target_pairs={{0,6},{2,4},{4,2},{6,0},{1,7},{3,5},{5,3},{7,1},{8,14},{10,12},{12... | collective-permute-start | bytes 196616 | tf_op jit(solution)/shard_map/ppermute | solution.py:785
  22.5 4.0 %collective-permute-start.4 = (f32[4,32,128]{2,1,0:T(8,128)}, f32[4,32,128]{2,1,0:T(8,128)S(1)}, u32[]{:S(2)}, u32[]{:S(2)}) collective-permute-start(f32[4,32,128]{2,1,0:T(8,128)} %get-tuple-element.47.refs_22_.refs_26_), channel_id=1, source_target_pairs={{0,1},{1,0},{2,3},{3,2},{4,5},{5,4},{6,7},{7,6},{8,9},{9,8},{10,11... | collective-permute-start | bytes 196616 | tf_op jit(solution)/shard_map/ppermute | solution.py:785
  22.5 4.8 %copy-start.3 = (f32[4,32,128]{2,1,0:T(8,128)}, f32[4,32,128]{2,1,0:T(8,128)S(1)}, u32[]{:S(2)}) copy-start(f32[4,32,128]{2,1,0:T(8,128)S(1)} %collective-permute-done.refs_23_.refs_27_) | copy-start | bytes 196612
  23.3 4.0 %copy-start.4 = (f32[4,32,128]{2,1,0:T(8,128)}, f32[4,32,128]{2,1,0:T(8,128)S(1)}, u32[]{:S(2)}) copy-start(f32[4,32,128]{2,1,0:T(8,128)S(1)} %collective-permute-done.1.refs_24_.refs_28_) | copy-start | bytes 196612
  23.6 3.7 %copy-start.5 = (f32[4,32,128]{2,1,0:T(8,128)}, f32[4,32,128]{2,1,0:T(8,128)S(1)}, u32[]{:S(2)}) copy-start(f32[4,32,128]{2,1,0:T(8,128)S(1)} %collective-permute-done.2.refs_25_.refs_29_) | copy-start | bytes 196612
  26.5 0.8 copy-start.6
  26.6 0.8 copy-start.7
  27.3 0.7 copy-start
  46.2 14.9 %all-to-all-start.1 = ((f32[16,24,128]{2,1,0:T(8,128)}), f32[16,24,128]{2,1,0:T(8,128)S(1)}, u32[]{:S(2)}, u32[]{:S(2)}) async-start(f32[16,24,128]{2,1,0:T(8,128)} %get-tuple-element.57), calls=%async_computation.1 | async-start | bytes 393216 | tf_op jit(solution)/shard_map/all_to_all | solution.py:783
  50.2 7.2 %collective-permute-start.5 = (f32[3,32,128]{2,1,0:T(8,128)}, f32[3,32,128]{2,1,0:T(8,128)S(1)}, u32[]{:S(2)}, u32[]{:S(2)}) collective-permute-start(f32[3,32,128]{2,1,0:T(8,128)} %get-tuple-element.58.refs_32_), channel_id=1, source_target_pairs={{0,8},{8,0},{16,24},{24,16},{1,9},{9,1},{17,25},{25,17},{2,10},{10... | collective-permute-start | bytes 147464 | tf_op jit(solution)/shard_map/ppermute | solution.py:785
  52.1 5.3 %collective-permute-start.6 = (f32[3,32,128]{2,1,0:T(8,128)}, f32[3,32,128]{2,1,0:T(8,128)S(1)}, u32[]{:S(2)}, u32[]{:S(2)}) collective-permute-start(f32[3,32,128]{2,1,0:T(8,128)} %get-tuple-element.59.refs_33_), channel_id=1, source_target_pairs={{0,24},{8,16},{16,8},{24,0},{1,25},{9,17},{17,9},{25,1},{2,26},{10... | collective-permute-start | bytes 147464 | tf_op jit(solution)/shard_map/ppermute | solution.py:785
  53.6 4.6 %collective-permute-start.7 = (f32[3,32,128]{2,1,0:T(8,128)}, f32[3,32,128]{2,1,0:T(8,128)S(1)}, u32[]{:S(2)}, u32[]{:S(2)}) collective-permute-start(f32[3,32,128]{2,1,0:T(8,128)} %get-tuple-element.60.refs_34_), channel_id=1, source_target_pairs={{0,2},{2,0},{4,6},{6,4},{1,3},{3,1},{5,7},{7,5},{8,10},{10,8},{12,... | collective-permute-start | bytes 147464 | tf_op jit(solution)/shard_map/ppermute | solution.py:785
  55.0 6.1 %collective-permute-start.8 = (f32[3,32,128]{2,1,0:T(8,128)}, f32[3,32,128]{2,1,0:T(8,128)S(1)}, u32[]{:S(2)}, u32[]{:S(2)}) collective-permute-start(f32[3,32,128]{2,1,0:T(8,128)} %get-tuple-element.61.refs_35_), channel_id=1, source_target_pairs={{0,6},{2,4},{4,2},{6,0},{1,7},{3,5},{5,3},{7,1},{8,14},{10,12},{12... | collective-permute-start | bytes 147464 | tf_op jit(solution)/shard_map/ppermute | solution.py:785
  57.4 3.7 %collective-permute-start.9 = (f32[3,32,128]{2,1,0:T(8,128)}, f32[3,32,128]{2,1,0:T(8,128)S(1)}, u32[]{:S(2)}, u32[]{:S(2)}) collective-permute-start(f32[3,32,128]{2,1,0:T(8,128)} %get-tuple-element.62.refs_36_), channel_id=1, source_target_pairs={{0,1},{1,0},{2,3},{3,2},{4,5},{5,4},{6,7},{7,6},{8,9},{9,8},{10,11... | collective-permute-start | bytes 147464 | tf_op jit(solution)/shard_map/ppermute | solution.py:785
  57.4 3.8 %copy-start.12 = (f32[3,32,128]{2,1,0:T(8,128)}, f32[3,32,128]{2,1,0:T(8,128)S(1)}, u32[]{:S(2)}) copy-start(f32[3,32,128]{2,1,0:T(8,128)S(1)} %collective-permute-done.5.refs_37_) | copy-start | bytes 147460
  57.4 3.7 %copy-start.14 = (f32[3,32,128]{2,1,0:T(8,128)}, f32[3,32,128]{2,1,0:T(8,128)S(1)}, u32[]{:S(2)}) copy-start(f32[3,32,128]{2,1,0:T(8,128)S(1)} %collective-permute-done.6.refs_38_) | copy-start | bytes 147460
  58.2 3.0 %copy-start.15 = (f32[3,32,128]{2,1,0:T(8,128)}, f32[3,32,128]{2,1,0:T(8,128)S(1)}, u32[]{:S(2)}) copy-start(f32[3,32,128]{2,1,0:T(8,128)S(1)} %collective-permute-done.7.refs_39_) | copy-start | bytes 147460
  61.1 0.6 copy-start.16
  61.1 0.6 copy-start.17
  61.1 0.7 copy-start.1
  79.8 15.6 %all-to-all-start.2 = ((f32[16,24,128]{2,1,0:T(8,128)}), f32[16,24,128]{2,1,0:T(8,128)S(1)}, u32[]{:S(2)}, u32[]{:S(2)}) async-start(f32[16,24,128]{2,1,0:T(8,128)} %get-tuple-element.66), calls=%async_computation.2 | async-start | bytes 393216 | tf_op jit(solution)/shard_map/all_to_all | solution.py:783
  84.4 7.2 %collective-permute-start.10 = (f32[3,32,128]{2,1,0:T(8,128)}, f32[3,32,128]{2,1,0:T(8,128)S(1)}, u32[]{:S(2)}, u32[]{:S(2)}) collective-permute-start(f32[3,32,128]{2,1,0:T(8,128)} %get-tuple-element.67.refs_32_), channel_id=1, source_target_pairs={{0,8},{8,0},{16,24},{24,16},{1,9},{9,1},{17,25},{25,17},{2,10},{10... | collective-permute-start | bytes 147464 | tf_op jit(solution)/shard_map/ppermute | solution.py:785
  86.4 5.5 %collective-permute-start.11 = (f32[3,32,128]{2,1,0:T(8,128)}, f32[3,32,128]{2,1,0:T(8,128)S(1)}, u32[]{:S(2)}, u32[]{:S(2)}) collective-permute-start(f32[3,32,128]{2,1,0:T(8,128)} %get-tuple-element.68.refs_33_), channel_id=1, source_target_pairs={{0,24},{8,16},{16,8},{24,0},{1,25},{9,17},{17,9},{25,1},{2,26},{10... | collective-permute-start | bytes 147464 | tf_op jit(solution)/shard_map/ppermute | solution.py:785
  87.8 4.3 %collective-permute-start.12 = (f32[3,32,128]{2,1,0:T(8,128)}, f32[3,32,128]{2,1,0:T(8,128)S(1)}, u32[]{:S(2)}, u32[]{:S(2)}) collective-permute-start(f32[3,32,128]{2,1,0:T(8,128)} %get-tuple-element.69.refs_34_), channel_id=1, source_target_pairs={{0,2},{2,0},{4,6},{6,4},{1,3},{3,1},{5,7},{7,5},{8,10},{10,8},{12,... | collective-permute-start | bytes 147464 | tf_op jit(solution)/shard_map/ppermute | solution.py:785
  89.3 6.1 %collective-permute-start.13 = (f32[3,32,128]{2,1,0:T(8,128)}, f32[3,32,128]{2,1,0:T(8,128)S(1)}, u32[]{:S(2)}, u32[]{:S(2)}) collective-permute-start(f32[3,32,128]{2,1,0:T(8,128)} %get-tuple-element.70.refs_35_), channel_id=1, source_target_pairs={{0,6},{2,4},{4,2},{6,0},{1,7},{3,5},{5,3},{7,1},{8,14},{10,12},{12... | collective-permute-start | bytes 147464 | tf_op jit(solution)/shard_map/ppermute | solution.py:785
  91.7 3.7 %collective-permute-start.14 = (f32[3,32,128]{2,1,0:T(8,128)}, f32[3,32,128]{2,1,0:T(8,128)S(1)}, u32[]{:S(2)}, u32[]{:S(2)}) collective-permute-start(f32[3,32,128]{2,1,0:T(8,128)} %get-tuple-element.71.refs_36_), channel_id=1, source_target_pairs={{0,1},{1,0},{2,3},{3,2},{4,5},{5,4},{6,7},{7,6},{8,9},{9,8},{10,11... | collective-permute-start | bytes 147464 | tf_op jit(solution)/shard_map/ppermute | solution.py:785
  91.7 3.8 %copy-start.8 = (f32[3,32,128]{2,1,0:T(8,128)}, f32[3,32,128]{2,1,0:T(8,128)S(1)}, u32[]{:S(2)}) copy-start(f32[3,32,128]{2,1,0:T(8,128)S(1)} %collective-permute-done.10.refs_37_) | copy-start | bytes 147460
  91.8 3.6 %copy-start.9 = (f32[3,32,128]{2,1,0:T(8,128)}, f32[3,32,128]{2,1,0:T(8,128)S(1)}, u32[]{:S(2)}) copy-start(f32[3,32,128]{2,1,0:T(8,128)S(1)} %collective-permute-done.11.refs_38_) | copy-start | bytes 147460
  92.2 3.3 %copy-start.10 = (f32[3,32,128]{2,1,0:T(8,128)}, f32[3,32,128]{2,1,0:T(8,128)S(1)}, u32[]{:S(2)}) copy-start(f32[3,32,128]{2,1,0:T(8,128)S(1)} %collective-permute-done.12.refs_39_) | copy-start | bytes 147460
  95.4 0.6 copy-start.11
  95.4 0.6 copy-start.13
  95.4 0.7 copy-start.2

commit v2 on v1

v2 whole, which is shorter than its diff:
```python
import functools

import jax
import jax.numpy as jnp
from jax import lax
from jax.experimental import pallas as pl
from jax.experimental.pallas import tpu as pltpu
from jax.sharding import PartitionSpec as P

F32 = jnp.float32
BF16 = jnp.bfloat16
EPS = 1e-06
PLANE = ("gx", "gy")


def swap_slots(mesh_shape):
    slots = []
    for axis in ("gx", "gy", "gz"):
        if mesh_shape[axis] > 1:
            slots.append((axis, 0))
        if mesh_shape[axis] > 2:
            slots.append((axis, 1))
    return tuple(slots)


def swap_pairs(size, odd):
    pairs = []
    for i in range(size):
        up = i % 2 == odd
        partner = (i + 1 if up else i - 1) % size
        pairs.append((i, partner))
    if sorted(j for _, j in pairs) != list(range(size)):
        pairs = [(i, j if abs(i - j) == 1 else i) for i, j in pairs]
    return pairs


def slot_side(axis, odd, sizes):
    index = lax.axis_index(axis)
    high = lax.rem(index, 2) == odd
    valid = jnp.where(high, index + 1 < sizes[axis], index > 0)
    return high, valid


def mobilities(p, s, d):
    share = (1.0 - s) * (1.0 - s)
    scaled = (1.0 + 0.05 * p) * share
    mg = (2.0 + p) * (s * s)
    return scaled * (1.0 - d), scaled * d + mg, mg


def mobility_steps(p, s, d, dp, ds, dd):
    lb = 1.0 + 0.05 * p
    gas = 2.0 + p
    open_s = 1.0 - s
    scaled = lb * (open_s * open_s)
    mg = gas * (s * s)
    solute = scaled * d
    steps = mobility_moves(lb, gas, open_s, s, d, dp, ds, dd)
    return scaled - solute, solute + mg, mg, steps[0], steps[1], steps[2]


def mobility_moves(lb, gas, open_s, s, d, dp, ds, dd):
    by_s = lb * ds
    move = (0.05 * dp) * open_s - by_s
    move_d = (lb * open_s) * dd
    step = open_s * (move - by_s)
    by_p, by_gas = s * dp, gas * ds
    both = by_p + by_gas
    dmg = s * (both + by_gas)
    dml = step * d + open_s * move_d
    return step - dml, dml + dmg, dmg, move, move_d, 0.1 * both


def cell_steps(p, s, d, dp, ds, dd):
    lb = 1.0 + 0.05 * p
    dmw, dmh, dmg, move, move_d, gas_mass = mobility_moves(
        lb, 2.0 + p, 1.0 - s, s, d, dp, ds, dd
    )
    in_liquid = move * d + move_d
    return dmw, dmh, dmg, move - in_liquid, in_liquid + gas_mass, closure_step(p, s, d, dp, ds, dd)


def masses(p, s, d):
    lb_open = (1.0 + 0.05 * p) * (1.0 - s)
    return lb_open * (1.0 - d), lb_open * d + (0.2 + 0.1 * p) * s


def closure(p, s, d):
    gap = 0.05 + 0.025 * p - d
    return s + gap - jnp.sqrt(s * s + gap * gap + 1e-4)


def closure_step(p, s, d, dp, ds, dd):
    gap = 0.05 + 0.025 * p - d
    inverse = lax.rsqrt(s * s + gap * gap + 1e-4)
    dgap = 0.025 * dp - dd
    return ds + dgap - (s * ds + gap * dgap) * inverse


def halves(value):
    high = value.astype(BF16)
    return high, (value - high.astype(F32)).astype(BF16)


def split_dot(value, weights, dims):
    high, low = halves(value)
    dot = functools.partial(
        lax.dot_general, dimension_numbers=(dims, ((), ())), preferred_element_type=F32
    )
    return dot(high, weights) + dot(low, weights)


def one_hot(size, index_row):
    shape = (size, index_row.shape[1])
    rows = lax.broadcasted_iota(jnp.int32, shape, 0)
    return jnp.where(rows == index_row, 1.0, 0.0)


class Plan:
    def __init__(self, mesh_shape, pressure, frac, column, cap):
        self.sizes = dict(mesh_shape)
        self.slots = swap_slots(mesh_shape)
        self.z, self.x, self.y = pressure.shape
        self.seg = frac.shape[1]
        self.pairs = column.shape[1]
        self.peers = self.pairs // cap
        self.cap = cap
        self.rows = self.z * self.x
        self.groups = 128 // cap
        self.pack_rows = 6 * self.z // self.groups
        self.half = self.x // 2
        assert self.y == 128 and self.x == self.z == 32
        assert self.groups == 8 and self.peers % self.groups == 0
        self.faces = []
        for axis, _ in self.slots:
            if axis != "gy" or axis not in self.faces:
                self.faces.append(axis)
        self.slot_face = []
        spot = 0
        for i, (axis, _) in enumerate(self.slots):
            if i and not (axis == "gy" and self.slots[i - 1][0] == "gy"):
                spot += 1
            self.slot_face.append(spot)


def plane_rows(plan, z):
    return pl.ds(pl.multiple_of(z * plan.x, 8), plan.x)


def column_masks(plan, column):
    x, y = lax.div(column, plan.y), lax.rem(column, plan.y)
    wide = one_hot(2 * plan.y, lax.div(x, plan.half) * plan.y + y).astype(BF16)
    return wide, one_hot(plan.half, lax.rem(x, plan.half))


STEP = 8


def gather_cells(plan, fields, column, dst):
    wide, one_x = column_masks(plan, column)

    def body(c, carry):
        for f, field in enumerate(fields):
            rows = pl.ds(pl.multiple_of(c * STEP * plan.x, 8), STEP * plan.x)
            value = field[rows, :].reshape(STEP, plan.x, plan.y)
            sides = [
                value[:, i * plan.half : (i + 1) * plan.half].reshape(STEP * plan.half, plan.y)
                for i in (0, 1)
            ]
            got = split_dot(jnp.concatenate(sides, axis=1), wide, ((1,), (0,)))
            got = got.reshape(STEP, plan.half, plan.pairs) * one_x[None]
            start = pl.multiple_of((3 + f) * plan.z + c * STEP, 8)
            dst[pl.ds(start, STEP), :] = jnp.sum(got, axis=1)
        return carry

    lax.fori_loop(0, plan.z // STEP, body, 0)


def scatter_cells(plan, rates, column, dsts, y_store):
    wide, one_x = column_masks(plan, column)
    lane = lax.broadcasted_iota(jnp.int32, (plan.x, 128), 1)
    edge = (lane == 0) | (lane == 127)

    def body(c, carry):
        for f, dst in enumerate(dsts):
            block = rates[pl.ds(pl.multiple_of(f * plan.z + c * STEP, 8), STEP), :]
            spread = jnp.concatenate(
                [one_x * block[j : j + 1, :] for j in range(STEP)], axis=0
            )
            got = split_dot(spread, wide, ((1,), (1,)))
            for j in range(STEP):
                z = c * STEP + j
                here = plane_rows(plan, z)
                rows = slice(j * plan.half, (j + 1) * plan.half)
                off = jnp.concatenate(
                    [got[rows, i * plan.y : (i + 1) * plan.y] for i in (0, 1)], axis=0
                )
                if "gy" in plan.faces:
                    turn = lax.rem(255 - 2 * z, 128)
                    off = off - jnp.where(edge, pltpu.roll(y_store[f], turn, 1), 0.0)
                dst[here, :] = dst[here, :] - off
        return carry

    lax.fori_loop(0, plan.z // STEP, body, 0)


def gather_segments(plan, fields, segment, dst):
    one_s = one_hot(plan.seg, segment).astype(BF16)
    for f, field in enumerate(fields):
        dst[f * plan.z : (f + 1) * plan.z, :] = split_dot(field[...], one_s, ((1,), (0,)))


def scatter_segments(plan, rate, segment):
    one_s = one_hot(plan.seg, segment).astype(BF16)
    return split_dot(rate, one_s, ((1,), (1,)))


def block_transpose(plan, tiles):
    tiles = list(tiles)
    block = lax.broadcasted_iota(jnp.int32, tiles[0].shape, 1) // plan.cap
    bit = 1
    while bit < plan.groups:
        clear = (block & bit) == 0
        for i in range(plan.groups):
            if i & bit:
                continue
            low, high = tiles[i], tiles[i | bit]
            shift = bit * plan.cap
            tiles[i] = jnp.where(clear, low, pltpu.roll(high, shift, 1))
            tiles[i | bit] = jnp.where(clear, pltpu.roll(low, 128 - shift, 1), high)
        bit *= 2
    return tiles


def pack_pairs(plan, own, dst):
    n = plan.pack_rows
    for half in range(plan.pairs // 128):
        lanes = slice(half * 128, (half + 1) * 128)
        tiles = [own[g * n : (g + 1) * n, lanes] for g in range(plan.groups)]
        for c, tile in enumerate(block_transpose(plan, tiles)):
            dst[half * plan.groups + c, 0:n, :] = tile


def unpack_pairs(plan, src, dst):
    n = plan.pack_rows
    for half in range(plan.pairs // 128):
        lanes = slice(half * 128, (half + 1) * 128)
        tiles = [src[half * plan.groups + c, 0:n, :] for c in range(plan.groups)]
        for g, tile in enumerate(block_transpose(plan, tiles)):
            dst[g * n : (g + 1) * n, lanes] = tile


def write_faces(plan, fields, outs):
    pair = lax.broadcasted_iota(jnp.int32, (plan.x, 128), 1) // 2
    y_out = None
    for (axis, odd), spot in zip(plan.slots, plan.slot_face):
        out = outs[spot]
        high, _ = slot_side(axis, odd, plan.sizes)
        if axis == "gx":
            row = jnp.where(high, plan.x - 1, 0)
            for f, field in enumerate(fields):
                out[f] = field[pl.ds(row, plan.z, stride=plan.x), :]
        elif axis == "gz":
            start = pl.multiple_of(jnp.where(high, (plan.z - 1) * plan.x, 0), 8)
            for f, field in enumerate(fields):
                out[f] = field[pl.ds(start, plan.x), :]
        else:
            y_out = out
    if y_out is None:
        return
    zero = jnp.zeros((plan.x, 128), F32)

    def body(c, carry):
        carry = list(carry)
        for j in range(4):
            z = c * 4 + j
            for f, field in enumerate(fields):
                value = field[plane_rows(plan, z), :]
                carry[f] = jnp.where(pair == z, pltpu.roll(value, 2 * z + 1, 1), carry[f])
        return tuple(carry)

    for f, value in enumerate(lax.fori_loop(0, plan.z // 4, body, (zero,) * len(fields))):
        y_out[f] = value


def merge_faces(plan, own, recv, count):
    lane = lax.broadcasted_iota(jnp.int32, (plan.x, 128), 1)
    even = lane % 2 == 0
    found = []
    y_recv = []
    for i, (axis, odd) in enumerate(plan.slots):
        high, valid = slot_side(axis, odd, plan.sizes)
        mine = tuple(own[plan.slot_face[i]][f] for f in range(count))
        theirs = tuple(recv[i][f] for f in range(count))
        if axis != "gy":
            found.append((axis, high, valid, mine, theirs))
            continue
        y_recv.append((high, theirs))
        if odd or plan.sizes["gy"] == 2:
            first = y_recv[0][0]
            above = tuple(jnp.where(first, a, b) for a, b in zip(y_recv[0][1], y_recv[-1][1]))
            below = tuple(jnp.where(first, b, a) for a, b in zip(y_recv[0][1], y_recv[-1][1]))
            merged = tuple(
                jnp.where(even, pltpu.roll(a, 127, 1), pltpu.roll(b, 1, 1))
                for a, b in zip(above, below)
            )
            index = lax.axis_index("gy")
            up = jnp.where(index + 1 < plan.sizes["gy"], 1, 0)
            down = jnp.where(index > 0, 1, 0)
            inside = jnp.where(even, up, down) * jnp.where(lane < 2 * plan.z, 1, 0)
            found.append((axis, None, inside == 1, mine, merged))
    return found


def vertical_sign(axis, high):
    if axis != "gz":
        return None
    return jnp.where(high, 1.0, -1.0).astype(F32)


def add_faces(plan, faces, fluxes, dsts, y_store):
    for (axis, high, *_), pair in zip(faces, fluxes):
        for i, (dst, flux) in enumerate(zip(dsts, pair)):
            if axis == "gx":
                rows = pl.ds(jnp.where(high, plan.x - 1, 0), plan.z, stride=plan.x)
                dst[rows, :] = dst[rows, :] + flux
            elif axis == "gz":
                start = pl.multiple_of(jnp.where(high, (plan.z - 1) * plan.x, 0), 8)
                rows = pl.ds(start, plan.x)
                dst[rows, :] = dst[rows, :] + flux
            else:
                y_store[i] = flux


UNROLL = 2


def sweep(plan, plane, dsts, fx, carry, first, count):
    def body(c, carry):
        carry = list(carry)
        for u in range(UNROLL):
            z = first + c * UNROLL + u
            here = plane_rows(plan, z)
            for i, (along_y, along_x, along_z) in enumerate(plane(z)):
                slot = 2 * u + i
                total = dsts[i][here, :] + (along_y - pltpu.roll(along_y, 1, 1))
                fx[slot, 8 : 8 + plan.x, :] = along_x
                total = total + (along_x - fx[slot, 7 : 7 + plan.x, :])
                dsts[i][here, :] = total + (along_z - carry[i])
                carry[i] = along_z
        return tuple(carry)

    return lax.fori_loop(0, count // UNROLL, body, carry)


def sweep_start(plan, fx):
    zero = jnp.zeros((plan.x, 128), F32)
    for i in range(2 * UNROLL):
        fx[i, 0:8, :] = jnp.zeros((8, 128), F32)
    return zero, zero


CHUNKS = 4


def chunk_rows(plan, c):
    size = plan.rows // CHUNKS
    return pl.ds(c * size, size)


def chunk_loop(plan, c, body):
    size = plan.z // CHUNKS
    lax.fori_loop(c * size, (c + 1) * size, body, 0)


def residual_plane(plan, base, k_ref, coef):
    p_ref, w_ref, h_ref, g_ref = base
    lane = lax.broadcasted_iota(jnp.int32, (plan.x, 128), 1)
    row = lax.broadcasted_iota(jnp.int32, (plan.x, 128), 0)
    back = lambda v: pltpu.roll(v, 127, 1)

    def plane(z):
        here, below = plane_rows(plan, z), plane_rows(plan, z + 1)
        beside = pl.ds(z * plan.x + 1, plan.x)
        p0, w0, h0, k0 = (r[here, :] for r in (p_ref, w_ref, h_ref, k_ref))
        flows = []
        sides = (
            (0, lane == 127, tuple(back(v) for v in (p0, w0, h0, k0))),
            (3, row == plan.x - 1, tuple(r[beside, :] for r in (p_ref, w_ref, h_ref, k_ref))),
        )
        for spot, last, (p1, w1, h1, k1) in sides:
            k = jnp.where(last, 0.0, k0 * k1 / (k0 + k1))
            drop, w, h = k * (p0 - p1), w0 + w1, h0 + h1
            coef[spot, here, :] = drop
            coef[spot + 1, here, :] = k * w
            coef[spot + 2, here, :] = k * h
            flows.append((drop * w, drop * h))
        p1, w1, h1, k1 = (r[below, :] for r in (p_ref, w_ref, h_ref, k_ref))
        k = jnp.where(z == plan.z - 1, 0.0, 0.2).astype(F32) * (k0 * k1 / (k0 + k1))
        total = 0.0125 * (p0 + p1)
        drop = k * (p0 - p1 + (0.5 + total))
        extra = k * (total - 0.4)
        w, h, g = w0 + w1, h0 + h1, g_ref[here, :] + g_ref[below, :]
        for i, value in enumerate((drop, k * w, k * h, extra, k * g)):
            coef[6 + i, here, :] = value
        flows.append((drop * w, drop * h + extra * g))
        return tuple(zip(*flows))

    return plane


def jacobian_plane(plan, steps, coef):
    q_ref, a_ref, b_ref, c_ref = steps
    back = lambda v: pltpu.roll(v, 127, 1)

    def plane(z):
        here, below = plane_rows(plan, z), plane_rows(plan, z + 1)
        beside = pl.ds(z * plan.x + 1, plan.x)
        q0, a0, b0 = q_ref[here, :], a_ref[here, :], b_ref[here, :]
        flows = []
        sides = (
            (0, tuple(back(v) for v in (q0, a0, b0))),
            (3, tuple(r[beside, :] for r in (q_ref, a_ref, b_ref))),
        )
        for spot, (q1, a1, b1) in sides:
            drop, w, h = (coef[spot + i, here, :] for i in range(3))
            dq = q0 - q1
            flows.append(((a0 + a1) * drop + w * dq, (b0 + b1) * drop + h * dq))
        q1, a1, b1 = q_ref[below, :], a_ref[below, :], b_ref[below, :]
        drop, w, h, extra, g = (coef[6 + i, here, :] for i in range(5))
        dtotal = 0.0125 * (q0 + q1)
        dq = q0 - q1 + dtotal
        c = c_ref[here, :] + c_ref[below, :]
        flows.append(
            ((a0 + a1) * drop + w * dq, (b0 + b1) * drop + h * dq + (c * extra + g * dtotal))
        )
        return tuple(zip(*flows))

    return plane


class Copies:
    def __init__(self, sems):
        self.sems, self.used = sems, 0

    def start(self, src, dst):
        copy = pltpu.make_async_copy(src, dst, self.sems.at[self.used])
        self.used += 1
        copy.start()
        return copy


def wait_all(copies):
    for copy in copies:
        copy.wait()


def clear_tails(plan, refs):
    for ref in refs:
        ref[plan.rows : plan.rows + plan.x + 8, :] = jnp.zeros((plan.x + 8, 128), F32)


def face_flux(sign, conductance, own, other, own_step=None, other_step=None):
    p0, p1 = own[0], other[0]
    if own_step is None:
        (w0, h0, g0), (w1, h1, g1) = mobilities(*own), mobilities(*other)
    else:
        w0, h0, g0, a0, b0, c0 = mobility_steps(*own, *own_step)
        w1, h1, g1, a1, b1, c1 = mobility_steps(*other, *other_step)
        q0, q1 = own_step[0], other_step[0]
    drop = p0 - p1
    if sign is not None:
        total = 0.0125 * (p0 + p1)
        drop = drop + sign * (0.5 + total)
        extra = sign * (total - 0.4)
    if own_step is None:
        water = (w0 + w1) * drop
        hydrogen = (h0 + h1) * drop
        if sign is not None:
            hydrogen = hydrogen + (g0 + g1) * extra
        return conductance * water, conductance * hydrogen
    dq = q0 - q1
    if sign is not None:
        dtotal = sign * (0.0125 * (q0 + q1))
        dq = dq + dtotal
    water = (a0 + a1) * drop + (w0 + w1) * dq
    hydrogen = (b0 + b1) * drop + (h0 + h1) * dq
    if sign is not None:
        hydrogen = hydrogen + (c0 + c1) * extra + (g0 + g1) * dtotal
    return conductance * water, conductance * hydrogen


def first_kernel(plan, *refs):
    n = len(plan.faces)
    grids = refs[:4]
    fp, fs, fd, segment, column, kind, count, table = refs[4:12]
    faces, (pack, own, weight) = refs[12 : 12 + n], refs[12 + n : 15 + n]
    local, sems = refs[15 + n :]
    copies = Copies(sems)
    loads = [copies.start(g, local.at[i]) for i, g in enumerate(grids)]
    gather_segments(plan, (fp, fs, fd), segment[...], own)
    kinds = kind[...]
    picked = jnp.zeros(kinds.shape, F32)
    for j in range(table.shape[0]):
        picked = jnp.where(kinds == j, table[j], picked)
    slot = lax.broadcasted_iota(jnp.int32, kinds.shape, 1)
    block, rank = slot // plan.cap, lax.rem(slot, plan.cap)
    live = jnp.zeros(kinds.shape, jnp.int32)
    for j in range(plan.peers):
        live = jnp.where(block == j, count[0, j], live)
    picked = jnp.where(rank < live, picked, 0.0)
    weight[...] = picked
    for half in range(plan.pairs // 128):
        tile = jnp.broadcast_to(picked[:, half * 128 : (half + 1) * 128], (8, 128))
        for c in range(plan.groups):
            moved = pltpu.roll(tile, 128 - c * plan.cap, 1) if c else tile
            pack[half * plan.groups + c, plan.pack_rows : plan.pack_rows + 8, :] = moved
    wait_all(loads[:3])
    fields = tuple(local.at[i] for i in range(4))
    gather_cells(plan, fields[:3], column[...], own)
    pack_pairs(plan, own, pack)
    wait_all(loads[3:])
    write_faces(plan, fields, faces)


def pair_values(plan, ref, side):
    first = 3 * side
    return tuple(ref[(first + f) * plan.z : (first + f + 1) * plan.z, :] for f in range(3))


def residual_inner(plan, *refs):
    grids, (_, res_out, coef_out) = refs[:7], refs[7:10]
    sp, sk, sw, sh, sg, local, res, coef, fx, sems = refs[10:]
    copies = Copies(sems)
    places = [sp] + [local.at[i] for i in range(5)] + [sk]
    loads = [
        [
            copies.start(grid.at[chunk_rows(plan, c)], place.at[chunk_rows(plan, c)])
            for grid, place in zip(grids, places)
        ]
        for c in range(CHUNKS)
    ]
    s, d, old_water, old_hydrogen, volume = (local.at[i] for i in range(5))
    res_w, res_h, res_c = (res.at[i] for i in range(3))
    clear_tails(plan, (sp, sw, sh, sg))
    sk[plan.rows : plan.rows + plan.x + 8, :] = jnp.ones((plan.x + 8, 128), F32)

    def cells(z, carry):
        here = plane_rows(plan, z)
        pv, sv, dv = sp[here, :], s[here, :], d[here, :]
        sw[here, :], sh[here, :], sg[here, :] = mobilities(pv, sv, dv)
        mw, mh = masses(pv, sv, dv)
        vol = volume[here, :]
        res_w[here, :] = vol * (mw - old_water[here, :])
        res_h[here, :] = vol * (mh - old_hydrogen[here, :])
        res_c[here, :] = closure(pv, sv, dv)
        return carry

    for c in range(CHUNKS):
        wait_all(loads[c])
        chunk_loop(plan, c, cells)
    plane = residual_plane(plan, (sp, sw, sh, sg), sk, coef)
    carry = sweep_start(plan, fx)
    stores = []
    for c in range(CHUNKS):
        size = plan.z // CHUNKS
        carry = sweep(plan, plane, (res_w, res_h), fx, carry, c * size, size)
        rows = chunk_rows(plan, c)
        stores.append(copies.start(res.at[:, rows], res_out.at[:, rows]))
        stores.append(copies.start(coef.at[:, rows], coef_out.at[:, rows]))
    wait_all(stores)


def residual_kernel(plan, *refs):
    n, m = len(plan.slots), len(plan.faces)
    refs = list(refs)
    take = lambda count: [refs.pop(0) for _ in range(count)]
    (res_in,) = take(1)
    fp, fs, fd, frac_water, frac_hydrogen, frac_volume = take(6)
    segment, column, weight, own, recv = take(5)
    own_faces, recv_faces = take(m), take(n)
    res_out, frac_res, kb = take(3)
    faces = take(m)
    pack, own_res, got, weight_back = take(4)
    res, y_store, rates, sems = take(4)
    fields = tuple(res.at[i] for i in range(3))
    copies = Copies(sems)
    load = copies.start(res_in, res)

    unpack_pairs(plan, recv, got)
    lane8 = lax.broadcasted_iota(jnp.int32, (8, 128), 1) // plan.cap
    for half in range(plan.pairs // 128):
        total = None
        for c in range(plan.groups):
            tile = recv[half * plan.groups + c, plan.pack_rows : plan.pack_rows + 8, :]
            moved = pltpu.roll(tile, c * plan.cap, 1) if c else tile
            total = moved if total is None else jnp.where(lane8 == c, moved, total)
        weight_back[:, half * 128 : (half + 1) * 128] = total[0:1, :]

    def pair_rates(weights, seg_values, cell_values):
        w0, h0, _ = mobilities(*seg_values)
        w1, h1, _ = mobilities(*cell_values)
        flow = (0.5 * weights) * (seg_values[0] - cell_values[0])
        return flow * (w0 + w1), flow * (h0 + h1)

    rate_w, rate_h = pair_rates(
        weight_back[...], pair_values(plan, own, 0), pair_values(plan, got, 1)
    )
    fpv, fsv, fdv = fp[...], fs[...], fd[...]
    mass_w, mass_h = masses(fpv, fsv, fdv)
    vol = frac_volume[...]
    frac_res[0] = vol * (mass_w - frac_water[...]) + scatter_segments(plan, rate_w, segment[...])
    frac_res[1] = vol * (mass_h - frac_hydrogen[...]) + scatter_segments(
        plan, rate_h, segment[...]
    )
    frac_res[2] = closure(fpv, fsv, fdv)
    rate_w, rate_h = pair_rates(weight[...], pair_values(plan, got, 0), pair_values(plan, own, 1))
    rates[0 : plan.z, :] = rate_w
    rates[plan.z : 2 * plan.z, :] = rate_h

    found = merge_faces(plan, own_faces, recv_faces, 4)
    fluxes = []
    for i, (axis, high, valid, mine, theirs) in enumerate(found):
        k0, k1 = mine[3], theirs[3]
        scale = 0.2 if axis == "gz" else 1.0
        conductance = jnp.where(
            valid, scale * (k0 * k1 / jnp.where(valid, k0 + k1, 1.0)), 0.0
        )
        kb[i] = conductance
        fluxes.append(face_flux(vertical_sign(axis, high), conductance, mine[:3], theirs[:3]))
    load.wait()
    add_faces(plan, found, fluxes, fields[:2], y_store)
    scatter_cells(plan, rates, column[...], fields[:2], y_store)
    store = copies.start(res, res_out)
    send_parts(plan, fields, frac_res, segment, column, faces, own_res, pack)
    store.wait()


def send_parts(plan, fields, frac_fields, segment, column, faces, own, pack):
    write_faces(plan, fields, faces)
    gather_segments(plan, tuple(frac_fields.at[i] for i in range(3)), segment[...], own)
    gather_cells(plan, fields, column[...], own)
    pack_pairs(plan, own, pack)


def total_of(value):
    return jnp.sum(jnp.sum(value, axis=0, keepdims=True), axis=1, keepdims=True)


def block_sums(plan, cell_refs, frac_refs, function, count):
    def body(z, carry):
        here = plane_rows(plan, z)
        for f in range(3):
            parts = function(*(group[f][here, :] for group in cell_refs))
            carry = tuple(c + part for c, part in zip(carry, parts))
        return carry

    zero = jnp.zeros((plan.x, 128), F32)
    sums = lax.fori_loop(0, plan.z, body, (zero,) * count, unroll=2)
    sums = [total_of(v) for v in sums]
    for f in range(3):
        parts = function(*(ref[f] for ref in frac_refs))
        sums = [v + total_of(part) for v, part in zip(sums, parts)]
    return sums


def safe_ratio(top, bottom):
    good = bottom > 0.0
    return jnp.where(good, top / jnp.where(good, bottom, 1.0), 0.0)


def jacobian_inner(plan, last, *refs):
    refs = list(refs)
    take = lambda count: [refs.pop(0) for _ in range(count)]
    grids = take(4)
    vec_in, coef_in = take(2)
    if last:
        base_in, base_frac, frac_vec = take(3)
        out_back, stats = take(2)
    else:
        (out_back,) = take(1)
    sq, sa, sb, sc, local, coef, out, fx, sems = take(9)
    copies = Copies(sems)
    places = [sq] + [local.at[i] for i in range(6)]
    sources = [vec_in.at[i] for i in range(3)] + list(grids)
    loads = [
        [
            copies.start(grid.at[chunk_rows(plan, c)], place.at[chunk_rows(plan, c)])
            for grid, place in zip(sources, places)
        ]
        for c in range(CHUNKS)
    ]
    coefs = [
        copies.start(coef_in.at[:, chunk_rows(plan, c)], coef.at[:, chunk_rows(plan, c)])
        for c in range(CHUNKS)
    ]
    if last:
        (base,) = take(1)
        late = copies.start(base_in, base)
    v1, v2, p, s, d, volume = (local.at[i] for i in range(6))
    out_w, out_h, out_c = (out.at[i] for i in range(3))
    clear_tails(plan, (sq, sa, sb, sc))

    def cells(z, carry):
        here = plane_rows(plan, z)
        values = tuple(r[here, :] for r in (p, s, d, sq, v1, v2))
        sa[here, :], sb[here, :], sc[here, :], mw, mh, out_c[here, :] = cell_steps(*values)
        vol = volume[here, :]
        out_w[here, :] = vol * mw
        out_h[here, :] = vol * mh
        return carry

    for c in range(CHUNKS):
        wait_all(loads[c])
        chunk_loop(plan, c, cells)
    plane = jacobian_plane(plan, (sq, sa, sb, sc), coef)
    carry = sweep_start(plan, fx)
    stores = []
    for c in range(CHUNKS):
        coefs[c].wait()
        size = plan.z // CHUNKS
        carry = sweep(plan, plane, (out_w, out_h), fx, carry, c * size, size)
        rows = chunk_rows(plan, c)
        stores.append(copies.start(out.at[:, rows], out_back.at[:, rows]))
    if last:
        late.wait()
        groups = (tuple(base.at[i] for i in range(3)), (sq, v1, v2))
        fracs = (base_frac, frac_vec)
        rr, rw = block_sums(plan, groups, fracs, lambda r, w: (r * r, r * w), 2)
        share = safe_ratio(rw, rr)
        (uu,) = block_sums(plan, groups, fracs, lambda r, w: (jnp.square(w - share * r),), 1)
        r11 = jnp.sqrt(rr)
        put_lanes(stats, (r11, safe_ratio(rw, r11), jnp.sqrt(uu), share, uu))
    wait_all(stores)


def put_lanes(out, values):
    lane = lax.broadcasted_iota(jnp.int32, out.shape, 1)
    total = jnp.zeros(out.shape, F32)
    for j, value in enumerate(values):
        total = jnp.where(lane == j, value, total)
    out[...] = total


def jacobian_kernel(plan, last, *refs):
    n, m = len(plan.slots), len(plan.faces)
    refs = list(refs)
    take = lambda count: [refs.pop(0) for _ in range(count)]
    out_in, kb = take(2)
    fp, fs, fd, frac_volume, frac_vec = take(5)
    segment, column, weight, weight_back, own, got, own_vec, recv = take(8)
    own_faces, recv_faces = take(m), take(n)
    own_vec_faces, recv_vec_faces = take(m), take(n)
    if last:
        vec_in, base_in, base_frac, stats_in = take(4)
        (stats,) = take(1)
    else:
        out_back, frac_out = take(2)
        faces = take(m)
        pack, own_out = take(2)
    out, y_store, rates, sems, got_vec = take(5)
    fields = tuple(out.at[i] for i in range(3))
    copies = Copies(sems)
    load = copies.start(out_in, out)
    if last:
        vec, base, frac_out = take(3)
        late = [copies.start(vec_in, vec), copies.start(base_in, base)]

    unpack_pairs(plan, recv, got_vec)

    def pair_rates(weights, seg_values, seg_steps, cell_values, cell_steps):
        w0, h0, _, a0, b0, _ = mobility_steps(*seg_values, *seg_steps)
        w1, h1, _, a1, b1, _ = mobility_steps(*cell_values, *cell_steps)
        drop = seg_values[0] - cell_values[0]
        dq = seg_steps[0] - cell_steps[0]
        half = 0.5 * weights
        return (
            half * ((a0 + a1) * drop + (w0 + w1) * dq),
            half * ((b0 + b1) * drop + (h0 + h1) * dq),
        )

    rate_w, rate_h = pair_rates(
        weight_back[...],
        pair_values(plan, own, 0),
        pair_values(plan, own_vec, 0),
        pair_values(plan, got, 1),
        pair_values(plan, got_vec, 1),
    )
    values = (fp[...], fs[...], fd[...], frac_vec[0], frac_vec[1], frac_vec[2])
    _, _, _, mass_w, mass_h, frac_out[2] = cell_steps(*values)
    vol = frac_volume[...]
    frac_out[0] = vol * mass_w + scatter_segments(plan, rate_w, segment[...])
    frac_out[1] = vol * mass_h + scatter_segments(plan, rate_h, segment[...])
    rate_w, rate_h = pair_rates(
        weight[...],
        pair_values(plan, got, 0),
        pair_values(plan, got_vec, 0),
        pair_values(plan, own, 1),
        pair_values(plan, own_vec, 1),
    )
    rates[0 : plan.z, :] = rate_w
    rates[plan.z : 2 * plan.z, :] = rate_h

    found = merge_faces(plan, own_faces, recv_faces, 3)
    found_vec = merge_faces(plan, own_vec_faces, recv_vec_faces, 3)
    fluxes = []
    for i, ((axis, high, _, mine, theirs), steps) in enumerate(zip(found, found_vec)):
        fluxes.append(
            face_flux(vertical_sign(axis, high), kb[i], mine, theirs, steps[3], steps[4])
        )
    load.wait()
    add_faces(plan, found, fluxes, fields[:2], y_store)
    scatter_cells(plan, rates, column[...], fields[:2], y_store)
    if not last:
        store = copies.start(out, out_back)
        send_parts(plan, fields, frac_out, segment, column, faces, own_out, pack)
        store.wait()
        return
    wait_all(late)
    known = stats_in[0:1, :]
    lane1 = lax.broadcasted_iota(jnp.int32, (1, 128), 1)
    r11, r12, r22, share, uu = (
        jnp.sum(jnp.where(lane1 == j, known, 0.0), axis=1, keepdims=True) for j in range(5)
    )
    three = lambda ref: tuple(ref.at[i] for i in range(3))
    refs3 = (three(base), three(vec), fields)
    fracs3 = (base_frac, frac_vec, frac_out)
    rz, uz = block_sums(
        plan, refs3, fracs3, lambda r, w, v: (r * v, (w - share * r) * v), 2
    )
    along_r, along_u = safe_ratio(rz, r11 * r11), safe_ratio(uz, uu)
    (vv,) = block_sums(
        plan,
        refs3,
        fracs3,
        lambda r, w, v: (jnp.square(v - along_r * r - along_u * (w - share * r)),),
        1,
    )
    put_lanes(stats, (r11, r12, r22, safe_ratio(rz, r11), safe_ratio(uz, r22), jnp.sqrt(vv)))


def step_kernel(plan, stats, res_in, frac_res, vec_in, frac_vec, out, frac_step, *scratch):
    res, vec, step, sems = scratch
    copies = Copies(sems)
    loads = [
        [copies.start(a.at[f], b.at[f]) for a, b in ((res_in, res), (vec_in, vec))]
        for f in range(3)
    ]
    table = stats[...]
    lane = lax.broadcasted_iota(jnp.int32, table.shape, 1)
    r11, r12, r22, r13, r23, r33 = (
        jnp.sum(jnp.where(lane == j, table, 0.0), axis=1, keepdims=True) for j in range(6)
    )
    add = lambda v: jnp.sum(v, axis=0, keepdims=True)
    norm2 = add(r11 * r11) + EPS
    norm = jnp.sqrt(norm2)
    c11 = add(r11 * r12) / norm2
    left1, left2 = r12 - c11 * r11, r22
    c21 = jnp.sqrt(add(left1 * left1 + left2 * left2) / norm2 + EPS)
    scale = 1.0 / (norm * c21)
    second1, second2 = -scale * left1, -scale * left2
    image1 = -scale * (r13 - c11 * r12)
    image2 = -scale * (r23 - c11 * r22)
    image3 = -scale * r33
    first1 = -r11 / norm
    c12 = add(image1 * first1)
    c22 = add(image1 * second1 + image2 * second2)
    u1 = image1 - c12 * first1 - c22 * second1
    u2 = image2 - c22 * second2
    c32_2 = add(u1 * u1 + u2 * u2 + image3 * image3) + EPS
    rho = jnp.sqrt(c11 * c11 + c21 * c21)
    co, si = c11 / rho, c21 / rho
    t1 = co * c12 + si * c22
    t2 = co * c22 - si * c12
    y2 = -si * norm * t2 / (t2 * t2 + c32_2)
    y1 = (co * norm - t1 * y2) / rho
    on_vec = -y2 * scale
    on_res = -y1 / norm - c11 * on_vec
    stores = []
    for f in range(3):
        wait_all(loads[f])

        def body(z, carry):
            here = plane_rows(plan, z)
            step[f, here, :] = on_res * res[f, here, :] + on_vec * vec[f, here, :]
            return carry

        lax.fori_loop(0, plan.z, body, 0, unroll=4)
        stores.append(copies.start(step.at[f], out.at[f]))
    for f in range(3):
        frac_step[f] = on_res * frac_res[f] + on_vec * frac_vec[f]
    wait_all(stores)


def call(kernel, out_shapes, args, scratch, copies, more=(), smem=(), far=(), far_out=(), work=0):
    place = lambda i: pltpu.SMEM if i in smem else pl.ANY if i in far else pltpu.VMEM
    cost = pl.CostEstimate(flops=work, bytes_accessed=work, transcendentals=0) if work else None
    return pl.pallas_call(
        kernel,
        out_shape=[jax.ShapeDtypeStruct(shape, F32) for shape in out_shapes],
        in_specs=[pl.BlockSpec(memory_space=place(i)) for i in range(len(args))],
        out_specs=[
            pl.BlockSpec(memory_space=pl.ANY if i in far_out else pltpu.VMEM)
            for i in range(len(out_shapes))
        ],
        scratch_shapes=[pltpu.VMEM(shape, F32) for shape in scratch]
        + [pltpu.SemaphoreType.DMA((copies,))]
        + [pltpu.VMEM(shape, F32) for shape in more],
        compiler_params=pltpu.CompilerParams(vmem_limit_bytes=56 << 20),
        cost_estimate=cost,
    )(*args)


def on_device(mesh_shape, *args):
    (
        pressure,
        saturation,
        dissolved,
        old_water,
        old_hydrogen,
        pore_volume,
        permeability,
        frac_pressure,
        frac_saturation,
        frac_dissolved,
        frac_old_water,
        frac_old_hydrogen,
        frac_volume,
        pair_segment,
        pair_column,
        pair_kind,
        pair_count,
        transfer_table,
    ) = args
    cap = pair_column.shape[1] // pair_count.shape[1]
    plan = Plan(mesh_shape, pressure, frac_pressure, pair_column, cap)
    slots = len(plan.slots)
    devices = plan.sizes["gx"] * plan.sizes["gy"] * plan.sizes["gz"]
    flat = lambda a: a.reshape(plan.rows, plan.y)
    p, s, d, k = (flat(a) for a in (pressure, saturation, dissolved, permeability))
    volume = flat(pore_volume)
    field = (plan.rows, plan.y)
    padded = (plan.rows + plan.x + 8, plan.y)
    pair_shape = (6 * plan.z, plan.pairs)
    face_count = len(plan.faces)
    sweep_scratch = (2 * UNROLL, plan.x + 8, plan.y)
    y_scratch = (2, plan.x, plan.y)
    rate_scratch = (2 * plan.z, plan.pairs)
    coef_shape = (11,) + field
    three = (3,) + field
    frac_shape = (3, plan.z, plan.seg)
    inner_work = 16 << 20

    def exchange(faces, pack):
        got = lax.all_to_all(pack, PLANE, 0, 0, tiled=True)
        moved = [
            lax.ppermute(faces[spot], axis, swap_pairs(plan.sizes[axis], odd))
            for (axis, odd), spot in zip(plan.slots, plan.slot_face)
        ]
        return moved, got

    outs = call(
        functools.partial(first_kernel, plan),
        [(4, 32, 128)] * face_count
        + [(plan.peers, plan.pack_rows + 8, 128), pair_shape, (1, plan.pairs)],
        [p, s, d, k, frac_pressure, frac_saturation, frac_dissolved]
        + [pair_segment, pair_column, pair_kind, pair_count, transfer_table],
        scratch=[(4,) + field],
        copies=4,
        smem=(10, 11),
        far=(0, 1, 2, 3),
    )
    faces, (pack, own, weight) = outs[:face_count], outs[face_count:]
    recv_faces, recv = exchange(faces, pack)
    res, coef = call(
        functools.partial(residual_inner, plan),
        [three, coef_shape],
        [p, s, d, flat(old_water), flat(old_hydrogen), volume, k, weight],
        scratch=[padded] * 5 + [(5,) + field, three, coef_shape, sweep_scratch],
        copies=9 * CHUNKS,
        far=range(7),
        far_out=(0, 1),
        work=inner_work,
    )
    outs = call(
        functools.partial(residual_kernel, plan),
        [three, frac_shape, (face_count, 32, 128)]
        + [(3, 32, 128)] * face_count
        + [(plan.peers, plan.pack_rows, 128), pair_shape, pair_shape, (1, plan.pairs)],
        [res, frac_pressure, frac_saturation, frac_dissolved]
        + [frac_old_water, frac_old_hydrogen, frac_volume]
        + [pair_segment, pair_column, weight, own, recv]
        + list(faces)
        + list(recv_faces),
        scratch=[three, y_scratch, rate_scratch],
        copies=2,
        far=(0,),
        far_out=(0,),
    )
    res, frac_res, kb = outs[:3]
    vec_faces = outs[3 : 3 + face_count]
    pack, own_vec, got, weight_back = outs[3 + face_count :]

    def image(vec, frac_vec, vec_faces, pack, own_vec, base):
        recv_vec_faces, recv_vec = exchange(vec_faces, pack)
        last = base is not None
        outs = call(
            functools.partial(jacobian_inner, plan, last),
            [three] + ([(8, 128)] if last else []),
            [p, s, d, volume, vec, coef] + ([*base, frac_vec] if last else []),
            scratch=[padded] * 4 + [(6,) + field, coef_shape, three, sweep_scratch],
            more=[three] if last else [],
            copies=9 * CHUNKS + 1,
            far=range(7 if last else 6),
            far_out=(0,),
            work=inner_work,
        )
        args = [outs[0], kb]
        args += [frac_pressure, frac_saturation, frac_dissolved, frac_volume, frac_vec]
        args += [pair_segment, pair_column, weight, weight_back, own, got, own_vec, recv_vec]
        args += list(faces) + list(recv_faces) + list(vec_faces) + list(recv_vec_faces)
        if last:
            far = (0, len(args), len(args) + 1)
            args += [vec, *base, outs[1]]
            shapes = [(devices, 128)]
        else:
            far = (0,)
            shapes = [three, frac_shape] + [(3, 32, 128)] * face_count
            shapes += [(plan.peers, plan.pack_rows, 128), pair_shape]
        return call(
            functools.partial(jacobian_kernel, plan, last),
            shapes,
            args,
            scratch=[three, y_scratch, rate_scratch],
            more=[pair_shape] + ([three, three, frac_shape] if last else []),
            copies=3,
            far=far,
            far_out=() if last else (0,),
        )

    outs = image(res, frac_res, vec_faces, pack, own_vec, None)
    vec, frac_vec = outs[:2]
    vec_faces = outs[2 : 2 + face_count]
    pack, own_vec = outs[2 + face_count :]
    (stats,) = image(vec, frac_vec, vec_faces, pack, own_vec, (res, frac_res))
    stats = lax.all_to_all(stats, ("gx", "gy", "gz"), 0, 0, tiled=True)
    step, frac_step = call(
        functools.partial(step_kernel, plan),
        [three, frac_shape],
        [stats, res, frac_res, vec, frac_vec],
        scratch=[three] * 3,
        copies=9,
        far=(1, 3),
        far_out=(0,),
    )
    shape = (3, plan.z, plan.x, plan.y)
    return step.reshape(shape), frac_step, res.reshape(shape), frac_res


def solution(mesh):
    grid = P("gz", "gx", "gy")
    segments = P("gz", PLANE)
    lists = P(PLANE, None)
    return jax.shard_map(
        functools.partial(on_device, dict(mesh.shape)),
        mesh=mesh,
        in_specs=(grid,) * 7 + (segments,) * 6 + (lists,) * 4 + (P(),),
        out_specs=(
            P(None, "gz", "gx", "gy"),
            P(None, "gz", PLANE),
            P(None, "gz", "gx", "gy"),
            P(None, "gz", PLANE),
        ),
        check_vma=False,
    )
```

time: 126 us -> 106 us (0.84)
  waiting for transfers between devices: 12.2 us -> 0.05 us
  Pallas kernels: 61.3 us -> 54.4 us
  starting transfers between devices: 38.6 us -> 37 us
    ppermute x15, waiting for transfers between devices: 11.5 us -> 0.04 us  [exchange(): lax.ppermute(faces[spot], axis, swap_pairs(plan.sizes[axis], odd))]
    pallas_call x5 -> x8, Pallas kernels: 61.3 us -> 54.4 us  [call(): pl.pallas_call(kernel, out_shape=[jax.ShapeDtypeStruct(shape, F32) for sh...]
    ppermute x15, starting transfers between devices: 21.7 us -> 20 us  [exchange(): lax.ppermute(faces[spot], axis, swap_pairs(plan.sizes[axis], odd))]
  transfers between devices with their start and end apart: 18 -> 18, of which waited for: 9 -> 0; matrix products, arithmetic and copies ran while one was open for 0% -> 0% of each run, Pallas kernels for 0% -> 21%
where the time goes in v2:
time: 106 us; the launch traced here: 105 us
  Pallas kernels  54.4 us (51%)
  starting transfers between devices  37 us (35%)
  blocking collectives  10.4 us (10%)
  local copies, waits for them, and re-layouts  2.11 us (2%)
    pallas_call x8, Pallas kernels, call(): pl.pallas_call(kernel, out_shape=[jax.ShapeDtypeStruct(shape, F32) for sh...  54.4 us
    ppermute x15, starting transfers between devices, exchange(): lax.ppermute(faces[spot], axis, swap_pairs(plan.sizes[axis], odd))  20 us
    all_to_all x3, starting transfers between devices, exchange(): got = lax.all_to_all(pack, PLANE, 0, 0, tiled=True)  17 us
    all_to_all x1, blocking collectives, on_device(): stats = lax.all_to_all(stats, ('gx', 'gy', 'gz'), 0, 0, tiled=True)  10.4 us
  transfers between devices with their start and end apart: 18, of which 0 were waited for; matrix products, arithmetic and copies ran while one was open for 0% of the time, Pallas kernels for 21%

profile of v2, /device:TPU:0, one launch (start us, length us, event | category | flops | bytes accessed | tf_op | source)
XLA Modules:
  0.0 104.9 jit_solution(3523383456646648126)
XLA Ops:
  0.6 5.8 %shard_map.201 = (f32[4,32,128]{2,1,0:T(8,128)}, f32[4,32,128]{2,1,0:T(8,128)}, f32[4,32,128]{2,1,0:T(8,128)}, f32[4,32,128]{2,1,0:T(8,128)}, f32[16,32,128]{2,1...) custom-call(f32[1024,128]{1,0:T(8,128)} %bitcast.14, f32[1024,128]{1,0:T(8,128)} %bitcast.18, f32[1024,128]{1,0:T(8,128)} %bitcast.22, ...), custom_call_target="tpu_custom_call" | custom-call | tf_op jit(solution)/shard_map/pallas_call | solution.py:898
  6.4 8.4 %all-to-all-start = ((f32[16,32,128]{2,1,0:T(8,128)}), f32[16,32,128]{2,1,0:T(8,128)S(1)}, u32[]{:S(2)}, u32[]{:S(2)}) async-start(f32[16,32,128]{2,1,0:T(8,128)} %get-tuple-element.39), calls=%async_computation | async-start | bytes 524288 | tf_op jit(solution)/shard_map/all_to_all | solution.py:955
  14.8 1.9 %collective-permute-start = (f32[4,32,128]{2,1,0:T(8,128)}, f32[4,32,128]{2,1,0:T(8,128)S(1)}, u32[]{:S(2)}, u32[]{:S(2)}) collective-permute-start(f32[4,32,128]{2,1,0:T(8,128)} %get-tuple-element.40.refs_12_.refs_15_), channel_id=1, source_target_pairs={{0,8},{8,0},{16,24},{24,16},{1,9},{9,1},{17,25},{25,17},{2,10},{10... | collective-permute-start | bytes 196616 | tf_op jit(solution)/shard_map/ppermute | solution.py:957
  16.7 1.5 %collective-permute-start.1 = (f32[4,32,128]{2,1,0:T(8,128)}, f32[4,32,128]{2,1,0:T(8,128)S(1)}, u32[]{:S(2)}, u32[]{:S(2)}) collective-permute-start(f32[4,32,128]{2,1,0:T(8,128)} %get-tuple-element.41.refs_13_.refs_16_), channel_id=1, source_target_pairs={{0,24},{8,16},{16,8},{24,0},{1,25},{9,17},{17,9},{25,1},{2,26},{10... | collective-permute-start | bytes 196616 | tf_op jit(solution)/shard_map/ppermute | solution.py:957
  18.1 0.0 collective-permute-start.4
  18.1 3.3 %collective-permute-start.3 = (f32[4,32,128]{2,1,0:T(8,128)}, f32[4,32,128]{2,1,0:T(8,128)S(1)}, u32[]{:S(2)}, u32[]{:S(2)}) collective-permute-start(f32[4,32,128]{2,1,0:T(8,128)} %get-tuple-element.42.refs_14_.refs_17_), channel_id=1, source_target_pairs={{0,6},{2,4},{4,2},{6,0},{1,7},{3,5},{5,3},{7,1},{8,14},{10,12},{12... | collective-permute-start | bytes 196616 | tf_op jit(solution)/shard_map/ppermute | solution.py:957
  21.4 7.3 %shard_map.202 = (f32[3,1024,128]{2,1,0:T(8,128)}, f32[11,1024,128]{2,1,0:T(8,128)}) custom-call(f32[1024,128]{1,0:T(8,128)} %bitcast.15, f32[1024,128]{1,0:T(8,128)} %bitcast.19, f32[1024,128]{1,0:T(8,128)} %bitcast.23, f32[1024,128]{1,0:T(8,128)} %bitcast.31, f32[1024,128]{1,0:T(8,128)} %bitcast.32, f32[1024,128]{1,0:T(8,128)} %bitcast.26, ...), custom_call_target="tpu_custom_call" | custom-call | flops 16777216 | bytes 16777216 | tf_op jit(solution)/shard_map/pallas_call | solution.py:898
  28.8 0.0 collective-permute-done.refs_16_.refs_19_
  28.8 0.0 collective-permute-done.4.refs_20_.refs_23_
  28.8 0.0 collective-permute-done.3.refs_19_.refs_22_
  28.9 0.0 all-to-all-done.refs_11_
  28.9 0.5 copy-done.3
  29.4 0.0 copy-done.4
  29.4 0.0 copy-done.5
  29.5 0.0 copy-done.6
  29.5 0.0 copy-done.7
  29.5 0.1 copy-done
  29.6 8.1 %shard_map.203 = (f32[3,1024,128]{2,1,0:T(8,128)}, f32[3,32,256]{2,1,0:T(8,128)}, f32[4,32,128]{2,1,0:T(8,128)}, f32[3,32,128]{2,1,0:T(8,128)}, f32[3,32,128]{2,...) custom-call(f32[3,1024,128]{2,1,0:T(8,128)} %get-tuple-element.37.re, ...), custom_call_target="tpu_custom_call" | custom-call | tf_op jit(solution)/shard_map/pallas_call | solution.py:898
  37.7 4.3 %all-to-all-start.1 = ((f32[16,24,128]{2,1,0:T(8,128)}), f32[16,24,128]{2,1,0:T(8,128)S(1)}, u32[]{:S(2)}, u32[]{:S(2)}) async-start(f32[16,24,128]{2,1,0:T(8,128)} %get-tuple-element.51), calls=%async_computation.1 | async-start | bytes 393216 | tf_op jit(solution)/shard_map/all_to_all | solution.py:955
  42.0 1.9 %collective-permute-start.5 = (f32[3,32,128]{2,1,0:T(8,128)}, f32[3,32,128]{2,1,0:T(8,128)S(1)}, u32[]{:S(2)}, u32[]{:S(2)}) collective-permute-start(f32[3,32,128]{2,1,0:T(8,128)} %get-tuple-element.52.refs_24_), channel_id=1, source_target_pairs={{0,8},{8,0},{16,24},{24,16},{1,9},{9,1},{17,25},{25,17},{2,10},{10... | collective-permute-start | bytes 147464 | tf_op jit(solution)/shard_map/ppermute | solution.py:957
  44.0 1.5 %collective-permute-start.6 = (f32[3,32,128]{2,1,0:T(8,128)}, f32[3,32,128]{2,1,0:T(8,128)S(1)}, u32[]{:S(2)}, u32[]{:S(2)}) collective-permute-start(f32[3,32,128]{2,1,0:T(8,128)} %get-tuple-element.53.refs_25_), channel_id=1, source_target_pairs={{0,24},{8,16},{16,8},{24,0},{1,25},{9,17},{17,9},{25,1},{2,26},{10... | collective-permute-start | bytes 147464 | tf_op jit(solution)/shard_map/ppermute | solution.py:957
  45.4 0.0 collective-permute-start.9
  45.4 3.3 %collective-permute-start.8 = (f32[3,32,128]{2,1,0:T(8,128)}, f32[3,32,128]{2,1,0:T(8,128)S(1)}, u32[]{:S(2)}, u32[]{:S(2)}) collective-permute-start(f32[3,32,128]{2,1,0:T(8,128)} %get-tuple-element.54.refs_26_), channel_id=1, source_target_pairs={{0,6},{2,4},{4,2},{6,0},{1,7},{3,5},{5,3},{7,1},{8,14},{10,12},{12... | collective-permute-start | bytes 147464 | tf_op jit(solution)/shard_map/ppermute | solution.py:957
  48.7 0.0 collective-permute-start.7
  48.7 6.4 %shard_map.204.refs_0_ = f32[3,1024,128]{2,1,0:T(8,128)} custom-call(f32[1024,128]{1,0:T(8,128)} %bitcast.16, f32[1024,128]{1,0:T(8,128)} %bitcast.20, f32[1024,128]{1,0:T(8,128)} %bitcast.24, f32[1024,128]{1,0:T(8,128)} %bitcast.27, f32[3,1024,128]{2,1,0:T(8,128)} %get-tuple-element.44.refs_4_.refs_6_.refs_34_.res_in, ...), custom_call_target="tpu_custom_call" | custom-call | flops 16777216 | bytes 16777216 | tf_op jit(solution)/shard_map/pallas_call | solution.py:898
  55.1 0.0 collective-permute-done.5.refs_28_
  55.2 0.0 collective-permute-done.9.refs_32_
  55.3 0.5 copy-done.11
  55.8 0.0 copy-done.13
  55.8 0.0 copy-done.15
  55.8 0.0 copy-done.16
  55.8 0.0 copy-done.17
  55.9 0.1 copy-done.1
  56.0 8.1 %shard_map.205 = (f32[3,1024,128]{2,1,0:T(8,128)}, f32[3,32,256]{2,1,0:T(8,128)}, f32[3,32,128]{2,1,0:T(8,128)}, f32[3,32,128]{2,1,0:T(8,128)}, f32[3,32,128]{2,...) custom-call(f32[3,1024,128]{2,1,0:T(8,128)} %shard_map.204.refs_0_, ...), custom_call_target="tpu_custom_call" | custom-call | tf_op jit(solution)/shard_map/pallas_call | solution.py:898
  64.1 4.3 %all-to-all-start.2 = ((f32[16,24,128]{2,1,0:T(8,128)}), f32[16,24,128]{2,1,0:T(8,128)S(1)}, u32[]{:S(2)}, u32[]{:S(2)}) async-start(f32[16,24,128]{2,1,0:T(8,128)} %get-tuple-element.60), calls=%async_computation.2 | async-start | bytes 393216 | tf_op jit(solution)/shard_map/all_to_all | solution.py:955
  68.4 1.9 %collective-permute-start.10 = (f32[3,32,128]{2,1,0:T(8,128)}, f32[3,32,128]{2,1,0:T(8,128)S(1)}, u32[]{:S(2)}, u32[]{:S(2)}) collective-permute-start(f32[3,32,128]{2,1,0:T(8,128)} %get-tuple-element.61.refs_24_), channel_id=1, source_target_pairs={{0,8},{8,0},{16,24},{24,16},{1,9},{9,1},{17,25},{25,17},{2,10},{10... | collective-permute-start | bytes 147464 | tf_op jit(solution)/shard_map/ppermute | solution.py:957
  70.3 1.5 %collective-permute-start.11 = (f32[3,32,128]{2,1,0:T(8,128)}, f32[3,32,128]{2,1,0:T(8,128)S(1)}, u32[]{:S(2)}, u32[]{:S(2)}) collective-permute-start(f32[3,32,128]{2,1,0:T(8,128)} %get-tuple-element.62.refs_25_), channel_id=1, source_target_pairs={{0,24},{8,16},{16,8},{24,0},{1,25},{9,17},{17,9},{25,1},{2,26},{10... | collective-permute-start | bytes 147464 | tf_op jit(solution)/shard_map/ppermute | solution.py:957
  71.8 3.3 %collective-permute-start.13 = (f32[3,32,128]{2,1,0:T(8,128)}, f32[3,32,128]{2,1,0:T(8,128)S(1)}, u32[]{:S(2)}, u32[]{:S(2)}) collective-permute-start(f32[3,32,128]{2,1,0:T(8,128)} %get-tuple-element.63.refs_26_), channel_id=1, source_target_pairs={{0,6},{2,4},{4,2},{6,0},{1,7},{3,5},{5,3},{7,1},{8,14},{10,12},{12... | collective-permute-start | bytes 147464 | tf_op jit(solution)/shard_map/ppermute | solution.py:957
  75.0 8.0 %shard_map.206 = (f32[3,1024,128]{2,1,0:T(8,128)}, f32[8,128]{1,0:T(8,128)}) custom-call(f32[1024,128]{1,0:T(8,128)} %bitcast.17, f32[1024,128]{1,0:T(8,128)} %bitcast.21, f32[1024,128]{1,0:T(8,128)} %bitcast.25, f32[1024,128]{1,0:T(8,128)} %bitcast.28, f32[3,1024,128]{2,1,0:T(8,128)} %get-tuple-element.56.refs_4_.refs_33_.vec_in, ...), custom_call_target="tpu_custom_call" | custom-call | flops 16777216 | bytes 16777216 | tf_op jit(solution)/shard_map/pallas_call | solution.py:898
  83.1 0.5 copy-done.8
  83.6 0.0 copy-done.9
  83.7 0.0 copy-done.10
  83.7 0.0 copy-done.12
  83.7 0.0 copy-done.14
  83.8 0.1 copy-done.2
  83.8 6.3 %shard_map.207 = f32[32,128]{1,0:T(8,128)} custom-call(f32[3,1024,128]{2,1,0:T(8,128)} %get-tuple-element.58.refs_0_, f32[4,32,128]{2,1,0:T(8,128)} %get-tuple-element.46.refs_1_, f32[32,256]{1,0:T(8,128)} %refs_2_.5, f32[32,256]{1,0:T(8,128)} %refs_3_.5, f32[32,256]{1,0:T(8,128)} %refs_4_.7, f32[32,256]{1,0:T(8,128)} %refs_5_.7, ...), custom_call_target="tpu_custom_call" | custom-call | tf_op jit(solution)/shard_map/pallas_call | solution.py:898
  90.1 10.4 %all_to_all.26 = f32[32,1,128]{2,1,0:T(1,128)} all-to-all(f32[32,1,128]{2,1,0:T(1,128)} %bitcast.33), channel_id=1, replica_groups=mesh['gx'=4,'gy'=4,'gz'=2] {'gx','gy','gz'}, dimensions={0} | all-to-all | bytes 32768 | tf_op jit(solution)/shard_map/all_to_all | solution.py:1046
  100.6 4.4 %shard_map.208 = (f32[3,1024,128]{2,1,0:T(8,128)}, f32[3,32,256]{2,1,0:T(8,128)}) custom-call(f32[32,128]{1,0:T(8,128)} %bitcast.34, f32[3,1024,128]{2,1,0:T(8,128)} %get-tuple-element.44.refs_4_.refs_6_.refs_34_.res_in, f32[3,32,256]{2,1,0:T(8,128)} %get-tuple-element.35.refs_6_.refs_7_.refs_35_.frac_res, ...), custom_call_target="tpu_custom_call" | custom-call | tf_op jit(solution)/shard_map/pallas_call | solution.py:898
  (33 shorter events, 0.1 us)
Async XLA Ops:
  6.4 22.5 %all-to-all-start = ((f32[16,32,128]{2,1,0:T(8,128)}), f32[16,32,128]{2,1,0:T(8,128)S(1)}, u32[]{:S(2)}, u32[]{:S(2)}) async-start(f32[16,32,128]{2,1,0:T(8,128)} %get-tuple-element.39), calls=%async_computation | async-start | bytes 524288 | tf_op jit(solution)/shard_map/all_to_all | solution.py:955
  14.8 14.0 %collective-permute-start = (f32[4,32,128]{2,1,0:T(8,128)}, f32[4,32,128]{2,1,0:T(8,128)S(1)}, u32[]{:S(2)}, u32[]{:S(2)}) collective-permute-start(f32[4,32,128]{2,1,0:T(8,128)} %get-tuple-element.40.refs_12_.refs_15_), channel_id=1, source_target_pairs={{0,8},{8,0},{16,24},{24,16},{1,9},{9,1},{17,25},{25,17},{2,10},{10... | collective-permute-start | bytes 196616 | tf_op jit(solution)/shard_map/ppermute | solution.py:957
  16.7 12.1 %collective-permute-start.1 = (f32[4,32,128]{2,1,0:T(8,128)}, f32[4,32,128]{2,1,0:T(8,128)S(1)}, u32[]{:S(2)}, u32[]{:S(2)}) collective-permute-start(f32[4,32,128]{2,1,0:T(8,128)} %get-tuple-element.41.refs_13_.refs_16_), channel_id=1, source_target_pairs={{0,24},{8,16},{16,8},{24,0},{1,25},{9,17},{17,9},{25,1},{2,26},{10... | collective-permute-start | bytes 196616 | tf_op jit(solution)/shard_map/ppermute | solution.py:957
  18.1 10.7 %collective-permute-start.4 = (f32[4,32,128]{2,1,0:T(8,128)}, f32[4,32,128]{2,1,0:T(8,128)S(1)}, u32[]{:S(2)}, u32[]{:S(2)}) collective-permute-start(f32[4,32,128]{2,1,0:T(8,128)} %get-tuple-element.43.refs_15_.refs_18_), channel_id=1, source_target_pairs={{0,1},{1,0},{2,3},{3,2},{4,5},{5,4},{6,7},{7,6},{8,9},{9,8},{10,11... | collective-permute-start | bytes 196616 | tf_op jit(solution)/shard_map/ppermute | solution.py:957
  18.1 10.7 %collective-permute-start.3 = (f32[4,32,128]{2,1,0:T(8,128)}, f32[4,32,128]{2,1,0:T(8,128)S(1)}, u32[]{:S(2)}, u32[]{:S(2)}) collective-permute-start(f32[4,32,128]{2,1,0:T(8,128)} %get-tuple-element.42.refs_14_.refs_17_), channel_id=1, source_target_pairs={{0,6},{2,4},{4,2},{6,0},{1,7},{3,5},{5,3},{7,1},{8,14},{10,12},{12... | collective-permute-start | bytes 196616 | tf_op jit(solution)/shard_map/ppermute | solution.py:957
  21.4 7.4 %collective-permute-start.2 = (f32[4,32,128]{2,1,0:T(8,128)}, f32[4,32,128]{2,1,0:T(8,128)S(1)}, u32[]{:S(2)}, u32[]{:S(2)}) collective-permute-start(f32[4,32,128]{2,1,0:T(8,128)} %get-tuple-element.42.refs_14_.refs_17_), channel_id=1, source_target_pairs={{0,2},{2,0},{4,6},{6,4},{1,3},{3,1},{5,7},{7,5},{8,10},{10,8},{12,... | collective-permute-start | bytes 196616 | tf_op jit(solution)/shard_map/ppermute | solution.py:957
  28.8 0.6 copy-start.3
  28.8 0.6 copy-start.4
  28.8 0.7 copy-start.5
  28.8 0.7 copy-start.6
  28.9 0.6 copy-start.7
  28.9 0.7 copy-start
  37.7 17.5 %all-to-all-start.1 = ((f32[16,24,128]{2,1,0:T(8,128)}), f32[16,24,128]{2,1,0:T(8,128)S(1)}, u32[]{:S(2)}, u32[]{:S(2)}) async-start(f32[16,24,128]{2,1,0:T(8,128)} %get-tuple-element.51), calls=%async_computation.1 | async-start | bytes 393216 | tf_op jit(solution)/shard_map/all_to_all | solution.py:955
  42.0 13.1 %collective-permute-start.5 = (f32[3,32,128]{2,1,0:T(8,128)}, f32[3,32,128]{2,1,0:T(8,128)S(1)}, u32[]{:S(2)}, u32[]{:S(2)}) collective-permute-start(f32[3,32,128]{2,1,0:T(8,128)} %get-tuple-element.52.refs_24_), channel_id=1, source_target_pairs={{0,8},{8,0},{16,24},{24,16},{1,9},{9,1},{17,25},{25,17},{2,10},{10... | collective-permute-start | bytes 147464 | tf_op jit(solution)/shard_map/ppermute | solution.py:957
  44.0 11.2 %collective-permute-start.6 = (f32[3,32,128]{2,1,0:T(8,128)}, f32[3,32,128]{2,1,0:T(8,128)S(1)}, u32[]{:S(2)}, u32[]{:S(2)}) collective-permute-start(f32[3,32,128]{2,1,0:T(8,128)} %get-tuple-element.53.refs_25_), channel_id=1, source_target_pairs={{0,24},{8,16},{16,8},{24,0},{1,25},{9,17},{17,9},{25,1},{2,26},{10... | collective-permute-start | bytes 147464 | tf_op jit(solution)/shard_map/ppermute | solution.py:957
  45.4 9.8 %collective-permute-start.9 = (f32[3,32,128]{2,1,0:T(8,128)}, f32[3,32,128]{2,1,0:T(8,128)S(1)}, u32[]{:S(2)}, u32[]{:S(2)}) collective-permute-start(f32[3,32,128]{2,1,0:T(8,128)} %get-tuple-element.55.refs_27_), channel_id=1, source_target_pairs={{0,1},{1,0},{2,3},{3,2},{4,5},{5,4},{6,7},{7,6},{8,9},{9,8},{10,11... | collective-permute-start | bytes 147464 | tf_op jit(solution)/shard_map/ppermute | solution.py:957
  45.4 9.8 %collective-permute-start.8 = (f32[3,32,128]{2,1,0:T(8,128)}, f32[3,32,128]{2,1,0:T(8,128)S(1)}, u32[]{:S(2)}, u32[]{:S(2)}) collective-permute-start(f32[3,32,128]{2,1,0:T(8,128)} %get-tuple-element.54.refs_26_), channel_id=1, source_target_pairs={{0,6},{2,4},{4,2},{6,0},{1,7},{3,5},{5,3},{7,1},{8,14},{10,12},{12... | collective-permute-start | bytes 147464 | tf_op jit(solution)/shard_map/ppermute | solution.py:957
  48.7 6.5 %collective-permute-start.7 = (f32[3,32,128]{2,1,0:T(8,128)}, f32[3,32,128]{2,1,0:T(8,128)S(1)}, u32[]{:S(2)}, u32[]{:S(2)}) collective-permute-start(f32[3,32,128]{2,1,0:T(8,128)} %get-tuple-element.54.refs_26_), channel_id=1, source_target_pairs={{0,2},{2,0},{4,6},{6,4},{1,3},{3,1},{5,7},{7,5},{8,10},{10,8},{12,... | collective-permute-start | bytes 147464 | tf_op jit(solution)/shard_map/ppermute | solution.py:957
  55.2 0.6 copy-start.11
  55.2 0.6 copy-start.13
  55.2 0.6 copy-start.15
  55.2 0.6 copy-start.16
  55.2 0.6 copy-start.17
  55.3 0.7 copy-start.1
  64.1 19.1 %all-to-all-start.2 = ((f32[16,24,128]{2,1,0:T(8,128)}), f32[16,24,128]{2,1,0:T(8,128)S(1)}, u32[]{:S(2)}, u32[]{:S(2)}) async-start(f32[16,24,128]{2,1,0:T(8,128)} %get-tuple-element.60), calls=%async_computation.2 | async-start | bytes 393216 | tf_op jit(solution)/shard_map/all_to_all | solution.py:955
  68.4 14.6 %collective-permute-start.10 = (f32[3,32,128]{2,1,0:T(8,128)}, f32[3,32,128]{2,1,0:T(8,128)S(1)}, u32[]{:S(2)}, u32[]{:S(2)}) collective-permute-start(f32[3,32,128]{2,1,0:T(8,128)} %get-tuple-element.61.refs_24_), channel_id=1, source_target_pairs={{0,8},{8,0},{16,24},{24,16},{1,9},{9,1},{17,25},{25,17},{2,10},{10... | collective-permute-start | bytes 147464 | tf_op jit(solution)/shard_map/ppermute | solution.py:957
  70.3 12.7 %collective-permute-start.11 = (f32[3,32,128]{2,1,0:T(8,128)}, f32[3,32,128]{2,1,0:T(8,128)S(1)}, u32[]{:S(2)}, u32[]{:S(2)}) collective-permute-start(f32[3,32,128]{2,1,0:T(8,128)} %get-tuple-element.62.refs_25_), channel_id=1, source_target_pairs={{0,24},{8,16},{16,8},{24,0},{1,25},{9,17},{17,9},{25,1},{2,26},{10... | collective-permute-start | bytes 147464 | tf_op jit(solution)/shard_map/ppermute | solution.py:957
  71.8 11.3 %collective-permute-start.14 = (f32[3,32,128]{2,1,0:T(8,128)}, f32[3,32,128]{2,1,0:T(8,128)S(1)}, u32[]{:S(2)}, u32[]{:S(2)}) collective-permute-start(f32[3,32,128]{2,1,0:T(8,128)} %get-tuple-element.64.refs_27_), channel_id=1, source_target_pairs={{0,1},{1,0},{2,3},{3,2},{4,5},{5,4},{6,7},{7,6},{8,9},{9,8},{10,11... | collective-permute-start | bytes 147464 | tf_op jit(solution)/shard_map/ppermute | solution.py:957
  71.8 11.3 %collective-permute-start.13 = (f32[3,32,128]{2,1,0:T(8,128)}, f32[3,32,128]{2,1,0:T(8,128)S(1)}, u32[]{:S(2)}, u32[]{:S(2)}) collective-permute-start(f32[3,32,128]{2,1,0:T(8,128)} %get-tuple-element.63.refs_26_), channel_id=1, source_target_pairs={{0,6},{2,4},{4,2},{6,0},{1,7},{3,5},{5,3},{7,1},{8,14},{10,12},{12... | collective-permute-start | bytes 147464 | tf_op jit(solution)/shard_map/ppermute | solution.py:957
  75.0 8.1 %collective-permute-start.12 = (f32[3,32,128]{2,1,0:T(8,128)}, f32[3,32,128]{2,1,0:T(8,128)S(1)}, u32[]{:S(2)}, u32[]{:S(2)}) collective-permute-start(f32[3,32,128]{2,1,0:T(8,128)} %get-tuple-element.63.refs_26_), channel_id=1, source_target_pairs={{0,2},{2,0},{4,6},{6,4},{1,3},{3,1},{5,7},{7,5},{8,10},{10,8},{12,... | collective-permute-start | bytes 147464 | tf_op jit(solution)/shard_map/ppermute | solution.py:957
  83.0 0.6 copy-start.8
  83.1 0.6 copy-start.9
  83.1 0.6 copy-start.10
  83.1 0.6 copy-start.12
  83.1 0.6 copy-start.14
  83.1 0.7 copy-start.2

commit v3 on v2

--- a/solution.py
+++ b/solution.py
@@ -11,6 +11,7 @@
 BF16 = jnp.bfloat16
 EPS = 1e-06
 PLANE = ("gx", "gy")
+VMEM_BYTES = 67043328
 
 
 def swap_slots(mesh_shape):
@@ -102,12 +103,17 @@
     return high, (value - high.astype(F32)).astype(BF16)
 
 
-def split_dot(value, weights, dims):
-    high, low = halves(value)
-    dot = functools.partial(
-        lax.dot_general, dimension_numbers=(dims, ((), ())), preferred_element_type=F32
-    )
-    return dot(high, weights) + dot(low, weights)
+def twice(weights, axis):
+    return jnp.concatenate([weights, weights], axis=axis)
+
+
+def split_dot(value, weights, axis):
+    return lax.dot_general(
+        jnp.concatenate(halves(value), axis=1),
+        weights,
+        dimension_numbers=(((1,), (axis,)), ((), ())),
+        preferred_element_type=F32,
+    )
 
 
 def one_hot(size, index_row):
@@ -158,6 +164,7 @@
 
 def gather_cells(plan, fields, column, dst):
     wide, one_x = column_masks(plan, column)
+    wide = twice(wide, 0)
 
     def body(c, carry):
         for f, field in enumerate(fields):
@@ -167,7 +174,7 @@
                 value[:, i * plan.half : (i + 1) * plan.half].reshape(STEP * plan.half, plan.y)
                 for i in (0, 1)
             ]
-            got = split_dot(jnp.concatenate(sides, axis=1), wide, ((1,), (0,)))
+            got = split_dot(jnp.concatenate(sides, axis=1), wide, 0)
             got = got.reshape(STEP, plan.half, plan.pairs) * one_x[None]
             start = pl.multiple_of((3 + f) * plan.z + c * STEP, 8)
             dst[pl.ds(start, STEP), :] = jnp.sum(got, axis=1)
@@ -180,6 +187,7 @@
     wide, one_x = column_masks(plan, column)
     lane = lax.broadcasted_iota(jnp.int32, (plan.x, 128), 1)
     edge = (lane == 0) | (lane == 127)
+    wide = twice(wide, 1)
 
     def body(c, carry):
         for f, dst in enumerate(dsts):
@@ -187,7 +195,7 @@
             spread = jnp.concatenate(
                 [one_x * block[j : j + 1, :] for j in range(STEP)], axis=0
             )
-            got = split_dot(spread, wide, ((1,), (1,)))
+            got = split_dot(spread, wide, 1)
             for j in range(STEP):
                 z = c * STEP + j
                 here = plane_rows(plan, z)
@@ -205,14 +213,14 @@
 
 
 def gather_segments(plan, fields, segment, dst):
-    one_s = one_hot(plan.seg, segment).astype(BF16)
+    one_s = twice(one_hot(plan.seg, segment).astype(BF16), 0)
     for f, field in enumerate(fields):
-        dst[f * plan.z : (f + 1) * plan.z, :] = split_dot(field[...], one_s, ((1,), (0,)))
+        dst[f * plan.z : (f + 1) * plan.z, :] = split_dot(field[...], one_s, 0)
 
 
 def scatter_segments(plan, rate, segment):
-    one_s = one_hot(plan.seg, segment).astype(BF16)
-    return split_dot(rate, one_s, ((1,), (1,)))
+    one_s = twice(one_hot(plan.seg, segment).astype(BF16), 1)
+    return split_dot(rate, one_s, 1)
 
 
 def block_transpose(plan, tiles):
@@ -332,7 +340,7 @@
                 y_store[i] = flux
 
 
-UNROLL = 2
+UNROLL = 4
 
 
 def sweep(plan, plane, dsts, fx, carry, first, count):
@@ -453,6 +461,34 @@
 def wait_all(copies):
     for copy in copies:
         copy.wait()
+
+
+class Transfers:
+    def __init__(self, sems):
+        self.copies = Copies(sems)
+        self.loads, self.results, self.stores = {}, {}, []
+
+    def load(self, src, dst):
+        self.loads[id(dst)] = self.copies.start(src, dst)
+
+    def result(self, src, dst):
+        self.results[id(src)] = (src, dst)
+
+    def ready(self, *refs):
+        for ref in refs:
+            copy = self.loads.pop(id(ref), None)
+            if copy is not None:
+                copy.wait()
+
+    def done(self, *refs):
+        for ref in refs:
+            self.stores.append(self.copies.start(*self.results.pop(id(ref))))
+
+    def finish(self):
+        wait_all(list(self.loads.values()))
+        for src, dst in self.results.values():
+            self.stores.append(self.copies.start(src, dst))
+        wait_all(self.stores)
 
 
 def clear_tails(plan, refs):
@@ -490,7 +526,7 @@
     return conductance * water, conductance * hydrogen
 
 
-def first_kernel(plan, *refs):
+def first_kernel(plan, io, *refs):
     n = len(plan.faces)
     grids = refs[:4]
     fp, fs, fd, segment, column, kind, count, table = refs[4:12]
@@ -498,6 +534,7 @@
     local, sems = refs[15 + n :]
     copies = Copies(sems)
     loads = [copies.start(g, local.at[i]) for i, g in enumerate(grids)]
+    io.ready(fp, fs, fd, segment, kind, column)
     gather_segments(plan, (fp, fs, fd), segment[...], own)
     kinds = kind[...]
     picked = jnp.zeros(kinds.shape, F32)
@@ -519,6 +556,7 @@
     fields = tuple(local.at[i] for i in range(4))
     gather_cells(plan, fields[:3], column[...], own)
     pack_pairs(plan, own, pack)
+    io.done(own, pack, weight)
     wait_all(loads[3:])
     write_faces(plan, fields, faces)
 
@@ -528,7 +566,7 @@
     return tuple(ref[(first + f) * plan.z : (first + f + 1) * plan.z, :] for f in range(3))
 
 
-def residual_inner(plan, *refs):
+def residual_inner(plan, io, *refs):
     grids, (_, res_out, coef_out) = refs[:7], refs[7:10]
     sp, sk, sw, sh, sg, local, res, coef, fx, sems = refs[10:]
     copies = Copies(sems)
@@ -571,7 +609,7 @@
     wait_all(stores)
 
 
-def residual_kernel(plan, *refs):
+def residual_kernel(plan, io, *refs):
     n, m = len(plan.slots), len(plan.faces)
     refs = list(refs)
     take = lambda count: [refs.pop(0) for _ in range(count)]
@@ -587,6 +625,7 @@
     copies = Copies(sems)
     load = copies.start(res_in, res)
 
+    io.ready(recv)
     unpack_pairs(plan, recv, got)
     lane8 = lax.broadcasted_iota(jnp.int32, (8, 128), 1) // plan.cap
     for half in range(plan.pairs // 128):
@@ -596,6 +635,9 @@
             moved = pltpu.roll(tile, c * plan.cap, 1) if c else tile
             total = moved if total is None else jnp.where(lane8 == c, moved, total)
         weight_back[:, half * 128 : (half + 1) * 128] = total[0:1, :]
+    io.done(got, weight_back)
+    io.ready(own, weight, segment, column, fp, fs, fd)
+    io.ready(frac_water, frac_hydrogen, frac_volume)
 
     def pair_rates(weights, seg_values, cell_values):
         w0, h0, _ = mobilities(*seg_values)
@@ -614,10 +656,12 @@
         plan, rate_h, segment[...]
     )
     frac_res[2] = closure(fpv, fsv, fdv)
+    io.done(frac_res)
     rate_w, rate_h = pair_rates(weight[...], pair_values(plan, got, 0), pair_values(plan, own, 1))
     rates[0 : plan.z, :] = rate_w
     rates[plan.z : 2 * plan.z, :] = rate_h
 
+    io.ready(*own_faces, *recv_faces)
     found = merge_faces(plan, own_faces, recv_faces, 4)
     fluxes = []
     for i, (axis, high, valid, mine, theirs) in enumerate(found):
@@ -628,19 +672,22 @@
         )
         kb[i] = conductance
         fluxes.append(face_flux(vertical_sign(axis, high), conductance, mine[:3], theirs[:3]))
+    io.done(kb)
     load.wait()
     add_faces(plan, found, fluxes, fields[:2], y_store)
     scatter_cells(plan, rates, column[...], fields[:2], y_store)
     store = copies.start(res, res_out)
-    send_parts(plan, fields, frac_res, segment, column, faces, own_res, pack)
+    send_parts(plan, io, fields, frac_res, segment, column, faces, own_res, pack)
     store.wait()
 
 
-def send_parts(plan, fields, frac_fields, segment, column, faces, own, pack):
-    write_faces(plan, fields, faces)
+def send_parts(plan, io, fields, frac_fields, segment, column, faces, own, pack):
     gather_segments(plan, tuple(frac_fields.at[i] for i in range(3)), segment[...], own)
     gather_cells(plan, fields, column[...], own)
     pack_pairs(plan, own, pack)
+    io.done(own, pack)
+    write_faces(plan, fields, faces)
+    io.done(*faces)
 
 
 def total_of(value):
@@ -669,7 +716,7 @@
     return jnp.where(good, top / jnp.where(good, bottom, 1.0), 0.0)
 
 
-def jacobian_inner(plan, last, *refs):
+def jacobian_inner(plan, last, io, *refs):
     refs = list(refs)
     take = lambda count: [refs.pop(0) for _ in range(count)]
     grids = take(4)
@@ -724,6 +771,7 @@
         stores.append(copies.start(out.at[:, rows], out_back.at[:, rows]))
     if last:
         late.wait()
+        io.ready(base_frac, frac_vec)
         groups = (tuple(base.at[i] for i in range(3)), (sq, v1, v2))
         fracs = (base_frac, frac_vec)
         rr, rw = block_sums(plan, groups, fracs, lambda r, w: (r * r, r * w), 2)
@@ -742,7 +790,7 @@
     out[...] = total
 
 
-def jacobian_kernel(plan, last, *refs):
+def jacobian_kernel(plan, last, io, *refs):
     n, m = len(plan.slots), len(plan.faces)
     refs = list(refs)
     take = lambda count: [refs.pop(0) for _ in range(count)]
@@ -766,7 +814,10 @@
         vec, base, frac_out = take(3)
         late = [copies.start(vec_in, vec), copies.start(base_in, base)]
 
+    io.ready(recv)
     unpack_pairs(plan, recv, got_vec)
+    io.ready(own, got, own_vec, weight, weight_back, segment, column)
+    io.ready(fp, fs, fd, frac_volume, frac_vec)
 
     def pair_rates(weights, seg_values, seg_steps, cell_values, cell_steps):
         w0, h0, _, a0, b0, _ = mobility_steps(*seg_values, *seg_steps)
@@ -791,6 +842,8 @@
     vol = frac_volume[...]
     frac_out[0] = vol * mass_w + scatter_segments(plan, rate_w, segment[...])
     frac_out[1] = vol * mass_h + scatter_segments(plan, rate_h, segment[...])
+    if not last:
+        io.done(frac_out)
     rate_w, rate_h = pair_rates(
         weight[...],
         pair_values(plan, got, 0),
@@ -801,6 +854,7 @@
     rates[0 : plan.z, :] = rate_w
     rates[plan.z : 2 * plan.z, :] = rate_h
 
+    io.ready(*own_faces, *recv_faces, *own_vec_faces, *recv_vec_faces, kb)
     found = merge_faces(plan, own_faces, recv_faces, 3)
     found_vec = merge_faces(plan, own_vec_faces, recv_vec_faces, 3)
     fluxes = []
@@ -813,10 +867,11 @@
     scatter_cells(plan, rates, column[...], fields[:2], y_store)
     if not last:
         store = copies.start(out, out_back)
-        send_parts(plan, fields, frac_out, segment, column, faces, own_out, pack)
+        send_parts(plan, io, fields, frac_out, segment, column, faces, own_out, pack)
         store.wait()
         return
     wait_all(late)
+    io.ready(base_frac, stats_in)
     known = stats_in[0:1, :]
     lane1 = lax.broadcasted_iota(jnp.int32, (1, 128), 1)
     r11, r12, r22, share, uu = (
@@ -839,13 +894,14 @@
     put_lanes(stats, (r11, r12, r22, safe_ratio(rz, r11), safe_ratio(uz, r22), jnp.sqrt(vv)))
 
 
-def step_kernel(plan, stats, res_in, frac_res, vec_in, frac_vec, out, frac_step, *scratch):
+def step_kernel(plan, io, stats, res_in, frac_res, vec_in, frac_vec, out, frac_step, *scratch):
     res, vec, step, sems = scratch
     copies = Copies(sems)
     loads = [
         [copies.start(a.at[f], b.at[f]) for a, b in ((res_in, res), (vec_in, vec))]
         for f in range(3)
     ]
+    io.ready(stats)
     table = stats[...]
     lane = lax.broadcasted_iota(jnp.int32, table.shape, 1)
     r11, r12, r22, r13, r23, r33 = (
@@ -887,26 +943,60 @@
 
         lax.fori_loop(0, plan.z, body, 0, unroll=4)
         stores.append(copies.start(step.at[f], out.at[f]))
+    io.ready(frac_res, frac_vec)
     for f in range(3):
         frac_step[f] = on_res * frac_res[f] + on_vec * frac_vec[f]
     wait_all(stores)
 
 
-def call(kernel, out_shapes, args, scratch, copies, more=(), smem=(), far=(), far_out=(), work=0):
-    place = lambda i: pltpu.SMEM if i in smem else pl.ANY if i in far else pltpu.VMEM
+def call(
+    kernel,
+    out_shapes,
+    args,
+    scratch,
+    copies,
+    more=(),
+    smem=(),
+    far=(),
+    far_out=(),
+    first=(),
+    work=0,
+):
+    place = lambda i: pltpu.SMEM if i in smem else pl.ANY
     cost = pl.CostEstimate(flops=work, bytes_accessed=work, transcendentals=0) if work else None
+    near = [i for i in first + tuple(range(len(args))) if i not in smem and i not in far]
+    near = list(dict.fromkeys(near))
+    near_out = [i for i in range(len(out_shapes)) if i not in far_out]
+
+    def body(*refs):
+        refs = list(refs)
+        take = lambda count: [refs.pop(0) for _ in range(count)]
+        ins, outs = take(len(args)), take(len(out_shapes))
+        own = take(len(scratch) + 1 + len(more))
+        io = Transfers(refs[-1])
+        for i in near:
+            buffer = refs.pop(0)
+            io.load(ins[i], buffer)
+            ins[i] = buffer
+        for i in near_out:
+            buffer = refs.pop(0)
+            io.result(buffer, outs[i])
+            outs[i] = buffer
+        kernel(io, *ins, *outs, *own)
+        io.finish()
+
     return pl.pallas_call(
-        kernel,
+        body,
         out_shape=[jax.ShapeDtypeStruct(shape, F32) for shape in out_shapes],
         in_specs=[pl.BlockSpec(memory_space=place(i)) for i in range(len(args))],
-        out_specs=[
-            pl.BlockSpec(memory_space=pl.ANY if i in far_out else pltpu.VMEM)
-            for i in range(len(out_shapes))
-        ],
+        out_specs=[pl.BlockSpec(memory_space=pl.ANY)] * len(out_shapes),
         scratch_shapes=[pltpu.VMEM(shape, F32) for shape in scratch]
         + [pltpu.SemaphoreType.DMA((copies,))]
-        + [pltpu.VMEM(shape, F32) for shape in more],
-        compiler_params=pltpu.CompilerParams(vmem_limit_bytes=56 << 20),
+        + [pltpu.VMEM(shape, F32) for shape in more]
+        + [pltpu.VMEM(args[i].shape, args[i].dtype) for i in near]
+        + [pltpu.VMEM(out_shapes[i], F32) for i in near_out]
+        + [pltpu.SemaphoreType.DMA((len(near) + len(near_out) + 1,))],
+        compiler_params=pltpu.CompilerParams(vmem_limit_bytes=VMEM_BYTES),
         cost_estimate=cost,
     )(*args)
 
@@ -996,6 +1086,7 @@
         copies=2,
         far=(0,),
         far_out=(0,),
+        first=(11, 10, 9),
     )
     res, frac_res, kb = outs[:3]
     vec_faces = outs[3 : 3 + face_count]
@@ -1036,6 +1127,7 @@
             copies=3,
             far=far,
             far_out=() if last else (0,),
+            first=(14, 11, 12, 13),
         )
 
     outs = image(res, frac_res, vec_faces, pack, own_vec, None)

time: 106 us -> 96 us (0.906)
  Pallas kernels: 54.4 us -> 47.2 us
  local copies, waits for them, and re-layouts: 2.11 us -> 0 us
    pallas_call x8, Pallas kernels: 54.4 us -> 47.2 us  [call(): pl.pallas_call(body, out_shape=[jax.ShapeDtypeStruct(shape, F32) for shap...]
    unnamed x36 -> x0, local copies, waits for them, and re-layouts: 2.11 us -> none
  transfers between devices with their start and end apart: 18 -> 18, of which waited for: 0 -> 0; matrix products, arithmetic and copies ran while one was open for 0% -> 0% of each run, Pallas kernels for 21% -> 19%
where the time goes in v3:
time: 96 us; the launch traced here: 95.5 us
  Pallas kernels  47.2 us (49%)
  starting transfers between devices  37 us (39%)
  blocking collectives  10.4 us (11%)
    pallas_call x8, Pallas kernels, call(): pl.pallas_call(body, out_shape=[jax.ShapeDtypeStruct(shape, F32) for shap...  47.2 us
    ppermute x15, starting transfers between devices, exchange(): lax.ppermute(faces[spot], axis, swap_pairs(plan.sizes[axis], odd))  19.8 us
    all_to_all x3, starting transfers between devices, exchange(): got = lax.all_to_all(pack, PLANE, 0, 0, tiled=True)  17.1 us
    all_to_all x1, blocking collectives, on_device(): stats = lax.all_to_all(stats, ('gx', 'gy', 'gz'), 0, 0, tiled=True)  10.4 us
  transfers between devices with their start and end apart: 18, of which 0 were waited for; matrix products, arithmetic and copies ran while one was open for 0% of the time, Pallas kernels for 19%

profile of v3, /device:TPU:0, one launch (start us, length us, event | category | flops | bytes accessed | tf_op | source)
XLA Modules:
  0.0 95.5 jit_solution(10558724852445252913)
XLA Ops:
  0.6 5.7 %shard_map.201 = (f32[4,32,128]{2,1,0:T(8,128)}, f32[4,32,128]{2,1,0:T(8,128)}, f32[4,32,128]{2,1,0:T(8,128)}, f32[4,32,128]{2,1,0:T(8,128)}, f32[16,32,128]{2,1...) custom-call(f32[1024,128]{1,0:T(8,128)} %bitcast.14, f32[1024,128]{1,0:T(8,128)} %bitcast.18, f32[1024,128]{1,0:T(8,128)} %bitcast.22, ...), custom_call_target="tpu_custom_call" | custom-call | tf_op jit(solution)/shard_map/pallas_call | solution.py:988
  6.4 8.4 %all-to-all-start = ((f32[16,32,128]{2,1,0:T(8,128)}), f32[16,32,128]{2,1,0:T(8,128)}, u32[]{:S(2)}, u32[]{:S(2)}) async-start(f32[16,32,128]{2,1,0:T(8,128)} %get-tuple-element.39), calls=%async_computation | async-start | bytes 524288 | tf_op jit(solution)/shard_map/all_to_all | solution.py:1045
  14.8 1.9 %collective-permute-start = (f32[4,32,128]{2,1,0:T(8,128)}, f32[4,32,128]{2,1,0:T(8,128)}, u32[]{:S(2)}, u32[]{:S(2)}) collective-permute-start(f32[4,32,128]{2,1,0:T(8,128)} %get-tuple-element.40.refs_12_.refs_15_), channel_id=1, source_target_pairs={{0,8},{8,0},{16,24},{24,16},{1,9},{9,1},{17,25},{25,17},{2,10},{10... | collective-permute-start | bytes 196616 | tf_op jit(solution)/shard_map/ppermute | solution.py:1047
  16.6 1.5 %collective-permute-start.1 = (f32[4,32,128]{2,1,0:T(8,128)}, f32[4,32,128]{2,1,0:T(8,128)}, u32[]{:S(2)}, u32[]{:S(2)}) collective-permute-start(f32[4,32,128]{2,1,0:T(8,128)} %get-tuple-element.41.refs_13_.refs_16_), channel_id=1, source_target_pairs={{0,24},{8,16},{16,8},{24,0},{1,25},{9,17},{17,9},{25,1},{2,26},{10... | collective-permute-start | bytes 196616 | tf_op jit(solution)/shard_map/ppermute | solution.py:1047
  18.1 0.0 collective-permute-start.4
  18.1 3.3 %collective-permute-start.3 = (f32[4,32,128]{2,1,0:T(8,128)}, f32[4,32,128]{2,1,0:T(8,128)}, u32[]{:S(2)}, u32[]{:S(2)}) collective-permute-start(f32[4,32,128]{2,1,0:T(8,128)} %get-tuple-element.42.refs_14_.refs_17_), channel_id=1, source_target_pairs={{0,6},{2,4},{4,2},{6,0},{1,7},{3,5},{5,3},{7,1},{8,14},{10,12},{12... | collective-permute-start | bytes 196616 | tf_op jit(solution)/shard_map/ppermute | solution.py:1047
  21.4 0.0 collective-permute-start.2
  21.4 6.2 %shard_map.202 = (f32[3,1024,128]{2,1,0:T(8,128)}, f32[11,1024,128]{2,1,0:T(8,128)}) custom-call(f32[1024,128]{1,0:T(8,128)} %bitcast.15, f32[1024,128]{1,0:T(8,128)} %bitcast.19, f32[1024,128]{1,0:T(8,128)} %bitcast.23, f32[1024,128]{1,0:T(8,128)} %bitcast.31, f32[1024,128]{1,0:T(8,128)} %bitcast.32, f32[1024,128]{1,0:T(8,128)} %bitcast.26, ...), custom_call_target="tpu_custom_call" | custom-call | flops 16777216 | bytes 16777216 | tf_op jit(solution)/shard_map/pallas_call | solution.py:988
  27.5 0.0 collective-permute-done.refs_16_.refs_19_
  27.5 0.0 collective-permute-done.1.refs_17_.refs_20_
  27.6 0.0 collective-permute-done.4.refs_20_.refs_23_
  27.6 0.0 collective-permute-done.3.refs_19_.refs_22_
  27.6 0.0 collective-permute-done.2.refs_18_.refs_21_
  27.6 0.0 all-to-all-done.refs_11_
  27.6 7.0 %shard_map.203 = (f32[3,1024,128]{2,1,0:T(8,128)}, f32[3,32,256]{2,1,0:T(8,128)}, f32[4,32,128]{2,1,0:T(8,128)}, f32[3,32,128]{2,1,0:T(8,128)}, f32[3,32,128]{2,...) custom-call(f32[3,1024,128]{2,1,0:T(8,128)} %get-tuple-element.37.re, ...), custom_call_target="tpu_custom_call" | custom-call | tf_op jit(solution)/shard_map/pallas_call | solution.py:988
  34.6 4.4 %all-to-all-start.1 = ((f32[16,24,128]{2,1,0:T(8,128)}), f32[16,24,128]{2,1,0:T(8,128)}, u32[]{:S(2)}, u32[]{:S(2)}) async-start(f32[16,24,128]{2,1,0:T(8,128)} %get-tuple-element.51), calls=%async_computation.1 | async-start | bytes 393216 | tf_op jit(solution)/shard_map/all_to_all | solution.py:1045
  39.0 1.9 %collective-permute-start.5 = (f32[3,32,128]{2,1,0:T(8,128)}, f32[3,32,128]{2,1,0:T(8,128)}, u32[]{:S(2)}, u32[]{:S(2)}) collective-permute-start(f32[3,32,128]{2,1,0:T(8,128)} %get-tuple-element.52.refs_24_), channel_id=1, source_target_pairs={{0,8},{8,0},{16,24},{24,16},{1,9},{9,1},{17,25},{25,17},{2,10},{10... | collective-permute-start | bytes 147464 | tf_op jit(solution)/shard_map/ppermute | solution.py:1047
  40.8 1.5 %collective-permute-start.6 = (f32[3,32,128]{2,1,0:T(8,128)}, f32[3,32,128]{2,1,0:T(8,128)}, u32[]{:S(2)}, u32[]{:S(2)}) collective-permute-start(f32[3,32,128]{2,1,0:T(8,128)} %get-tuple-element.53.refs_25_), channel_id=1, source_target_pairs={{0,24},{8,16},{16,8},{24,0},{1,25},{9,17},{17,9},{25,1},{2,26},{10... | collective-permute-start | bytes 147464 | tf_op jit(solution)/shard_map/ppermute | solution.py:1047
  42.3 0.0 collective-permute-start.9
  42.3 3.3 %collective-permute-start.8 = (f32[3,32,128]{2,1,0:T(8,128)}, f32[3,32,128]{2,1,0:T(8,128)}, u32[]{:S(2)}, u32[]{:S(2)}) collective-permute-start(f32[3,32,128]{2,1,0:T(8,128)} %get-tuple-element.54.refs_26_), channel_id=1, source_target_pairs={{0,6},{2,4},{4,2},{6,0},{1,7},{3,5},{5,3},{7,1},{8,14},{10,12},{12... | collective-permute-start | bytes 147464 | tf_op jit(solution)/shard_map/ppermute | solution.py:1047
  45.6 0.0 collective-permute-start.7
  45.6 5.4 %shard_map.204.refs_0_ = f32[3,1024,128]{2,1,0:T(8,128)} custom-call(f32[1024,128]{1,0:T(8,128)} %bitcast.16, f32[1024,128]{1,0:T(8,128)} %bitcast.20, f32[1024,128]{1,0:T(8,128)} %bitcast.24, f32[1024,128]{1,0:T(8,128)} %bitcast.27, f32[3,1024,128]{2,1,0:T(8,128)} %get-tuple-element.44.refs_4_.refs_6_.refs_34_.refs_1_, ...), custom_call_target="tpu_custom_call" | custom-call | flops 16777216 | bytes 16777216 | tf_op jit(solution)/shard_map/pallas_call | solution.py:988
  51.0 0.0 collective-permute-done.5.refs_28_
  51.0 0.0 collective-permute-done.6.refs_29_
  51.0 0.0 collective-permute-done.9.refs_32_
  51.0 0.0 collective-permute-done.8.refs_31_
  51.0 0.0 collective-permute-done.7.refs_30_
  51.1 0.0 all-to-all-done.1.refs_14_
  51.1 7.4 %shard_map.205 = (f32[3,1024,128]{2,1,0:T(8,128)}, f32[3,32,256]{2,1,0:T(8,128)}, f32[3,32,128]{2,1,0:T(8,128)}, f32[3,32,128]{2,1,0:T(8,128)}, f32[3,32,128]{2,...) custom-call(f32[3,1024,128]{2,1,0:T(8,128)} %shard_map.204.refs_0_, ...), custom_call_target="tpu_custom_call" | custom-call | tf_op jit(solution)/shard_map/pallas_call | solution.py:988
  58.4 4.4 %all-to-all-start.2 = ((f32[16,24,128]{2,1,0:T(8,128)}), f32[16,24,128]{2,1,0:T(8,128)}, u32[]{:S(2)}, u32[]{:S(2)}) async-start(f32[16,24,128]{2,1,0:T(8,128)} %get-tuple-element.60), calls=%async_computation.2 | async-start | bytes 393216 | tf_op jit(solution)/shard_map/all_to_all | solution.py:1045
  62.8 1.9 %collective-permute-start.10 = (f32[3,32,128]{2,1,0:T(8,128)}, f32[3,32,128]{2,1,0:T(8,128)}, u32[]{:S(2)}, u32[]{:S(2)}) collective-permute-start(f32[3,32,128]{2,1,0:T(8,128)} %get-tuple-element.61.refs_24_), channel_id=1, source_target_pairs={{0,8},{8,0},{16,24},{24,16},{1,9},{9,1},{17,25},{25,17},{2,10},{10... | collective-permute-start | bytes 147464 | tf_op jit(solution)/shard_map/ppermute | solution.py:1047
  64.7 1.5 %collective-permute-start.11 = (f32[3,32,128]{2,1,0:T(8,128)}, f32[3,32,128]{2,1,0:T(8,128)}, u32[]{:S(2)}, u32[]{:S(2)}) collective-permute-start(f32[3,32,128]{2,1,0:T(8,128)} %get-tuple-element.62.refs_25_), channel_id=1, source_target_pairs={{0,24},{8,16},{16,8},{24,0},{1,25},{9,17},{17,9},{25,1},{2,26},{10... | collective-permute-start | bytes 147464 | tf_op jit(solution)/shard_map/ppermute | solution.py:1047
  66.2 0.0 collective-permute-start.14
  66.2 3.3 %collective-permute-start.13 = (f32[3,32,128]{2,1,0:T(8,128)}, f32[3,32,128]{2,1,0:T(8,128)}, u32[]{:S(2)}, u32[]{:S(2)}) collective-permute-start(f32[3,32,128]{2,1,0:T(8,128)} %get-tuple-element.63.refs_26_), channel_id=1, source_target_pairs={{0,6},{2,4},{4,2},{6,0},{1,7},{3,5},{5,3},{7,1},{8,14},{10,12},{12... | collective-permute-start | bytes 147464 | tf_op jit(solution)/shard_map/ppermute | solution.py:1047
  69.4 0.0 collective-permute-start.12
  69.4 6.3 %shard_map.206 = (f32[3,1024,128]{2,1,0:T(8,128)}, f32[8,128]{1,0:T(8,128)}) custom-call(f32[1024,128]{1,0:T(8,128)} %bitcast.17, f32[1024,128]{1,0:T(8,128)} %bitcast.21, f32[1024,128]{1,0:T(8,128)} %bitcast.25, f32[1024,128]{1,0:T(8,128)} %bitcast.28, f32[3,1024,128]{2,1,0:T(8,128)} %get-tuple-element.56.refs_4_.refs_33_.refs_3_, ...), custom_call_target="tpu_custom_call" | custom-call | flops 16777216 | bytes 16777216 | tf_op jit(solution)/shard_map/pallas_call | solution.py:988
  75.7 0.0 collective-permute-done.10.refs_28_
  75.7 0.0 collective-permute-done.11.refs_29_
  75.7 0.0 collective-permute-done.14.refs_32_
  75.7 0.0 collective-permute-done.13.refs_31_
  75.7 0.0 collective-permute-done.12.refs_30_
  75.7 0.0 all-to-all-done.2.refs_14_
  75.8 5.8 %shard_map.207 = f32[32,128]{1,0:T(8,128)} custom-call(f32[3,1024,128]{2,1,0:T(8,128)} %get-tuple-element.58.refs_0_, f32[4,32,128]{2,1,0:T(8,128)} %get-tuple-element.46.refs_1_, f32[32,256]{1,0:T(8,128)} %refs_2_.5, f32[32,256]{1,0:T(8,128)} %refs_3_.5, f32[32,256]{1,0:T(8,128)} %refs_4_.7, f32[32,256]{1,0:T(8,128)} %refs_5_.7, ...), custom_call_target="tpu_custom_call" | custom-call | tf_op jit(solution)/shard_map/pallas_call | solution.py:988
  81.5 10.4 %all_to_all.26 = f32[32,1,128]{2,1,0:T(1,128)} all-to-all(f32[32,1,128]{2,1,0:T(1,128)} %bitcast.33), channel_id=1, replica_groups=mesh['gx'=4,'gy'=4,'gz'=2] {'gx','gy','gz'}, dimensions={0} | all-to-all | bytes 32768 | tf_op jit(solution)/shard_map/all_to_all | solution.py:1138
  92.0 3.5 %shard_map.208 = (f32[3,1024,128]{2,1,0:T(8,128)}, f32[3,32,256]{2,1,0:T(8,128)}) custom-call(f32[32,128]{1,0:T(8,128)} %bitcast.34, f32[3,1024,128]{2,1,0:T(8,128)} %get-tuple-element.44.refs_4_.refs_6_.refs_34_.refs_1_, f32[3,32,256]{2,1,0:T(8,128)} %get-tuple-element.35.refs_6_.refs_7_.refs_35_.refs_2_, ...), custom_call_target="tpu_custom_call" | custom-call | tf_op jit(solution)/shard_map/pallas_call | solution.py:988
Async XLA Ops:
  6.4 21.2 %all-to-all-start = ((f32[16,32,128]{2,1,0:T(8,128)}), f32[16,32,128]{2,1,0:T(8,128)}, u32[]{:S(2)}, u32[]{:S(2)}) async-start(f32[16,32,128]{2,1,0:T(8,128)} %get-tuple-element.39), calls=%async_computation | async-start | bytes 524288 | tf_op jit(solution)/shard_map/all_to_all | solution.py:1045
  14.8 12.8 %collective-permute-start = (f32[4,32,128]{2,1,0:T(8,128)}, f32[4,32,128]{2,1,0:T(8,128)}, u32[]{:S(2)}, u32[]{:S(2)}) collective-permute-start(f32[4,32,128]{2,1,0:T(8,128)} %get-tuple-element.40.refs_12_.refs_15_), channel_id=1, source_target_pairs={{0,8},{8,0},{16,24},{24,16},{1,9},{9,1},{17,25},{25,17},{2,10},{10... | collective-permute-start | bytes 196616 | tf_op jit(solution)/shard_map/ppermute | solution.py:1047
  16.6 10.9 %collective-permute-start.1 = (f32[4,32,128]{2,1,0:T(8,128)}, f32[4,32,128]{2,1,0:T(8,128)}, u32[]{:S(2)}, u32[]{:S(2)}) collective-permute-start(f32[4,32,128]{2,1,0:T(8,128)} %get-tuple-element.41.refs_13_.refs_16_), channel_id=1, source_target_pairs={{0,24},{8,16},{16,8},{24,0},{1,25},{9,17},{17,9},{25,1},{2,26},{10... | collective-permute-start | bytes 196616 | tf_op jit(solution)/shard_map/ppermute | solution.py:1047
  18.1 9.5 %collective-permute-start.4 = (f32[4,32,128]{2,1,0:T(8,128)}, f32[4,32,128]{2,1,0:T(8,128)}, u32[]{:S(2)}, u32[]{:S(2)}) collective-permute-start(f32[4,32,128]{2,1,0:T(8,128)} %get-tuple-element.43.refs_15_.refs_18_), channel_id=1, source_target_pairs={{0,1},{1,0},{2,3},{3,2},{4,5},{5,4},{6,7},{7,6},{8,9},{9,8},{10,11... | collective-permute-start | bytes 196616 | tf_op jit(solution)/shard_map/ppermute | solution.py:1047
  18.1 9.5 %collective-permute-start.3 = (f32[4,32,128]{2,1,0:T(8,128)}, f32[4,32,128]{2,1,0:T(8,128)}, u32[]{:S(2)}, u32[]{:S(2)}) collective-permute-start(f32[4,32,128]{2,1,0:T(8,128)} %get-tuple-element.42.refs_14_.refs_17_), channel_id=1, source_target_pairs={{0,6},{2,4},{4,2},{6,0},{1,7},{3,5},{5,3},{7,1},{8,14},{10,12},{12... | collective-permute-start | bytes 196616 | tf_op jit(solution)/shard_map/ppermute | solution.py:1047
  21.4 6.2 %collective-permute-start.2 = (f32[4,32,128]{2,1,0:T(8,128)}, f32[4,32,128]{2,1,0:T(8,128)}, u32[]{:S(2)}, u32[]{:S(2)}) collective-permute-start(f32[4,32,128]{2,1,0:T(8,128)} %get-tuple-element.42.refs_14_.refs_17_), channel_id=1, source_target_pairs={{0,2},{2,0},{4,6},{6,4},{1,3},{3,1},{5,7},{7,5},{8,10},{10,8},{12,... | collective-permute-start | bytes 196616 | tf_op jit(solution)/shard_map/ppermute | solution.py:1047
  34.6 16.5 %all-to-all-start.1 = ((f32[16,24,128]{2,1,0:T(8,128)}), f32[16,24,128]{2,1,0:T(8,128)}, u32[]{:S(2)}, u32[]{:S(2)}) async-start(f32[16,24,128]{2,1,0:T(8,128)} %get-tuple-element.51), calls=%async_computation.1 | async-start | bytes 393216 | tf_op jit(solution)/shard_map/all_to_all | solution.py:1045
  39.0 12.0 %collective-permute-start.5 = (f32[3,32,128]{2,1,0:T(8,128)}, f32[3,32,128]{2,1,0:T(8,128)}, u32[]{:S(2)}, u32[]{:S(2)}) collective-permute-start(f32[3,32,128]{2,1,0:T(8,128)} %get-tuple-element.52.refs_24_), channel_id=1, source_target_pairs={{0,8},{8,0},{16,24},{24,16},{1,9},{9,1},{17,25},{25,17},{2,10},{10... | collective-permute-start | bytes 147464 | tf_op jit(solution)/shard_map/ppermute | solution.py:1047
  40.8 10.2 %collective-permute-start.6 = (f32[3,32,128]{2,1,0:T(8,128)}, f32[3,32,128]{2,1,0:T(8,128)}, u32[]{:S(2)}, u32[]{:S(2)}) collective-permute-start(f32[3,32,128]{2,1,0:T(8,128)} %get-tuple-element.53.refs_25_), channel_id=1, source_target_pairs={{0,24},{8,16},{16,8},{24,0},{1,25},{9,17},{17,9},{25,1},{2,26},{10... | collective-permute-start | bytes 147464 | tf_op jit(solution)/shard_map/ppermute | solution.py:1047
  42.3 8.7 %collective-permute-start.9 = (f32[3,32,128]{2,1,0:T(8,128)}, f32[3,32,128]{2,1,0:T(8,128)}, u32[]{:S(2)}, u32[]{:S(2)}) collective-permute-start(f32[3,32,128]{2,1,0:T(8,128)} %get-tuple-element.55.refs_27_), channel_id=1, source_target_pairs={{0,1},{1,0},{2,3},{3,2},{4,5},{5,4},{6,7},{7,6},{8,9},{9,8},{10,11... | collective-permute-start | bytes 147464 | tf_op jit(solution)/shard_map/ppermute | solution.py:1047
  42.3 8.7 %collective-permute-start.8 = (f32[3,32,128]{2,1,0:T(8,128)}, f32[3,32,128]{2,1,0:T(8,128)}, u32[]{:S(2)}, u32[]{:S(2)}) collective-permute-start(f32[3,32,128]{2,1,0:T(8,128)} %get-tuple-element.54.refs_26_), channel_id=1, source_target_pairs={{0,6},{2,4},{4,2},{6,0},{1,7},{3,5},{5,3},{7,1},{8,14},{10,12},{12... | collective-permute-start | bytes 147464 | tf_op jit(solution)/shard_map/ppermute | solution.py:1047
  45.6 5.5 %collective-permute-start.7 = (f32[3,32,128]{2,1,0:T(8,128)}, f32[3,32,128]{2,1,0:T(8,128)}, u32[]{:S(2)}, u32[]{:S(2)}) collective-permute-start(f32[3,32,128]{2,1,0:T(8,128)} %get-tuple-element.54.refs_26_), channel_id=1, source_target_pairs={{0,2},{2,0},{4,6},{6,4},{1,3},{3,1},{5,7},{7,5},{8,10},{10,8},{12,... | collective-permute-start | bytes 147464 | tf_op jit(solution)/shard_map/ppermute | solution.py:1047
  58.4 17.3 %all-to-all-start.2 = ((f32[16,24,128]{2,1,0:T(8,128)}), f32[16,24,128]{2,1,0:T(8,128)}, u32[]{:S(2)}, u32[]{:S(2)}) async-start(f32[16,24,128]{2,1,0:T(8,128)} %get-tuple-element.60), calls=%async_computation.2 | async-start | bytes 393216 | tf_op jit(solution)/shard_map/all_to_all | solution.py:1045
  62.8 12.9 %collective-permute-start.10 = (f32[3,32,128]{2,1,0:T(8,128)}, f32[3,32,128]{2,1,0:T(8,128)}, u32[]{:S(2)}, u32[]{:S(2)}) collective-permute-start(f32[3,32,128]{2,1,0:T(8,128)} %get-tuple-element.61.refs_24_), channel_id=1, source_target_pairs={{0,8},{8,0},{16,24},{24,16},{1,9},{9,1},{17,25},{25,17},{2,10},{10... | collective-permute-start | bytes 147464 | tf_op jit(solution)/shard_map/ppermute | solution.py:1047
  64.7 11.0 %collective-permute-start.11 = (f32[3,32,128]{2,1,0:T(8,128)}, f32[3,32,128]{2,1,0:T(8,128)}, u32[]{:S(2)}, u32[]{:S(2)}) collective-permute-start(f32[3,32,128]{2,1,0:T(8,128)} %get-tuple-element.62.refs_25_), channel_id=1, source_target_pairs={{0,24},{8,16},{16,8},{24,0},{1,25},{9,17},{17,9},{25,1},{2,26},{10... | collective-permute-start | bytes 147464 | tf_op jit(solution)/shard_map/ppermute | solution.py:1047
  66.2 9.6 %collective-permute-start.14 = (f32[3,32,128]{2,1,0:T(8,128)}, f32[3,32,128]{2,1,0:T(8,128)}, u32[]{:S(2)}, u32[]{:S(2)}) collective-permute-start(f32[3,32,128]{2,1,0:T(8,128)} %get-tuple-element.64.refs_27_), channel_id=1, source_target_pairs={{0,1},{1,0},{2,3},{3,2},{4,5},{5,4},{6,7},{7,6},{8,9},{9,8},{10,11... | collective-permute-start | bytes 147464 | tf_op jit(solution)/shard_map/ppermute | solution.py:1047
  66.2 9.6 %collective-permute-start.13 = (f32[3,32,128]{2,1,0:T(8,128)}, f32[3,32,128]{2,1,0:T(8,128)}, u32[]{:S(2)}, u32[]{:S(2)}) collective-permute-start(f32[3,32,128]{2,1,0:T(8,128)} %get-tuple-element.63.refs_26_), channel_id=1, source_target_pairs={{0,6},{2,4},{4,2},{6,0},{1,7},{3,5},{5,3},{7,1},{8,14},{10,12},{12... | collective-permute-start | bytes 147464 | tf_op jit(solution)/shard_map/ppermute | solution.py:1047
  69.4 6.3 %collective-permute-start.12 = (f32[3,32,128]{2,1,0:T(8,128)}, f32[3,32,128]{2,1,0:T(8,128)}, u32[]{:S(2)}, u32[]{:S(2)}) collective-permute-start(f32[3,32,128]{2,1,0:T(8,128)} %get-tuple-element.63.refs_26_), channel_id=1, source_target_pairs={{0,2},{2,0},{4,6},{6,4},{1,3},{3,1},{5,7},{7,5},{8,10},{10,8},{12,... | collective-permute-start | bytes 147464 | tf_op jit(solution)/shard_map/ppermute | solution.py:1047

commit v4 on v3

--- a/solution.py
+++ b/solution.py
@@ -11,6 +11,7 @@
 BF16 = jnp.bfloat16
 EPS = 1e-06
 PLANE = ("gx", "gy")
+DEVICES = ("gx", "gy", "gz")
 VMEM_BYTES = 67043328
 
 
@@ -24,14 +25,20 @@
     return tuple(slots)
 
 
-def swap_pairs(size, odd):
+def swap_pairs(sizes, axis, odd):
     pairs = []
-    for i in range(size):
-        up = i % 2 == odd
-        partner = (i + 1 if up else i - 1) % size
-        pairs.append((i, partner))
-    if sorted(j for _, j in pairs) != list(range(size)):
-        pairs = [(i, j if abs(i - j) == 1 else i) for i, j in pairs]
+    for x in range(sizes["gx"]):
+        for y in range(sizes["gy"]):
+            for z in range(sizes["gz"]):
+                spot = {"gx": x, "gy": y, "gz": z}
+                index = spot[axis] + (1 if spot[axis] % 2 == odd else -1)
+                other = dict(spot, **{axis: index})
+                if not 0 <= index < sizes[axis]:
+                    other = dict(spot, gz=(z + 1 if z % 2 == 0 else z - 1))
+                    if other["gz"] >= sizes["gz"] or axis == "gz":
+                        other = spot
+                rank = lambda at: (at["gx"] * sizes["gy"] + at["gy"]) * sizes["gz"] + at["gz"]
+                pairs.append((rank(spot), rank(other)))
     return pairs
 
 
@@ -47,17 +54,6 @@
     scaled = (1.0 + 0.05 * p) * share
     mg = (2.0 + p) * (s * s)
     return scaled * (1.0 - d), scaled * d + mg, mg
-
-
-def mobility_steps(p, s, d, dp, ds, dd):
-    lb = 1.0 + 0.05 * p
-    gas = 2.0 + p
-    open_s = 1.0 - s
-    scaled = lb * (open_s * open_s)
-    mg = gas * (s * s)
-    solute = scaled * d
-    steps = mobility_moves(lb, gas, open_s, s, d, dp, ds, dd)
-    return scaled - solute, solute + mg, mg, steps[0], steps[1], steps[2]
 
 
 def mobility_moves(lb, gas, open_s, s, d, dp, ds, dd):
@@ -180,7 +176,7 @@
             dst[pl.ds(start, STEP), :] = jnp.sum(got, axis=1)
         return carry
 
-    lax.fori_loop(0, plan.z // STEP, body, 0)
+    lax.fori_loop(0, plan.z // STEP, body, 0, unroll=2)
 
 
 def scatter_cells(plan, rates, column, dsts, y_store):
@@ -209,7 +205,7 @@
                 dst[here, :] = dst[here, :] - off
         return carry
 
-    lax.fori_loop(0, plan.z // STEP, body, 0)
+    lax.fori_loop(0, plan.z // STEP, body, 0, unroll=2)
 
 
 def gather_segments(plan, fields, segment, dst):
@@ -280,26 +276,27 @@
 
     def body(c, carry):
         carry = list(carry)
-        for j in range(4):
-            z = c * 4 + j
+        for j in range(8):
+            z = c * 8 + j
             for f, field in enumerate(fields):
                 value = field[plane_rows(plan, z), :]
                 carry[f] = jnp.where(pair == z, pltpu.roll(value, 2 * z + 1, 1), carry[f])
         return tuple(carry)
 
-    for f, value in enumerate(lax.fori_loop(0, plan.z // 4, body, (zero,) * len(fields))):
+    for f, value in enumerate(lax.fori_loop(0, plan.z // 8, body, (zero,) * len(fields))):
         y_out[f] = value
 
 
-def merge_faces(plan, own, recv, count):
+def merge_faces(plan, own, recv, count, gas=0):
     lane = lax.broadcasted_iota(jnp.int32, (plan.x, 128), 1)
     even = lane % 2 == 0
     found = []
     y_recv = []
     for i, (axis, odd) in enumerate(plan.slots):
         high, valid = slot_side(axis, odd, plan.sizes)
-        mine = tuple(own[plan.slot_face[i]][f] for f in range(count))
-        theirs = tuple(recv[i][f] for f in range(count))
+        many = count + (gas if axis == "gz" else 0)
+        mine = tuple(own[plan.slot_face[i]][f] for f in range(many))
+        theirs = tuple(recv[i][f] for f in range(many))
         if axis != "gy":
             found.append((axis, high, valid, mine, theirs))
             continue
@@ -496,34 +493,41 @@
         ref[plan.rows : plan.rows + plan.x + 8, :] = jnp.zeros((plan.x + 8, 128), F32)
 
 
-def face_flux(sign, conductance, own, other, own_step=None, other_step=None):
+def face_base(sign, conductance, own, other, coef):
+    (w0, h0, g0), (w1, h1, g1) = mobilities(*own), mobilities(*other)
     p0, p1 = own[0], other[0]
-    if own_step is None:
-        (w0, h0, g0), (w1, h1, g1) = mobilities(*own), mobilities(*other)
-    else:
-        w0, h0, g0, a0, b0, c0 = mobility_steps(*own, *own_step)
-        w1, h1, g1, a1, b1, c1 = mobility_steps(*other, *other_step)
-        q0, q1 = own_step[0], other_step[0]
+    water, hydrogen = w0 + w1, h0 + h1
     drop = p0 - p1
     if sign is not None:
         total = 0.0125 * (p0 + p1)
         drop = drop + sign * (0.5 + total)
-        extra = sign * (total - 0.4)
-    if own_step is None:
-        water = (w0 + w1) * drop
-        hydrogen = (h0 + h1) * drop
-        if sign is not None:
-            hydrogen = hydrogen + (g0 + g1) * extra
-        return conductance * water, conductance * hydrogen
+    drop = conductance * drop
+    coef[0], coef[1], coef[2] = drop, conductance * water, conductance * hydrogen
+    if sign is None:
+        coef[3] = jnp.zeros(drop.shape, F32)
+        coef[4] = jnp.zeros(drop.shape, F32)
+        return drop * water, drop * hydrogen
+    extra = conductance * (sign * (total - 0.4))
+    coef[3], coef[4] = extra, conductance * (g0 + g1)
+    return drop * water, drop * hydrogen + extra * (g0 + g1)
+
+
+def face_step(sign, coef, own, other):
+    q0, q1 = own[0], other[0]
+    water, hydrogen = own[1] + other[1], own[2] + other[2]
     dq = q0 - q1
     if sign is not None:
         dtotal = sign * (0.0125 * (q0 + q1))
         dq = dq + dtotal
-    water = (a0 + a1) * drop + (w0 + w1) * dq
-    hydrogen = (b0 + b1) * drop + (h0 + h1) * dq
+    out_w = water * coef[0] + coef[1] * dq
+    out_h = hydrogen * coef[0] + coef[2] * dq
     if sign is not None:
-        hydrogen = hydrogen + (c0 + c1) * extra + (g0 + g1) * dtotal
-    return conductance * water, conductance * hydrogen
+        out_h = out_h + (own[3] + other[3]) * coef[3] + coef[4] * dtotal
+    return out_w, out_h
+
+
+def moves_of(p, s, d, dp, ds, dd):
+    return mobility_moves(1.0 + 0.05 * p, 2.0 + p, 1.0 - s, s, d, dp, ds, dd)[:3]
 
 
 def first_kernel(plan, io, *refs):
@@ -617,10 +621,10 @@
     fp, fs, fd, frac_water, frac_hydrogen, frac_volume = take(6)
     segment, column, weight, own, recv = take(5)
     own_faces, recv_faces = take(m), take(n)
-    res_out, frac_res, kb = take(3)
+    res_out, frac_res, face_coef = take(3)
     faces = take(m)
-    pack, own_res, got, weight_back = take(4)
-    res, y_store, rates, sems = take(4)
+    pack, own_res, pair_coef = take(3)
+    res, y_store, rates, sems, got, weight_back = take(6)
     fields = tuple(res.at[i] for i in range(3))
     copies = Copies(sems)
     load = copies.start(res_in, res)
@@ -635,18 +639,22 @@
             moved = pltpu.roll(tile, c * plan.cap, 1) if c else tile
             total = moved if total is None else jnp.where(lane8 == c, moved, total)
         weight_back[:, half * 128 : (half + 1) * 128] = total[0:1, :]
-    io.done(got, weight_back)
     io.ready(own, weight, segment, column, fp, fs, fd)
     io.ready(frac_water, frac_hydrogen, frac_volume)
 
-    def pair_rates(weights, seg_values, cell_values):
+    def pair_rates(side, weights, seg_values, cell_values):
         w0, h0, _ = mobilities(*seg_values)
         w1, h1, _ = mobilities(*cell_values)
-        flow = (0.5 * weights) * (seg_values[0] - cell_values[0])
-        return flow * (w0 + w1), flow * (h0 + h1)
+        half = 0.5 * weights
+        flow = half * (seg_values[0] - cell_values[0])
+        water, hydrogen = w0 + w1, h0 + h1
+        for j, value in enumerate((flow, half * water, half * hydrogen)):
+            start = (3 * side + j) * plan.z
+            pair_coef[start : start + plan.z, :] = value
+        return flow * water, flow * hydrogen
 
     rate_w, rate_h = pair_rates(
-        weight_back[...], pair_values(plan, own, 0), pair_values(plan, got, 1)
+        1, weight_back[...], pair_values(plan, own, 0), pair_values(plan, got, 1)
     )
     fpv, fsv, fdv = fp[...], fs[...], fd[...]
     mass_w, mass_h = masses(fpv, fsv, fdv)
@@ -657,7 +665,10 @@
     )
     frac_res[2] = closure(fpv, fsv, fdv)
     io.done(frac_res)
-    rate_w, rate_h = pair_rates(weight[...], pair_values(plan, got, 0), pair_values(plan, own, 1))
+    rate_w, rate_h = pair_rates(
+        0, weight[...], pair_values(plan, got, 0), pair_values(plan, own, 1)
+    )
+    io.done(pair_coef)
     rates[0 : plan.z, :] = rate_w
     rates[plan.z : 2 * plan.z, :] = rate_h
 
@@ -670,24 +681,36 @@
         conductance = jnp.where(
             valid, scale * (k0 * k1 / jnp.where(valid, k0 + k1, 1.0)), 0.0
         )
-        kb[i] = conductance
-        fluxes.append(face_flux(vertical_sign(axis, high), conductance, mine[:3], theirs[:3]))
-    io.done(kb)
+        sign = vertical_sign(axis, high)
+        fluxes.append(face_base(sign, conductance, mine[:3], theirs[:3], face_coef.at[i]))
+    io.done(face_coef)
     load.wait()
     add_faces(plan, found, fluxes, fields[:2], y_store)
     scatter_cells(plan, rates, column[...], fields[:2], y_store)
     store = copies.start(res, res_out)
-    send_parts(plan, io, fields, frac_res, segment, column, faces, own_res, pack)
+    send_parts(plan, io, fields, frac_res, segment, column, faces, own_res, pack, own, own_faces)
     store.wait()
 
 
-def send_parts(plan, io, fields, frac_fields, segment, column, faces, own, pack):
+def send_parts(
+    plan, io, fields, frac_fields, segment, column, faces, own, pack, base_own, base_faces
+):
     gather_segments(plan, tuple(frac_fields.at[i] for i in range(3)), segment[...], own)
     gather_cells(plan, fields, column[...], own)
+    for side in (0, 1):
+        moves = moves_of(*pair_values(plan, base_own, side), *pair_values(plan, own, side))
+        for j in (0, 1):
+            start = (3 * side + 1 + j) * plan.z
+            own[start : start + plan.z, :] = moves[j]
     pack_pairs(plan, own, pack)
     io.done(own, pack)
     write_faces(plan, fields, faces)
-    io.done(*faces)
+    for axis, face, base in zip(plan.faces, faces, base_faces):
+        three = lambda ref: tuple(ref[f] for f in range(3))
+        moves = moves_of(*three(base), *three(face))
+        for j in range(3 if axis == "gz" else 2):
+            face[1 + j] = moves[j]
+        io.done(face)
 
 
 def total_of(value):
@@ -794,15 +817,16 @@
     n, m = len(plan.slots), len(plan.faces)
     refs = list(refs)
     take = lambda count: [refs.pop(0) for _ in range(count)]
-    out_in, kb = take(2)
+    out_in, face_coef, pair_coef = take(3)
     fp, fs, fd, frac_volume, frac_vec = take(5)
-    segment, column, weight, weight_back, own, got, own_vec, recv = take(8)
-    own_faces, recv_faces = take(m), take(n)
+    segment, column, own_vec, recv = take(4)
     own_vec_faces, recv_vec_faces = take(m), take(n)
     if last:
         vec_in, base_in, base_frac, stats_in = take(4)
         (stats,) = take(1)
     else:
+        (own,) = take(1)
+        own_faces = take(m)
         out_back, frac_out = take(2)
         faces = take(m)
         pack, own_out = take(2)
@@ -816,27 +840,15 @@
 
     io.ready(recv)
     unpack_pairs(plan, recv, got_vec)
-    io.ready(own, got, own_vec, weight, weight_back, segment, column)
+    io.ready(own_vec, pair_coef, segment, column)
     io.ready(fp, fs, fd, frac_volume, frac_vec)
 
-    def pair_rates(weights, seg_values, seg_steps, cell_values, cell_steps):
-        w0, h0, _, a0, b0, _ = mobility_steps(*seg_values, *seg_steps)
-        w1, h1, _, a1, b1, _ = mobility_steps(*cell_values, *cell_steps)
-        drop = seg_values[0] - cell_values[0]
-        dq = seg_steps[0] - cell_steps[0]
-        half = 0.5 * weights
-        return (
-            half * ((a0 + a1) * drop + (w0 + w1) * dq),
-            half * ((b0 + b1) * drop + (h0 + h1) * dq),
-        )
-
-    rate_w, rate_h = pair_rates(
-        weight_back[...],
-        pair_values(plan, own, 0),
-        pair_values(plan, own_vec, 0),
-        pair_values(plan, got, 1),
-        pair_values(plan, got_vec, 1),
-    )
+    def pair_rates(side, seg_steps, cell_steps):
+        flow, water, hydrogen = pair_values(plan, pair_coef, side)
+        q, a, b = (f(x, y) for f, x, y in zip((lax.sub, lax.add, lax.add), seg_steps, cell_steps))
+        return a * flow + water * q, b * flow + hydrogen * q
+
+    rate_w, rate_h = pair_rates(1, pair_values(plan, own_vec, 0), pair_values(plan, got_vec, 1))
     values = (fp[...], fs[...], fd[...], frac_vec[0], frac_vec[1], frac_vec[2])
     _, _, _, mass_w, mass_h, frac_out[2] = cell_steps(*values)
     vol = frac_volume[...]
@@ -844,30 +856,25 @@
     frac_out[1] = vol * mass_h + scatter_segments(plan, rate_h, segment[...])
     if not last:
         io.done(frac_out)
-    rate_w, rate_h = pair_rates(
-        weight[...],
-        pair_values(plan, got, 0),
-        pair_values(plan, got_vec, 0),
-        pair_values(plan, own, 1),
-        pair_values(plan, own_vec, 1),
-    )
+    rate_w, rate_h = pair_rates(0, pair_values(plan, got_vec, 0), pair_values(plan, own_vec, 1))
     rates[0 : plan.z, :] = rate_w
     rates[plan.z : 2 * plan.z, :] = rate_h
 
-    io.ready(*own_faces, *recv_faces, *own_vec_faces, *recv_vec_faces, kb)
-    found = merge_faces(plan, own_faces, recv_faces, 3)
-    found_vec = merge_faces(plan, own_vec_faces, recv_vec_faces, 3)
-    fluxes = []
-    for i, ((axis, high, _, mine, theirs), steps) in enumerate(zip(found, found_vec)):
-        fluxes.append(
-            face_flux(vertical_sign(axis, high), kb[i], mine, theirs, steps[3], steps[4])
-        )
+    io.ready(*own_vec_faces, *recv_vec_faces, face_coef)
+    found = merge_faces(plan, own_vec_faces, recv_vec_faces, 3, gas=1)
+    fluxes = [
+        face_step(vertical_sign(axis, high), face_coef.at[i], mine, theirs)
+        for i, (axis, high, _, mine, theirs) in enumerate(found)
+    ]
     load.wait()
     add_faces(plan, found, fluxes, fields[:2], y_store)
     scatter_cells(plan, rates, column[...], fields[:2], y_store)
     if not last:
         store = copies.start(out, out_back)
-        send_parts(plan, io, fields, frac_out, segment, column, faces, own_out, pack)
+        io.ready(own, *own_faces)
+        send_parts(
+            plan, io, fields, frac_out, segment, column, faces, own_out, pack, own, own_faces
+        )
         store.wait()
         return
     wait_all(late)
@@ -880,15 +887,17 @@
     three = lambda ref: tuple(ref.at[i] for i in range(3))
     refs3 = (three(base), three(vec), fields)
     fracs3 = (base_frac, frac_vec, frac_out)
-    rz, uz = block_sums(
-        plan, refs3, fracs3, lambda r, w, v: (r * v, (w - share * r) * v), 2
-    )
+    rz, wz = block_sums(
+        plan, refs3, fracs3, lambda r, w, v: (r * v, w * v), 2
+    )
+    uz = wz - share * rz
     along_r, along_u = safe_ratio(rz, r11 * r11), safe_ratio(uz, uu)
+    rest = along_r - along_u * share
     (vv,) = block_sums(
         plan,
         refs3,
         fracs3,
-        lambda r, w, v: (jnp.square(v - along_r * r - along_u * (w - share * r)),),
+        lambda r, w, v: (jnp.square((v - rest * r) - along_u * w),),
         1,
     )
     put_lanes(stats, (r11, r12, r22, safe_ratio(rz, r11), safe_ratio(uz, r22), jnp.sqrt(vv)))
@@ -1040,11 +1049,12 @@
     three = (3,) + field
     frac_shape = (3, plan.z, plan.seg)
     inner_work = 16 << 20
+    step_faces = [(4 if axis == "gz" else 3, 32, 128) for axis in plan.faces]
 
     def exchange(faces, pack):
         got = lax.all_to_all(pack, PLANE, 0, 0, tiled=True)
         moved = [
-            lax.ppermute(faces[spot], axis, swap_pairs(plan.sizes[axis], odd))
+            lax.ppermute(faces[spot], DEVICES, swap_pairs(plan.sizes, axis, odd))
             for (axis, odd), spot in zip(plan.slots, plan.slot_face)
         ]
         return moved, got
@@ -1074,23 +1084,24 @@
     )
     outs = call(
         functools.partial(residual_kernel, plan),
-        [three, frac_shape, (face_count, 32, 128)]
-        + [(3, 32, 128)] * face_count
-        + [(plan.peers, plan.pack_rows, 128), pair_shape, pair_shape, (1, plan.pairs)],
+        [three, frac_shape, (face_count, 5, 32, 128)]
+        + step_faces
+        + [(plan.peers, plan.pack_rows, 128), pair_shape, pair_shape],
         [res, frac_pressure, frac_saturation, frac_dissolved]
         + [frac_old_water, frac_old_hydrogen, frac_volume]
         + [pair_segment, pair_column, weight, own, recv]
         + list(faces)
         + list(recv_faces),
         scratch=[three, y_scratch, rate_scratch],
+        more=[pair_shape, (1, plan.pairs)],
         copies=2,
         far=(0,),
         far_out=(0,),
         first=(11, 10, 9),
     )
-    res, frac_res, kb = outs[:3]
+    res, frac_res, face_coef = outs[:3]
     vec_faces = outs[3 : 3 + face_count]
-    pack, own_vec, got, weight_back = outs[3 + face_count :]
+    pack, own_vec, pair_coef = outs[3 + face_count :]
 
     def image(vec, frac_vec, vec_faces, pack, own_vec, base):
         recv_vec_faces, recv_vec = exchange(vec_faces, pack)
@@ -1106,17 +1117,18 @@
             far_out=(0,),
             work=inner_work,
         )
-        args = [outs[0], kb]
+        args = [outs[0], face_coef, pair_coef]
         args += [frac_pressure, frac_saturation, frac_dissolved, frac_volume, frac_vec]
-        args += [pair_segment, pair_column, weight, weight_back, own, got, own_vec, recv_vec]
-        args += list(faces) + list(recv_faces) + list(vec_faces) + list(recv_vec_faces)
+        args += [pair_segment, pair_column, own_vec, recv_vec]
+        args += list(vec_faces) + list(recv_vec_faces)
         if last:
             far = (0, len(args), len(args) + 1)
             args += [vec, *base, outs[1]]
-            shapes = [(devices, 128)]
+            shapes = [(devices, 8)]
         else:
             far = (0,)
-            shapes = [three, frac_shape] + [(3, 32, 128)] * face_count
+            args += [own] + list(faces)
+            shapes = [three, frac_shape] + step_faces
             shapes += [(plan.peers, plan.pack_rows, 128), pair_shape]
         return call(
             functools.partial(jacobian_kernel, plan, last),
@@ -1127,7 +1139,7 @@
             copies=3,
             far=far,
             far_out=() if last else (0,),
-            first=(14, 11, 12, 13),
+            first=(11, 2, 10),
         )
 
     outs = image(res, frac_res, vec_faces, pack, own_vec, None)

time: 96 us -> 90.2 us (0.940)
  starting transfers between devices: 37 us -> 33.7 us
  Pallas kernels: 47.2 us -> 44 us
    ppermute x15, starting transfers between devices: 19.8 us -> 15.4 us  [exchange(): lax.ppermute(faces[spot], DEVICES, swap_pairs(plan.sizes, axis, odd))]
    pallas_call x8, Pallas kernels: 47.2 us -> 44 us  [call(): pl.pallas_call(body, out_shape=[jax.ShapeDtypeStruct(shape, F32) for shap...]
    all_to_all x3, starting transfers between devices: 17.1 us -> 18.3 us  [exchange(): got = lax.all_to_all(pack, PLANE, 0, 0, tiled=True)]
  transfers between devices with their start and end apart: 18 -> 18, of which waited for: 0 -> 0; matrix products, arithmetic and copies ran while one was open for 0% -> 0% of each run, Pallas kernels for 19% -> 20%
where the time goes in v4:
time: 90.2 us; the launch traced here: 89.7 us
  Pallas kernels  44 us (49%)
  starting transfers between devices  33.7 us (37%)
  blocking collectives  11.1 us (12%)
    pallas_call x8, Pallas kernels, call(): pl.pallas_call(body, out_shape=[jax.ShapeDtypeStruct(shape, F32) for shap...  44 us
    all_to_all x3, starting transfers between devices, exchange(): got = lax.all_to_all(pack, PLANE, 0, 0, tiled=True)  18.3 us
    ppermute x15, starting transfers between devices, exchange(): lax.ppermute(faces[spot], DEVICES, swap_pairs(plan.sizes, axis, odd))  15.4 us
    all_to_all x1, blocking collectives, on_device(): stats = lax.all_to_all(stats, ('gx', 'gy', 'gz'), 0, 0, tiled=True)  11.1 us
  transfers between devices with their start and end apart: 18, of which 0 were waited for; matrix products, arithmetic and copies ran while one was open for 0% of the time, Pallas kernels for 20%

profile of v4, /device:TPU:0, one launch (start us, length us, event | category | flops | bytes accessed | tf_op | source)
XLA Modules:
  0.0 89.7 jit_solution(8476925993727936256)
XLA Ops:
  0.6 5.1 %shard_map.201 = (f32[4,32,128]{2,1,0:T(8,128)}, f32[4,32,128]{2,1,0:T(8,128)}, f32[4,32,128]{2,1,0:T(8,128)}, f32[4,32,128]{2,1,0:T(8,128)}, f32[16,32,128]{2,1...) custom-call(f32[1024,128]{1,0:T(8,128)} %bitcast.14, f32[1024,128]{1,0:T(8,128)} %bitcast.18, f32[1024,128]{1,0:T(8,128)} %bitcast.22, ...), custom_call_target="tpu_custom_call" | custom-call | tf_op jit(solution)/shard_map/pallas_call | solution.py:997
  5.7 8.4 %all-to-all-start = ((f32[16,32,128]{2,1,0:T(8,128)}), f32[16,32,128]{2,1,0:T(8,128)}, u32[]{:S(2)}, u32[]{:S(2)}) async-start(f32[16,32,128]{2,1,0:T(8,128)} %get-tuple-element.38), calls=%async_computation | async-start | bytes 524288 | tf_op jit(solution)/shard_map/all_to_all | solution.py:1055
  14.1 1.9 %collective-permute-start = (f32[4,32,128]{2,1,0:T(8,128)}, f32[4,32,128]{2,1,0:T(8,128)}, u32[]{:S(2)}, u32[]{:S(2)}) collective-permute-start(f32[4,32,128]{2,1,0:T(8,128)} %get-tuple-element.39.refs_12_.refs_22_), channel_id=1, source_target_pairs={{0,8},{1,9},{2,10},{3,11},{4,12},{5,13},{6,14},{7,15},{8,0},{9,1},... | collective-permute-start | bytes 196616 | tf_op jit(solution)/shard_map/ppermute | solution.py:1057
  16.0 0.0 collective-permute-start.1
  16.0 0.5 collective-permute-start.4
  16.5 0.0 collective-permute-start.3
  16.5 2.9 %collective-permute-start.2 = (f32[4,32,128]{2,1,0:T(8,128)}, f32[4,32,128]{2,1,0:T(8,128)}, u32[]{:S(2)}, u32[]{:S(2)}) collective-permute-start(f32[4,32,128]{2,1,0:T(8,128)} %get-tuple-element.41.refs_14_.refs_24_), channel_id=1, source_target_pairs={{0,2},{1,3},{2,0},{3,1},{4,6},{5,7},{6,4},{7,5},{8,10},{9,11},{10,... | collective-permute-start | bytes 196616 | tf_op jit(solution)/shard_map/ppermute | solution.py:1057
  19.5 6.1 %shard_map.202 = (f32[3,1024,128]{2,1,0:T(8,128)}, f32[11,1024,128]{2,1,0:T(8,128)}) custom-call(f32[1024,128]{1,0:T(8,128)} %bitcast.15, f32[1024,128]{1,0:T(8,128)} %bitcast.19, f32[1024,128]{1,0:T(8,128)} %bitcast.23, f32[1024,128]{1,0:T(8,128)} %bitcast.31, f32[1024,128]{1,0:T(8,128)} %bitcast.32, f32[1024,128]{1,0:T(8,128)} %bitcast.26, ...), custom_call_target="tpu_custom_call" | custom-call | flops 16777216 | bytes 16777216 | tf_op jit(solution)/shard_map/pallas_call | solution.py:997
  25.6 0.0 collective-permute-done.refs_16_
  25.6 0.0 collective-permute-done.1.refs_17_
  25.6 0.0 collective-permute-done.4.refs_20_
  25.6 0.0 collective-permute-done.3.refs_19_
  25.7 0.0 collective-permute-done.2.refs_18_
  25.7 0.0 all-to-all-done.refs_11_
  25.7 6.1 %shard_map.203 = (f32[3,1024,128]{2,1,0:T(8,128)}, f32[3,32,256]{2,1,0:T(8,128)}, f32[4,5,32,128]{3,2,1,0:T(8,128)}, f32[3,32,128]{2,1,0:T(8,128)}, f32[3,32,128...) custom-call(f32[3,1024,128]{2,1,0:T(8,128)} %get-tuple-element.36.re, ...), custom_call_target="tpu_custom_call" | custom-call | tf_op jit(solution)/shard_map/pallas_call | solution.py:997
  31.8 4.8 %all-to-all-start.1 = ((f32[16,24,128]{2,1,0:T(8,128)}), f32[16,24,128]{2,1,0:T(8,128)}, u32[]{:S(2)}, u32[]{:S(2)}) async-start(f32[16,24,128]{2,1,0:T(8,128)} %get-tuple-element.49), calls=%async_computation.1 | async-start | bytes 393216 | tf_op jit(solution)/shard_map/all_to_all | solution.py:1055
  36.5 0.1 collective-permute-start.9
  36.6 1.9 %collective-permute-start.5 = (f32[3,32,128]{2,1,0:T(8,128)}, f32[3,32,128]{2,1,0:T(8,128)}, u32[]{:S(2)}, u32[]{:S(2)}) collective-permute-start(f32[3,32,128]{2,1,0:T(8,128)} %get-tuple-element.50.refs_12_), channel_id=1, source_target_pairs={{0,8},{1,9},{2,10},{3,11},{4,12},{5,13},{6,14},{7,15},{8,0},{9,1},... | collective-permute-start | bytes 147464 | tf_op jit(solution)/shard_map/ppermute | solution.py:1057
  38.5 0.2 collective-permute-start.6
  38.7 0.4 collective-permute-start.8
  39.0 2.5 %collective-permute-start.7 = (f32[3,32,128]{2,1,0:T(8,128)}, f32[3,32,128]{2,1,0:T(8,128)}, u32[]{:S(2)}, u32[]{:S(2)}) collective-permute-start(f32[3,32,128]{2,1,0:T(8,128)} %get-tuple-element.52.refs_14_), channel_id=1, source_target_pairs={{0,2},{1,3},{2,0},{3,1},{4,6},{5,7},{6,4},{7,5},{8,10},{9,11},{10,... | collective-permute-start | bytes 147464 | tf_op jit(solution)/shard_map/ppermute | solution.py:1057
  41.6 5.4 %shard_map.204.refs_0_ = f32[3,1024,128]{2,1,0:T(8,128)} custom-call(f32[1024,128]{1,0:T(8,128)} %bitcast.16, f32[1024,128]{1,0:T(8,128)} %bitcast.20, f32[1024,128]{1,0:T(8,128)} %bitcast.24, f32[1024,128]{1,0:T(8,128)} %bitcast.27, f32[3,1024,128]{2,1,0:T(8,128)} %get-tuple-element.43.refs_4_.refs_6_.refs_22_.refs_1_, ...), custom_call_target="tpu_custom_call" | custom-call | flops 16777216 | bytes 16777216 | tf_op jit(solution)/shard_map/pallas_call | solution.py:997
  47.0 0.0 collective-permute-done.5.refs_16_
  47.0 0.0 collective-permute-done.6.refs_17_
  47.0 0.0 collective-permute-done.8.refs_19_
  47.0 0.0 collective-permute-done.7.refs_18_
  47.1 0.0 collective-permute-done.9.refs_20_
  47.1 0.0 all-to-all-done.1.refs_11_
  47.1 6.5 %shard_map.205 = (f32[3,1024,128]{2,1,0:T(8,128)}, f32[3,32,256]{2,1,0:T(8,128)}, f32[3,32,128]{2,1,0:T(8,128)}, f32[3,32,128]{2,1,0:T(8,128)}, f32[3,32,128]{2,...) custom-call(f32[3,1024,128]{2,1,0:T(8,128)} %shard_map.204.refs_0_, ...), custom_call_target="tpu_custom_call" | custom-call | tf_op jit(solution)/shard_map/pallas_call | solution.py:997
  53.5 5.1 %all-to-all-start.2 = ((f32[16,24,128]{2,1,0:T(8,128)}), f32[16,24,128]{2,1,0:T(8,128)}, u32[]{:S(2)}, u32[]{:S(2)}) async-start(f32[16,24,128]{2,1,0:T(8,128)} %get-tuple-element.58), calls=%async_computation.2 | async-start | bytes 393216 | tf_op jit(solution)/shard_map/all_to_all | solution.py:1055
  58.7 0.1 collective-permute-start.14
  58.7 1.9 %collective-permute-start.10 = (f32[3,32,128]{2,1,0:T(8,128)}, f32[3,32,128]{2,1,0:T(8,128)}, u32[]{:S(2)}, u32[]{:S(2)}) collective-permute-start(f32[3,32,128]{2,1,0:T(8,128)} %get-tuple-element.59.refs_12_), channel_id=1, source_target_pairs={{0,8},{1,9},{2,10},{3,11},{4,12},{5,13},{6,14},{7,15},{8,0},{9,1},... | collective-permute-start | bytes 147464 | tf_op jit(solution)/shard_map/ppermute | solution.py:1057
  60.6 0.2 collective-permute-start.11
  60.8 0.4 collective-permute-start.13
  61.2 2.5 %collective-permute-start.12 = (f32[3,32,128]{2,1,0:T(8,128)}, f32[3,32,128]{2,1,0:T(8,128)}, u32[]{:S(2)}, u32[]{:S(2)}) collective-permute-start(f32[3,32,128]{2,1,0:T(8,128)} %get-tuple-element.61.refs_14_), channel_id=1, source_target_pairs={{0,2},{1,3},{2,0},{3,1},{4,6},{5,7},{6,4},{7,5},{8,10},{9,11},{10,... | collective-permute-start | bytes 147464 | tf_op jit(solution)/shard_map/ppermute | solution.py:1057
  63.7 6.3 %shard_map.206 = (f32[3,1024,128]{2,1,0:T(8,128)}, f32[8,128]{1,0:T(8,128)}) custom-call(f32[1024,128]{1,0:T(8,128)} %bitcast.17, f32[1024,128]{1,0:T(8,128)} %bitcast.21, f32[1024,128]{1,0:T(8,128)} %bitcast.25, f32[1024,128]{1,0:T(8,128)} %bitcast.28, f32[3,1024,128]{2,1,0:T(8,128)} %get-tuple-element.54.refs_4_.refs_21_.refs_3_, ...), custom_call_target="tpu_custom_call" | custom-call | flops 16777216 | bytes 16777216 | tf_op jit(solution)/shard_map/pallas_call | solution.py:997
  70.0 0.0 collective-permute-done.10.refs_16_
  70.0 0.0 collective-permute-done.11.refs_17_
  70.0 0.0 collective-permute-done.13.refs_19_
  70.0 0.0 collective-permute-done.12.refs_18_
  70.0 0.0 collective-permute-done.14.refs_20_
  70.0 0.0 all-to-all-done.2.refs_11_
  70.0 5.0 %shard_map.207 = f32[32,8]{1,0:T(8,128)} custom-call(f32[3,1024,128]{2,1,0:T(8,128)} %get-tuple-element.56.refs_0_, f32[4,5,32,128]{3,2,1,0:T(8,128)} %get-tuple-element.45.refs_1_, f32[192,256]{1,0:T(8,128)} %get-tuple-element.46.refs_2_, f32[32,256]{1,0:T(8,128)} %refs_3_.5, f32[32,256]{1,0:T(8,128)} %refs_4_.7, f32[32,256]{1,0:T(8,128)} %refs_5_.7, ...), custom_call_target="tpu_custom_call" | custom-call | tf_op jit(solution)/shard_map/pallas_call | solution.py:997
  75.0 11.1 %all_to_all.26 = f32[32,1,8]{2,1,0:T(1,128)} all-to-all(f32[32,1,8]{2,1,0:T(1,128)} %bitcast.33), channel_id=1, replica_groups=mesh['gx'=4,'gy'=4,'gz'=2] {'gx','gy','gz'}, dimensions={0} | all-to-all | bytes 2048 | tf_op jit(solution)/shard_map/all_to_all | solution.py:1150
  86.1 3.5 %shard_map.208 = (f32[3,1024,128]{2,1,0:T(8,128)}, f32[3,32,256]{2,1,0:T(8,128)}) custom-call(f32[32,8]{1,0:T(8,128)} %bitcast.34, f32[3,1024,128]{2,1,0:T(8,128)} %get-tuple-element.43.refs_4_.refs_6_.refs_22_.refs_1_, f32[3,32,256]{2,1,0:T(8,128)} %get-tuple-element.34.refs_7_.refs_23_.refs_2_, f32[3,1024,128]{2,1,0:T(8,128)} %get-tuple-element.54.refs_4_.refs_21_.refs_3_, ...), custom_call_target="tpu_custom_call" | custom-call | tf_op jit(solution)/shard_map/pallas_call | solution.py:997
Async XLA Ops:
  5.7 20.0 %all-to-all-start = ((f32[16,32,128]{2,1,0:T(8,128)}), f32[16,32,128]{2,1,0:T(8,128)}, u32[]{:S(2)}, u32[]{:S(2)}) async-start(f32[16,32,128]{2,1,0:T(8,128)} %get-tuple-element.38), calls=%async_computation | async-start | bytes 524288 | tf_op jit(solution)/shard_map/all_to_all | solution.py:1055
  14.1 11.5 %collective-permute-start = (f32[4,32,128]{2,1,0:T(8,128)}, f32[4,32,128]{2,1,0:T(8,128)}, u32[]{:S(2)}, u32[]{:S(2)}) collective-permute-start(f32[4,32,128]{2,1,0:T(8,128)} %get-tuple-element.39.refs_12_.refs_22_), channel_id=1, source_target_pairs={{0,8},{1,9},{2,10},{3,11},{4,12},{5,13},{6,14},{7,15},{8,0},{9,1},... | collective-permute-start | bytes 196616 | tf_op jit(solution)/shard_map/ppermute | solution.py:1057
  16.0 9.6 %collective-permute-start.1 = (f32[4,32,128]{2,1,0:T(8,128)}, f32[4,32,128]{2,1,0:T(8,128)}, u32[]{:S(2)}, u32[]{:S(2)}) collective-permute-start(f32[4,32,128]{2,1,0:T(8,128)} %get-tuple-element.40.refs_13_.refs_23_), channel_id=1, source_target_pairs={{0,1},{1,0},{2,3},{3,2},{4,5},{5,4},{6,7},{7,6},{8,16},{9,17},{10,... | collective-permute-start | bytes 196616 | tf_op jit(solution)/shard_map/ppermute | solution.py:1057
  16.0 9.6 %collective-permute-start.4 = (f32[4,32,128]{2,1,0:T(8,128)}, f32[4,32,128]{2,1,0:T(8,128)}, u32[]{:S(2)}, u32[]{:S(2)}) collective-permute-start(f32[4,32,128]{2,1,0:T(8,128)} %get-tuple-element.42.refs_15_.refs_25_), channel_id=1, source_target_pairs={{0,1},{1,0},{2,3},{3,2},{4,5},{5,4},{6,7},{7,6},{8,9},{9,8},{10,11... | collective-permute-start | bytes 196616 | tf_op jit(solution)/shard_map/ppermute | solution.py:1057
  16.5 9.1 %collective-permute-start.3 = (f32[4,32,128]{2,1,0:T(8,128)}, f32[4,32,128]{2,1,0:T(8,128)}, u32[]{:S(2)}, u32[]{:S(2)}) collective-permute-start(f32[4,32,128]{2,1,0:T(8,128)} %get-tuple-element.41.refs_14_.refs_24_), channel_id=1, source_target_pairs={{0,1},{1,0},{2,4},{3,5},{4,2},{5,3},{6,7},{7,6},{8,9},{9,8},{10,12... | collective-permute-start | bytes 196616 | tf_op jit(solution)/shard_map/ppermute | solution.py:1057
  16.5 9.1 %collective-permute-start.2 = (f32[4,32,128]{2,1,0:T(8,128)}, f32[4,32,128]{2,1,0:T(8,128)}, u32[]{:S(2)}, u32[]{:S(2)}) collective-permute-start(f32[4,32,128]{2,1,0:T(8,128)} %get-tuple-element.41.refs_14_.refs_24_), channel_id=1, source_target_pairs={{0,2},{1,3},{2,0},{3,1},{4,6},{5,7},{6,4},{7,5},{8,10},{9,11},{10,... | collective-permute-start | bytes 196616 | tf_op jit(solution)/shard_map/ppermute | solution.py:1057
  31.8 15.3 %all-to-all-start.1 = ((f32[16,24,128]{2,1,0:T(8,128)}), f32[16,24,128]{2,1,0:T(8,128)}, u32[]{:S(2)}, u32[]{:S(2)}) async-start(f32[16,24,128]{2,1,0:T(8,128)} %get-tuple-element.49), calls=%async_computation.1 | async-start | bytes 393216 | tf_op jit(solution)/shard_map/all_to_all | solution.py:1055
  36.5 10.5 %collective-permute-start.9 = (f32[4,32,128]{2,1,0:T(8,128)}, f32[4,32,128]{2,1,0:T(8,128)}, u32[]{:S(2)}, u32[]{:S(2)}) collective-permute-start(f32[4,32,128]{2,1,0:T(8,128)} %get-tuple-element.53.refs_15_), channel_id=1, source_target_pairs={{0,1},{1,0},{2,3},{3,2},{4,5},{5,4},{6,7},{7,6},{8,9},{9,8},{10,11... | collective-permute-start | bytes 196616 | tf_op jit(solution)/shard_map/ppermute | solution.py:1057
  36.6 10.4 %collective-permute-start.5 = (f32[3,32,128]{2,1,0:T(8,128)}, f32[3,32,128]{2,1,0:T(8,128)}, u32[]{:S(2)}, u32[]{:S(2)}) collective-permute-start(f32[3,32,128]{2,1,0:T(8,128)} %get-tuple-element.50.refs_12_), channel_id=1, source_target_pairs={{0,8},{1,9},{2,10},{3,11},{4,12},{5,13},{6,14},{7,15},{8,0},{9,1},... | collective-permute-start | bytes 147464 | tf_op jit(solution)/shard_map/ppermute | solution.py:1057
  38.5 8.5 %collective-permute-start.6 = (f32[3,32,128]{2,1,0:T(8,128)}, f32[3,32,128]{2,1,0:T(8,128)}, u32[]{:S(2)}, u32[]{:S(2)}) collective-permute-start(f32[3,32,128]{2,1,0:T(8,128)} %get-tuple-element.51.refs_13_), channel_id=1, source_target_pairs={{0,1},{1,0},{2,3},{3,2},{4,5},{5,4},{6,7},{7,6},{8,16},{9,17},{10,... | collective-permute-start | bytes 147464 | tf_op jit(solution)/shard_map/ppermute | solution.py:1057
  38.7 8.3 %collective-permute-start.8 = (f32[3,32,128]{2,1,0:T(8,128)}, f32[3,32,128]{2,1,0:T(8,128)}, u32[]{:S(2)}, u32[]{:S(2)}) collective-permute-start(f32[3,32,128]{2,1,0:T(8,128)} %get-tuple-element.52.refs_14_), channel_id=1, source_target_pairs={{0,1},{1,0},{2,4},{3,5},{4,2},{5,3},{6,7},{7,6},{8,9},{9,8},{10,12... | collective-permute-start | bytes 147464 | tf_op jit(solution)/shard_map/ppermute | solution.py:1057
  39.0 8.0 %collective-permute-start.7 = (f32[3,32,128]{2,1,0:T(8,128)}, f32[3,32,128]{2,1,0:T(8,128)}, u32[]{:S(2)}, u32[]{:S(2)}) collective-permute-start(f32[3,32,128]{2,1,0:T(8,128)} %get-tuple-element.52.refs_14_), channel_id=1, source_target_pairs={{0,2},{1,3},{2,0},{3,1},{4,6},{5,7},{6,4},{7,5},{8,10},{9,11},{10,... | collective-permute-start | bytes 147464 | tf_op jit(solution)/shard_map/ppermute | solution.py:1057
  53.5 16.5 %all-to-all-start.2 = ((f32[16,24,128]{2,1,0:T(8,128)}), f32[16,24,128]{2,1,0:T(8,128)}, u32[]{:S(2)}, u32[]{:S(2)}) async-start(f32[16,24,128]{2,1,0:T(8,128)} %get-tuple-element.58), calls=%async_computation.2 | async-start | bytes 393216 | tf_op jit(solution)/shard_map/all_to_all | solution.py:1055
  58.7 11.4 %collective-permute-start.14 = (f32[4,32,128]{2,1,0:T(8,128)}, f32[4,32,128]{2,1,0:T(8,128)}, u32[]{:S(2)}, u32[]{:S(2)}) collective-permute-start(f32[4,32,128]{2,1,0:T(8,128)} %get-tuple-element.62.refs_15_), channel_id=1, source_target_pairs={{0,1},{1,0},{2,3},{3,2},{4,5},{5,4},{6,7},{7,6},{8,9},{9,8},{10,11... | collective-permute-start | bytes 196616 | tf_op jit(solution)/shard_map/ppermute | solution.py:1057
  58.7 11.2 %collective-permute-start.10 = (f32[3,32,128]{2,1,0:T(8,128)}, f32[3,32,128]{2,1,0:T(8,128)}, u32[]{:S(2)}, u32[]{:S(2)}) collective-permute-start(f32[3,32,128]{2,1,0:T(8,128)} %get-tuple-element.59.refs_12_), channel_id=1, source_target_pairs={{0,8},{1,9},{2,10},{3,11},{4,12},{5,13},{6,14},{7,15},{8,0},{9,1},... | collective-permute-start | bytes 147464 | tf_op jit(solution)/shard_map/ppermute | solution.py:1057
  60.6 9.3 %collective-permute-start.11 = (f32[3,32,128]{2,1,0:T(8,128)}, f32[3,32,128]{2,1,0:T(8,128)}, u32[]{:S(2)}, u32[]{:S(2)}) collective-permute-start(f32[3,32,128]{2,1,0:T(8,128)} %get-tuple-element.60.refs_13_), channel_id=1, source_target_pairs={{0,1},{1,0},{2,3},{3,2},{4,5},{5,4},{6,7},{7,6},{8,16},{9,17},{10,... | collective-permute-start | bytes 147464 | tf_op jit(solution)/shard_map/ppermute | solution.py:1057
  60.8 9.2 %collective-permute-start.13 = (f32[3,32,128]{2,1,0:T(8,128)}, f32[3,32,128]{2,1,0:T(8,128)}, u32[]{:S(2)}, u32[]{:S(2)}) collective-permute-start(f32[3,32,128]{2,1,0:T(8,128)} %get-tuple-element.61.refs_14_), channel_id=1, source_target_pairs={{0,1},{1,0},{2,4},{3,5},{4,2},{5,3},{6,7},{7,6},{8,9},{9,8},{10,12... | collective-permute-start | bytes 147464 | tf_op jit(solution)/shard_map/ppermute | solution.py:1057
  61.2 8.8 %collective-permute-start.12 = (f32[3,32,128]{2,1,0:T(8,128)}, f32[3,32,128]{2,1,0:T(8,128)}, u32[]{:S(2)}, u32[]{:S(2)}) collective-permute-start(f32[3,32,128]{2,1,0:T(8,128)} %get-tuple-element.61.refs_14_), channel_id=1, source_target_pairs={{0,2},{1,3},{2,0},{3,1},{4,6},{5,7},{6,4},{7,5},{8,10},{9,11},{10,... | collective-permute-start | bytes 147464 | tf_op jit(solution)/shard_map/ppermute | solution.py:1057
